TPU v7x, 512 devices: a whole 4x8x8 slice. The times are simulated.
512 devices in a mesh: fsdp: 16 (over y, x_lo), ed: 32 (over x_hi, z, core).
Axes of the slice: x: 4 (x_hi: 2, x_lo: 2; x = x_hi * 2 + x_lo), y: 8, z: 8, core: 2. Of those that a mesh axis runs over, the one named last changes fastest.
Arguments:
- tokens: bfloat16 [9216, 6144], P('ed', 'fsdp'), may hold values from -6 to 6
- expert_ids: int32 [9216, 2], P('ed'), may hold values from 0 to 7, all different within a row; in each aligned block of 288 rows (0 to 287, 288 to 575, ...) at most 81 rows name the same one
- route_weights: float32 [9216, 2], P('ed'), may hold values from 0.1 to 1
- w_gate: bfloat16 [1, 6144, 8192], P(None, 'fsdp', 'ed'), may hold values from -0.078125 to 0.078125
- w_up: bfloat16 [1, 6144, 8192], P(None, 'fsdp', 'ed'), may hold values from -0.078125 to 0.078125
- w_down: bfloat16 [1, 8192, 6144], P(None, 'ed', 'fsdp'), may hold values from -0.0625 to 0.0625
Outputs:
- mixed: bfloat16 [9216, 6144], P('ed', 'fsdp')
Inputs may be any that keep to these rules, and one draw needn't show every extreme that they name: `expert_ids`: each row names two different experts. In each block of 288 rows that one index of ed holds, no expert is named by more than 81 rows, a bound that some block reaches.
All inputs are finite; a program needn't handle non-finite values.
Results may differ from a plain program's by a relative error of at most 0.025.
Values may be sent and summed in bfloat16 or wider, within the bound.
A program may use at most 64 MiB of HBM per device.

v0:
```python
import jax
import jax.numpy as jnp
from jax import lax
from jax.sharding import PartitionSpec as P

CAP = 81


def slot_match(routes, window, capacity):
    window_ids = jnp.arange(window, dtype=jnp.int32)
    routed = jnp.any(routes[:, :, None, :] == window_ids[None, None, :, None], axis=3)
    position = jnp.cumsum(routed.astype(jnp.int32), axis=1) - 1
    slot_ids = jnp.arange(capacity, dtype=jnp.int32)
    hits = routed[:, :, :, None] & (position[:, :, :, None] == slot_ids[None, None, None, :])
    return hits.astype(jnp.int32)


def take_block(block_rows, row_list):
    return jnp.take(block_rows, row_list, axis=0)


def pick_rows(blocks, routes, window, capacity):
    match = slot_match(routes, window, capacity)
    row_numbers = jnp.arange(blocks.shape[1], dtype=jnp.int32)
    source_row = jnp.sum(match * row_numbers[None, :, None, None], axis=1).reshape(
        blocks.shape[0], window * capacity
    )
    filled = jnp.sum(match, axis=1).reshape(blocks.shape[0], window * capacity)
    picked = jax.vmap(take_block)(blocks, source_row)
    picked = jnp.where(filled[:, :, None] > 0, picked, jnp.zeros_like(picked))
    return picked.reshape(blocks.shape[0], window, capacity, blocks.shape[2])


def combine_matrix(routes, weights, window, capacity):
    match = slot_match(routes[None], window, capacity)[0]
    window_ids = jnp.arange(window, dtype=jnp.int32)
    per_expert = jnp.sum(
        jnp.where(
            routes[:, None, :] == window_ids[None, :, None],
            weights[:, None, :],
            jnp.zeros_like(weights[:, None, :]),
        ),
        axis=2,
    )
    return (per_expert[:, :, None] * match.astype(weights.dtype)).reshape(
        routes.shape[0], window * capacity
    )


def local(tokens, expert_ids, route_weights, w_gate, w_up, w_down):
    window = w_gate.shape[0]
    features_dev = tokens.shape[1]
    own_slots = pick_rows(tokens[None], expert_ids[None], window, CAP)[0]
    selected = lax.all_gather(own_slots, "ed", axis=1, tiled=True)
    rows_full = lax.all_to_all(selected, "fsdp", split_axis=1, concat_axis=2, tiled=True)
    gate_part = jnp.einsum(
        "hnm,hmq->hnq",
        rows_full,
        lax.all_gather(w_gate, "fsdp", axis=1, tiled=True),
        preferred_element_type=jnp.float32,
    )
    up_part = jnp.einsum(
        "hnm,hmq->hnq",
        rows_full,
        lax.all_gather(w_up, "fsdp", axis=1, tiled=True),
        preferred_element_type=jnp.float32,
    )
    activation = (jax.nn.silu(gate_part) * up_part).astype(jnp.bfloat16)
    act_one = activation[0]

    def columns_out(shard_piece, first_col, act_one=act_one):
        return jnp.dot(act_one, shard_piece, preferred_element_type=jnp.float32)

    whole_rows = columns_out(lax.all_gather(w_down[0], "fsdp", axis=1, tiled=True), jnp.int32(0))
    outputs_list = [whole_rows.astype(jnp.bfloat16)]
    stacked = jnp.stack(outputs_list)
    exchanged = lax.all_to_all(stacked, "fsdp", split_axis=2, concat_axis=1, tiled=True)
    partial_out = exchanged.astype(jnp.float32)
    slot_out = lax.psum_scatter(
        partial_out.astype(jnp.bfloat16), "ed", scatter_dimension=1, tiled=True
    ).astype(jnp.float32)
    weights_matrix = combine_matrix(expert_ids, route_weights, window, CAP)
    mixed = jnp.dot(
        weights_matrix,
        slot_out.reshape(window * CAP, features_dev),
        precision=lax.Precision.HIGHEST,
        preferred_element_type=jnp.float32,
    )
    return mixed.astype(jnp.bfloat16)


def solution(mesh):
    return jax.shard_map(
        local,
        mesh=mesh,
        in_specs=(
            P("ed", "fsdp"),
            P("ed", None),
            P("ed", None),
            P(None, "fsdp", "ed"),
            P(None, "fsdp", "ed"),
            P(None, "ed", "fsdp"),
        ),
        out_specs=P("ed", "fsdp"),
        check_vma=False,
    )
```

profile of v0, /device:TPU:1, one launch (start us, length us, event | category | flops | bytes accessed | tf_op | source)
XLA Modules:
  0.0 640.9 jit_solution(6663339600788899471)
XLA Ops:
  8.1 3.0 convert_reduce_fusion
  15.4 96.3 %all-gather.6.cloned.1.call-done = bf16[1,2592,384]{2,0,1:T(2,128)(2,1)} async-done(((bf16[1,81,384]{2,0,1:T(2,128)(2,1)}), bf16[1,2592,384]{2,0,1:T(2,128)(2,1)}) %all-gather.6.cloned.1.call-update) | async-done | bytes 1990672 | tf_op jit(solution)/shard_map/all_gather | solution.py:54
  112.2 15.8 %reduce.14 = bf16[2592,384]{1,0:T(8,128)(2,1)S(1)} reduce(bf16[2592,1,384]{2,1,0:T(2,128)(2,1)} %bitcast.80, bf16[]{:T(256)} %broadcast.283), dimensions={1}, to_apply=%bitcast.61.reduce_sub_computation | reduce | bytes 3981314
  128.0 1.6 reshape.463
  129.6 71.7 %all_to_all.33 = bf16[16,2,31104]{2,1,0:T(2,128)(2,1)S(1)} all-to-all(bf16[16,2,31104]{2,1,0:T(2,128)(2,1)} %reshape.463), channel_id=1, replica_groups=mesh['fsdp'=16,'ed'=32] {'fsdp'}, dimensions={0} | all-to-all | bytes 3981312 | tf_op jit(solution)/shard_map/all_to_all | solution.py:55
  201.2 8.9 %reshape.464 = bf16[2592,1,384]{2,1,0:T(2,128)(2,1)} reshape(bf16[16,2,31104]{2,1,0:T(2,128)(2,1)S(1)} %all_to_all.33) | data formatting | bytes 3981312
  210.2 17.6 %bitcast_reduce_fusion = bf16[2592,384]{1,0:T(8,128)(2,1)} fusion(bf16[2592,1,384]{2,1,0:T(2,128)(2,1)} %reshape.464), kind=kLoop, calls=%fused_computation.46 | loop fusion | bytes 3981312 | tf_op jit(solution)/shard_map/all_to_all | solution.py:55
  227.8 1.8 all_to_all.25
  230.6 2.7 fusion.5
  233.3 66.1 %all-gather.10.cloned.1.call-done = bf16[1,6144,256]{2,1,0:T(8,128)(2,1)} async-done(((bf16[1,384,256]{2,1,0:T(8,128)(2,1)}), bf16[1,6144,256]{2,1,0:T(8,128)(2,1)}) %all-gather.10.cloned.1.call-update) | async-done | bytes 3145744 | tf_op jit(solution)/shard_map/all_gather | solution.py:65
  299.3 85.3 %all-gather.12.cloned.1.call-done = bf16[1,256,6144]{2,1,0:T(8,128)(2,1)} async-done(((bf16[1,256,384]{2,1,0:T(8,128)(2,1)}), bf16[1,256,6144]{2,1,0:T(8,128)(2,1)}) %all-gather.12.cloned.1.call-update) | async-done | bytes 3145744 | tf_op jit(solution)/shard_map/all_gather | solution.py:74
  384.6 6.5 %fusion.1 = bf16[1,162,6144]{2,1,0:T(8,128)(2,1)} fusion(bf16[1,256,6144]{2,1,0:T(8,128)(2,1)} %all-gather.12.cloned.1.call-done, bf16[162,6144]{1,0:T(8,128)(2,1)S(1)} %bitcast.74, bf16[1,6144,256]{2,1,0:T(8,128)(2,1)} %all-gather.10.cloned.1.call-done, f32[162,256]{1,0:T(8,128)S(1)} %fusion.5), kind=kOutput, calls=%fused_computation.2 | convolution fusion | flops 1020460032 | bytes 10438656 | tf_op jit(solution)/shard_map/dot_general | solution.py:72
  391.1 13.7 %copy.20 = bf16[1,162,6144]{1,0,2:T(2,128)(2,1)} copy(bf16[1,162,6144]{2,1,0:T(8,128)(2,1)} %fusion.1) | data formatting | bytes 3981312 | tf_op jit(solution)/shard_map/stack | solution.py:76
  404.8 34.6 %reduce.15 = bf16[6144,162]{1,0:T(8,128)(2,1)S(1)} reduce(bf16[6144,1,162]{2,1,0:T(2,128)(2,1)} %bitcast.71, bf16[]{:T(256)} %broadcast.283), dimensions={1}, to_apply=%bitcast.63.reduce_sub_computation | reduce | bytes 3981314
  439.4 6.9 %reshape.465 = bf16[16,2,31104]{2,1,0:T(2,128)(2,1)} reshape(bf16[6144,162]{1,0:T(8,128)(2,1)S(1)} %reduce.15) | data formatting | bytes 3981312
  446.4 4.2 all-to-all-start.1
  450.7 42.9 %all-to-all-done.1 = bf16[16,2,31104]{2,1,0:T(2,128)(2,1)S(1)} async-done(((bf16[16,2,31104]{2,1,0:T(2,128)(2,1)}), bf16[16,2,31104]{2,1,0:T(2,128)(2,1)S(1)}, u32[]{:S(2)}, u32[]{:S(2)}) %all-to-all-start.1) | async-done | bytes 1990688 | tf_op jit(solution)/shard_map/all_to_all | solution.py:77
  493.5 12.1 %reshape.466 = bf16[6144,1,162]{2,1,0:T(2,128)(2,1)} reshape(bf16[16,2,31104]{2,1,0:T(2,128)(2,1)S(1)} %all-to-all-done.1) | data formatting | bytes 3981312
  505.6 13.8 %copy.21 = bf16[1,162,6144]{2,1,0:T(8,128)(2,1)S(1)} copy(bf16[1,162,6144]{1,0,2:T(2,128)(2,1)} %bitcast.72) | data formatting | bytes 3981312 | tf_op jit(solution)/shard_map/all_to_all | solution.py:77
  522.0 81.8 %fusion = bf16[96,384]{1,0:T(8,128)(2,1)S(1)} fusion(bf16[1,2592,384]{2,1,0:T(8,128)(2,1)} %all_to_all.30), kind=kCustom, calls=%all-reduce-scatter | all-reduce-scatter fusion | flops 1179649 | bytes 2066432
  603.9 3.5 collective-permute-start
  611.4 16.7 %collective-permute-start.4 = (bf16[81,384]{1,0:T(8,128)(2,1)S(1)}, bf16[81,384]{1,0:T(8,128)(2,1)S(1)}, u32[]{:S(2)}, u32[]{:S(2)}) collective-permute-start(bf16[81,384]{1,0:T(8,128)(2,1)S(1)} %slice.16), channel_id=1, source_target_pairs={{0,5},{1,6},{2,7},{3,8},{4,9},{5,10},{6,11},{7,12},{8,13},{9,14},{... | collective-permute-start | bytes 186632
  628.1 1.7 convert_multiply_fusion
  631.8 1.6 concatenate.3
  (55 shorter events, 16.2 us)
Async XLA Ops:
  6.5 4.6 copy-start
  6.5 105.1 %all-gather.6.cloned.1.call-start = ((), (), s32[]{:S(2)}) async-start(), calls=%async_computation.2 | async-start | bytes 4105728 | tf_op jit(solution)/shard_map/all_gather | solution.py:54
  13.3 217.3 %all-gather.8.cloned.1.call-start = ((), (), s32[]{:S(2)}) async-start(), calls=%async_computation.3 | async-start | bytes 3342336 | tf_op jit(solution)/shard_map/all_gather | solution.py:59
  14.1 285.3 %all-gather.10.cloned.1.call-start = ((), (), s32[]{:S(2)}) async-start(), calls=%async_computation.4 | async-start | bytes 3342336 | tf_op jit(solution)/shard_map/all_gather | solution.py:65
  14.8 369.8 %all-gather.12.cloned.1.call-start = ((), (), s32[]{:S(2)}) async-start(), calls=%async_computation.5 | async-start | bytes 3342336 | tf_op jit(solution)/shard_map/all_gather | solution.py:74
  446.4 4.2 copy-start.2
  446.4 4.3 copy-start.3
  446.4 47.1 %all-to-all-start.1 = ((bf16[16,2,31104]{2,1,0:T(2,128)(2,1)}), bf16[16,2,31104]{2,1,0:T(2,128)(2,1)S(1)}, u32[]{:S(2)}, u32[]{:S(2)}) async-start(bf16[16,2,31104]{2,1,0:T(2,128)(2,1)} %reshape.465), calls=%async_computation.1 | async-start | bytes 3981312 | tf_op jit(solution)/shard_map/all_to_all | solution.py:77
  520.5 113.9 %copy-start.1 = (bf16[288,384]{1,0:T(8,128)(2,1)S(1)}, bf16[288,384]{1,0:T(8,128)(2,1)}, u32[]{:S(2)}) copy-start(bf16[288,384]{1,0:T(8,128)(2,1)} %param.6) | copy-start | bytes 663556
  603.9 27.8 %collective-permute-start = (bf16[96,384]{1,0:T(8,128)(2,1)S(1)}, bf16[96,384]{1,0:T(8,128)(2,1)S(1)}, u32[]{:S(2)}, u32[]{:S(2)}) collective-permute-start(bf16[96,384]{1,0:T(8,128)(2,1)S(1)} %fusion), channel_id=1, source_target_pairs={{0,1},{1,2},{2,3},{3,4},{4,5},{5,6},{6,7},{7,8},{8,9},{9,10},{10,1... | collective-permute-start | bytes 221192
  607.5 24.3 %collective-permute-start.1 = (bf16[96,384]{1,0:T(8,128)(2,1)S(1)}, bf16[96,384]{1,0:T(8,128)(2,1)S(1)}, u32[]{:S(2)}, u32[]{:S(2)}) collective-permute-start(bf16[96,384]{1,0:T(8,128)(2,1)S(1)} %fusion), channel_id=1, source_target_pairs={{0,2},{1,3},{2,4},{3,5},{4,6},{5,7},{6,8},{7,9},{8,10},{9,11},{10,... | collective-permute-start | bytes 221192
  608.8 23.0 %collective-permute-start.2 = (bf16[96,384]{1,0:T(8,128)(2,1)S(1)}, bf16[96,384]{1,0:T(8,128)(2,1)S(1)}, u32[]{:S(2)}, u32[]{:S(2)}) collective-permute-start(bf16[96,384]{1,0:T(8,128)(2,1)S(1)} %fusion), channel_id=1, source_target_pairs={{0,3},{1,4},{2,5},{3,6},{4,7},{5,8},{6,9},{7,10},{8,11},{9,12},{10... | collective-permute-start | bytes 221192
  610.1 21.7 %collective-permute-start.3 = (bf16[96,384]{1,0:T(8,128)(2,1)S(1)}, bf16[96,384]{1,0:T(8,128)(2,1)S(1)}, u32[]{:S(2)}, u32[]{:S(2)}) collective-permute-start(bf16[96,384]{1,0:T(8,128)(2,1)S(1)} %fusion), channel_id=1, source_target_pairs={{0,4},{1,5},{2,6},{3,7},{4,8},{5,9},{6,10},{7,11},{8,12},{9,13},{1... | collective-permute-start | bytes 221192
  611.4 20.3 %collective-permute-start.4 = (bf16[81,384]{1,0:T(8,128)(2,1)S(1)}, bf16[81,384]{1,0:T(8,128)(2,1)S(1)}, u32[]{:S(2)}, u32[]{:S(2)}) collective-permute-start(bf16[81,384]{1,0:T(8,128)(2,1)S(1)} %slice.16), channel_id=1, source_target_pairs={{0,5},{1,6},{2,7},{3,8},{4,9},{5,10},{6,11},{7,12},{8,13},{9,14},{... | collective-permute-start | bytes 186632
Sparse Core Ops, SparseCore 0:
  13.4 98.1 all-gather.5
  113.7 100.7 all-gather.7
  216.6 82.7 all-gather.9
  301.3 83.2 all-gather.11
where the time goes:
time: 642 us; the launch traced here: 641 us
  waiting for transfers between devices  292 us (45%)
  blocking collectives  154 us (24%)
  local copies, waits for them, and re-layouts  85.7 us (13%)
  other arithmetic  56.5 us (9%)
  starting transfers between devices  28.5 us (4%)
  between operations  14.1 us (2%)
  matrix products  10.2 us (2%)
    all_gather x1, waiting for transfers between devices, local(): selected = lax.all_gather(own_slots, 'ed', axis=1, tiled=True)  96.3 us
    all_gather x1, waiting for transfers between devices, local(): lax.all_gather(w_down[0], 'fsdp', axis=1, tiled=True)  85.3 us
    unnamed x1, blocking collectives  81.8 us
    all_to_all x1, blocking collectives, local(): lax.all_to_all(selected, 'fsdp', split_axis=1, concat_axis=2, tiled=True)  71.7 us
    all_gather x1, waiting for transfers between devices, local(): lax.all_gather(w_up, 'fsdp', axis=1, tiled=True)  66.1 us
    unnamed x2, other arithmetic  50.5 us
    all_to_all x1, waiting for transfers between devices, local(): lax.all_to_all(stacked, 'fsdp', split_axis=2, concat_axis=1, tiled=True)  42.9 us
    unnamed x19, local copies, waits for them, and re-layouts  34.1 us
  transfers between devices with their start and end apart: 10, of which 4 were waited for; matrix products, arithmetic and copies ran while one was open for 8% of the time, Pallas kernels for 0%

commit v1 on v0

--- a/solution.py
+++ b/solution.py
@@ -50,35 +50,25 @@
 def local(tokens, expert_ids, route_weights, w_gate, w_up, w_down):
     window = w_gate.shape[0]
     features_dev = tokens.shape[1]
-    own_slots = pick_rows(tokens[None], expert_ids[None], window, CAP)[0]
-    selected = lax.all_gather(own_slots, "ed", axis=1, tiled=True)
-    rows_full = lax.all_to_all(selected, "fsdp", split_axis=1, concat_axis=2, tiled=True)
-    gate_part = jnp.einsum(
-        "hnm,hmq->hnq",
-        rows_full,
-        lax.all_gather(w_gate, "fsdp", axis=1, tiled=True),
-        preferred_element_type=jnp.float32,
-    )
-    up_part = jnp.einsum(
-        "hnm,hmq->hnq",
-        rows_full,
-        lax.all_gather(w_up, "fsdp", axis=1, tiled=True),
-        preferred_element_type=jnp.float32,
-    )
+    hidden_dev = w_gate.shape[2]
+    n_ed = lax.axis_size("ed")
+    own_slots = pick_rows(tokens[None], expert_ids[None], window, CAP)[0, 0]
+    selected = lax.all_gather(own_slots, "ed", axis=0, tiled=True)
+    both = jnp.concatenate([w_gate[0], w_up[0]], axis=1)
+    partial = jnp.dot(selected, both, preferred_element_type=jnp.float32)
+    n_fsdp = lax.axis_size("fsdp")
+    rows = partial.shape[0]
+    band = -(-rows // (8 * n_fsdp)) * 8
+    partial = jnp.pad(partial, ((0, band * n_fsdp - rows), (0, 0)))
+    summed = lax.psum_scatter(partial, "fsdp", scatter_dimension=0, tiled=True)
+    gate_part = summed[:, :hidden_dev]
+    up_part = summed[:, hidden_dev:]
     activation = (jax.nn.silu(gate_part) * up_part).astype(jnp.bfloat16)
-    act_one = activation[0]
-
-    def columns_out(shard_piece, first_col, act_one=act_one):
-        return jnp.dot(act_one, shard_piece, preferred_element_type=jnp.float32)
-
-    whole_rows = columns_out(lax.all_gather(w_down[0], "fsdp", axis=1, tiled=True), jnp.int32(0))
-    outputs_list = [whole_rows.astype(jnp.bfloat16)]
-    stacked = jnp.stack(outputs_list)
-    exchanged = lax.all_to_all(stacked, "fsdp", split_axis=2, concat_axis=1, tiled=True)
-    partial_out = exchanged.astype(jnp.float32)
-    slot_out = lax.psum_scatter(
-        partial_out.astype(jnp.bfloat16), "ed", scatter_dimension=1, tiled=True
-    ).astype(jnp.float32)
+    act_rows = lax.all_gather(activation, "fsdp", axis=0, tiled=True)[:rows]
+    term = jnp.dot(act_rows, w_down[0], preferred_element_type=jnp.float32)
+    term = term.astype(jnp.bfloat16).reshape(n_ed, CAP, features_dev)
+    arrived = lax.all_to_all(term, "ed", split_axis=0, concat_axis=0, tiled=True)
+    slot_out = jnp.sum(arrived.astype(jnp.float32), axis=0)
     weights_matrix = combine_matrix(expert_ids, route_weights, window, CAP)
     mixed = jnp.dot(
         weights_matrix,

time: 642 us -> 386 us (0.60)
  blocking collectives: 154 us -> 0 us
  local copies, waits for them, and re-layouts: 85.7 us -> 8.17 us
  other arithmetic: 56.5 us -> 7.01 us
  waiting for transfers between devices: 292 us -> 333 us
  starting transfers between devices: 28.5 us -> 19.6 us
    reduce_scatter x0 -> x1, waiting for transfers between devices: none -> 123 us  [local(): summed = lax.psum_scatter(partial, 'fsdp', scatter_dimension=0, tiled=True)]
    all_gather x4 -> x2, waiting for transfers between devices: 248 us -> 158 us  [the longest x1 92.2 us: local(): selected = lax.all_gather(own_slots, 'ed', axis=0, tiled=True)]
    unnamed x1 -> x0, blocking collectives: 81.8 us -> none
    all_to_all x1 -> x0, blocking collectives: 71.7 us -> none  [local(): lax.all_to_all(selected, 'fsdp', split_axis=1, concat_axis=2, tiled=True)]
    unnamed x2 -> x1, other arithmetic: 50.5 us -> 0.73 us
    all_to_all x7 -> x0, local copies, waits for them, and re-layouts: 35.6 us -> none  [the longest x3 19.6 us: local(): lax.all_to_all(selected, 'fsdp', split_axis=1, concat_axis=2, tiled=True)]
    unnamed x19 -> x13, local copies, waits for them, and re-layouts: 34.1 us -> 1.91 us
    unnamed x5 -> x0, starting transfers between devices: 24.1 us -> none
  transfers between devices with their start and end apart: 10 -> 4, of which waited for: 4 -> 4; matrix products, arithmetic and copies ran while one was open for 8% -> 0% of each run, Pallas kernels for 0% -> 0%
where the time goes in v1:
time: 386 us
  waiting for transfers between devices  333 us (86%)
  starting transfers between devices  19.6 us (5%)
  between operations  13.2 us (3%)
  local copies, waits for them, and re-layouts  8.17 us (2%)
  other arithmetic  7.01 us (2%)
  matrix products  5.01 us (1%)
    reduce_scatter x1, waiting for transfers between devices, local(): summed = lax.psum_scatter(partial, 'fsdp', scatter_dimension=0, tiled=True)  123 us
    all_gather x1, waiting for transfers between devices, local(): selected = lax.all_gather(own_slots, 'ed', axis=0, tiled=True)  92.2 us
    all_gather x1, waiting for transfers between devices, local(): act_rows = lax.all_gather(activation, 'fsdp', axis=0, tiled=True)[:rows]  65.5 us
    all_to_all x1, waiting for transfers between devices, local(): lax.all_to_all(term, 'ed', split_axis=0, concat_axis=0, tiled=True)  52.3 us
    all_to_all x1, starting transfers between devices, local(): lax.all_to_all(term, 'ed', split_axis=0, concat_axis=0, tiled=True)  19.5 us
  transfers between devices with their start and end apart: 4, of which 4 were waited for; matrix products, arithmetic and copies ran while one was open for 0% of the time, Pallas kernels for 0%

profile of v1, /device:TPU:1, one launch (start us, length us, event | category | flops | bytes accessed | tf_op | source)
XLA Modules:
  0.0 385.9 jit_solution(4538146092871331298)
XLA Ops:
  6.5 0.7 fusion.18
  7.3 0.3 reduce-window.6
  7.6 0.2 slice_reduce_fusion
  7.8 0.2 reduce-window.9
  8.0 0.1 broadcast.184
  8.1 3.0 convert_reduce_fusion.1
  11.1 1.3 gather_fusion
  12.4 0.7 select_bitcast_fusion
  13.2 0.0 reduce-scatter.2.cloned.1.call-start
  13.3 92.2 %all-gather.6.cloned.1.call-done = bf16[32,81,384]{2,1,0:T(8,128)(2,1)} async-done(((bf16[1,81,384]{2,1,0:T(8,128)(2,1)}), bf16[32,81,384]{2,1,0:T(8,128)(2,1)}) %all-gather.6.cloned.1.call-update) | async-done | bytes 1990672 | tf_op jit(solution)/shard_map/all_gather | solution.py:56
  105.5 1.9 reshape.322
  107.4 1.5 fusion.1
  108.9 3.0 pad.9
  111.9 0.0 reduce-scatter.2.cloned.1.call-update
  111.9 0.0 all-gather.4.cloned.1.call-start
  112.0 122.9 %reduce-scatter.2.cloned.1.call-done = f32[168,512]{1,0:T(8,128)} async-done(((f32[2688,512]{1,0:T(8,128)}), f32[168,512]{1,0:T(8,128)}) %reduce-scatter.2.cloned.1.call-update) | async-done | bytes 344080 | tf_op jit(solution)/shard_map/reduce_scatter | solution.py:63
  234.9 1.7 fusion.6
  236.6 65.5 %all-gather.4.cloned.1.call-done = bf16[2688,256]{1,0:T(8,128)(2,1)} async-done(((bf16[168,256]{1,0:T(8,128)(2,1)}), bf16[2688,256]{1,0:T(8,128)(2,1)}) %all-gather.4.cloned.1.call-update) | async-done | bytes 1376272 | tf_op jit(solution)/shard_map/all_gather | solution.py:67
  302.1 2.2 convolution_convert_fusion
  304.2 1.7 reshape.310
  305.9 19.5 %all-to-all-start = ((bf16[32,81,384]{2,1,0:T(8,128)(2,1)}), bf16[32,81,384]{2,1,0:T(8,128)(2,1)S(1)}, u32[]{:S(2)}, u32[]{:S(2)}) async-start(bf16[32,81,384]{2,1,0:T(8,128)(2,1)} %reshape.310), calls=%async_computation.1 | async-start | bytes 4325376 | tf_op jit(solution)/shard_map/all_to_all | solution.py:70
  325.5 52.3 %all-to-all-done = bf16[32,81,384]{2,1,0:T(8,128)(2,1)S(1)} async-done(((bf16[32,81,384]{2,1,0:T(8,128)(2,1)}), bf16[32,81,384]{2,1,0:T(8,128)(2,1)S(1)}, u32[]{:S(2)}, u32[]{:S(2)}) %all-to-all-start) | async-done | bytes 1990688 | tf_op jit(solution)/shard_map/all_to_all | solution.py:70
  377.8 0.3 convert_reduce_fusion
  378.1 1.3 convolution_convert_fusion.1
  (26 shorter events, 0.2 us)
Async XLA Ops:
  6.5 4.6 %copy-start = (bf16[288,384]{1,0:T(8,128)(2,1)S(1)}, bf16[288,384]{1,0:T(8,128)(2,1)}, u32[]{:S(2)}) copy-start(bf16[288,384]{1,0:T(8,128)(2,1)} %param.6) | copy-start | bytes 663556
  6.5 98.9 %all-gather.6.cloned.1.call-start = ((), (), s32[]{:S(2)}) async-start(), calls=%async_computation.4 | async-start | bytes 2230272 | tf_op jit(solution)/shard_map/all_gather | solution.py:56
  13.2 94.2 %copy-start.1 = (bf16[1,384,256]{2,1,0:T(8,128)(2,1)S(1)}, bf16[1,384,256]{2,1,0:T(8,128)(2,1)}, u32[]{:S(2)}) copy-start(bf16[1,384,256]{2,1,0:T(8,128)(2,1)} %param.10) | copy-start | bytes 589828
  13.2 94.2 %copy-start.2 = (bf16[1,384,256]{2,1,0:T(8,128)(2,1)S(1)}, bf16[1,384,256]{2,1,0:T(8,128)(2,1)}, u32[]{:S(2)}) copy-start(bf16[1,384,256]{2,1,0:T(8,128)(2,1)} %param.9) | copy-start | bytes 589828
  13.2 221.7 %reduce-scatter.2.cloned.1.call-start = ((), (), s32[]{:S(2)}) async-start(), calls=%async_computation.2 | async-start | bytes 5849088 | tf_op jit(solution)/shard_map/reduce_scatter | solution.py:63
  111.9 190.1 %copy-start.3 = (bf16[1,256,384]{2,1,0:T(8,128)(2,1)S(1)}, bf16[1,256,384]{2,1,0:T(8,128)(2,1)}, u32[]{:S(2)}) copy-start(bf16[1,256,384]{2,1,0:T(8,128)(2,1)} %param.11) | copy-start | bytes 589828
  111.9 190.1 %all-gather.4.cloned.1.call-start = ((), (), s32[]{:S(2)}) async-start(), calls=%async_computation.3 | async-start | bytes 1462272 | tf_op jit(solution)/shard_map/all_gather | solution.py:67
  305.9 19.5 %copy-start.4 = (s32[288,2]{0,1:T(2,128)S(1)}, s32[288,2]{0,1:T(2,128)}, u32[]{:S(2)}) copy-start(s32[288,2]{0,1:T(2,128)} %param.7) | copy-start | bytes 6916
  305.9 19.6 %copy-start.5 = (f32[288,2]{0,1:T(2,128)S(1)}, f32[288,2]{0,1:T(2,128)}, u32[]{:S(2)}) copy-start(f32[288,2]{0,1:T(2,128)} %param.8) | copy-start | bytes 6916
  305.9 71.9 %all-to-all-start = ((bf16[32,81,384]{2,1,0:T(8,128)(2,1)}), bf16[32,81,384]{2,1,0:T(8,128)(2,1)S(1)}, u32[]{:S(2)}, u32[]{:S(2)}) async-start(bf16[32,81,384]{2,1,0:T(8,128)(2,1)} %reshape.310), calls=%async_computation.1 | async-start | bytes 4325376 | tf_op jit(solution)/shard_map/all_to_all | solution.py:70
Sparse Core Ops, SparseCore 0:
  13.3 92.1 all-gather.5
  112.1 122.7 reduce-scatter.1
  237.2 64.8 all-gather.3

commit v2 on v1

--- a/solution.py
+++ b/solution.py
@@ -1,9 +1,14 @@
+import functools
+
 import jax
 import jax.numpy as jnp
 from jax import lax
+from jax.experimental import pallas as pl
+from jax.experimental.pallas import tpu as pltpu
 from jax.sharding import PartitionSpec as P
 
 CAP = 81
+MESH = pl.DeviceIdType.MESH
 
 
 def slot_match(routes, window, capacity):
@@ -47,28 +52,101 @@
     )
 
 
+def _exchange_kernel(axis, n, gather, x_ref, o_ref, send_sem, recv_sem, own_sem):
+    me = lax.axis_index(axis)
+
+    def peer_of(i):
+        return lax.rem(me + 1 + i, n)
+
+    def source(peer):
+        return x_ref if gather else x_ref.at[peer]
+
+    def outgoing(peer):
+        return pltpu.make_async_remote_copy(
+            src_ref=source(peer),
+            dst_ref=o_ref.at[me],
+            send_sem=send_sem.at[peer],
+            recv_sem=recv_sem.at[me],
+            device_id={axis: peer},
+            device_id_type=MESH,
+        )
+
+    def incoming(peer):
+        return pltpu.make_async_remote_copy(
+            src_ref=source(peer),
+            dst_ref=o_ref.at[peer],
+            send_sem=send_sem.at[peer],
+            recv_sem=recv_sem.at[peer],
+            device_id={axis: peer},
+            device_id_type=MESH,
+        )
+
+    barrier = pltpu.get_barrier_semaphore()
+
+    def greet(i, carry):
+        pl.semaphore_signal(barrier, 1, device_id={axis: peer_of(i)}, device_id_type=MESH)
+        return carry
+
+    lax.fori_loop(0, n - 1, greet, 0)
+    pl.semaphore_wait(barrier, n - 1)
+
+    def send(i, carry):
+        outgoing(peer_of(i)).start()
+        return carry
+
+    lax.fori_loop(0, n - 1, send, 0)
+    own = pltpu.make_async_copy(source(me), o_ref.at[me], own_sem)
+    own.start()
+
+    def finish(i, carry):
+        peer = peer_of(i)
+        outgoing(peer).wait_send()
+        incoming(peer).wait_recv()
+        return carry
+
+    lax.fori_loop(0, n - 1, finish, 0)
+    own.wait()
+
+
+def exchange(x, axis, n, gather, cid):
+    block = x.shape if gather else x.shape[1:]
+    return pl.pallas_call(
+        functools.partial(_exchange_kernel, axis, n, gather),
+        out_shape=jax.ShapeDtypeStruct((n,) + tuple(block), x.dtype),
+        in_specs=[pl.BlockSpec(memory_space=pl.ANY)],
+        out_specs=pl.BlockSpec(memory_space=pl.ANY),
+        scratch_shapes=[
+            pltpu.SemaphoreType.DMA((n,)),
+            pltpu.SemaphoreType.DMA((n,)),
+            pltpu.SemaphoreType.DMA,
+        ],
+        compiler_params=pltpu.CompilerParams(collective_id=cid, has_side_effects=True),
+    )(x)
+
+
 def local(tokens, expert_ids, route_weights, w_gate, w_up, w_down):
     window = w_gate.shape[0]
     features_dev = tokens.shape[1]
     hidden_dev = w_gate.shape[2]
     n_ed = lax.axis_size("ed")
+    n_fsdp = lax.axis_size("fsdp")
+    per_band = n_ed // n_fsdp
     own_slots = pick_rows(tokens[None], expert_ids[None], window, CAP)[0, 0]
-    selected = lax.all_gather(own_slots, "ed", axis=0, tiled=True)
+    selected = exchange(own_slots, "ed", n_ed, True, 0)
+    selected = selected.reshape(n_fsdp, per_band, CAP, features_dev)
     both = jnp.concatenate([w_gate[0], w_up[0]], axis=1)
-    partial = jnp.dot(selected, both, preferred_element_type=jnp.float32)
-    n_fsdp = lax.axis_size("fsdp")
-    rows = partial.shape[0]
-    band = -(-rows // (8 * n_fsdp)) * 8
-    partial = jnp.pad(partial, ((0, band * n_fsdp - rows), (0, 0)))
-    summed = lax.psum_scatter(partial, "fsdp", scatter_dimension=0, tiled=True)
-    gate_part = summed[:, :hidden_dev]
-    up_part = summed[:, hidden_dev:]
+    partial = jnp.einsum("fbri,ih->fbrh", selected, both, preferred_element_type=jnp.float32)
+    arrived = exchange(partial, "fsdp", n_fsdp, False, 1)
+    summed = jnp.sum(arrived, axis=0)
+    gate_part = summed[..., :hidden_dev]
+    up_part = summed[..., hidden_dev:]
     activation = (jax.nn.silu(gate_part) * up_part).astype(jnp.bfloat16)
-    act_rows = lax.all_gather(activation, "fsdp", axis=0, tiled=True)[:rows]
-    term = jnp.dot(act_rows, w_down[0], preferred_element_type=jnp.float32)
-    term = term.astype(jnp.bfloat16).reshape(n_ed, CAP, features_dev)
-    arrived = lax.all_to_all(term, "ed", split_axis=0, concat_axis=0, tiled=True)
-    slot_out = jnp.sum(arrived.astype(jnp.float32), axis=0)
+    act_rows = exchange(activation, "fsdp", n_fsdp, True, 2)
+    act_rows = act_rows.reshape(n_ed, CAP, hidden_dev)
+    term = jnp.einsum("brh,hd->brd", act_rows, w_down[0], preferred_element_type=jnp.float32)
+    term = term.astype(jnp.bfloat16)
+    pieces = exchange(term, "ed", n_ed, False, 3)
+    slot_out = jnp.sum(pieces.astype(jnp.float32), axis=0)
     weights_matrix = combine_matrix(expert_ids, route_weights, window, CAP)
     mixed = jnp.dot(
         weights_matrix,

time: 386 us -> 331 us (0.86)
  waiting for transfers between devices: 333 us -> 0 us
  Pallas kernels: 0 us -> 307 us
  starting transfers between devices: 19.6 us -> 0 us
  between operations: 13.2 us -> 0.14 us
  local copies, waits for them, and re-layouts: 8.17 us -> 1.63 us
  matrix products: 5.01 us -> 10.7 us
  other arithmetic: 7.01 us -> 11.1 us
    pallas_call x0 -> x4, Pallas kernels: none -> 307 us  [exchange(): pl.pallas_call(functools.partial(_exchange_kernel, axis, n, gather), out_...]
    all_gather x2 -> x0, waiting for transfers between devices: 158 us -> none  [the longest x1 92.2 us: local(): selected = lax.all_gather(own_slots, 'ed', axis=0, tiled=True)]
    reduce_scatter x1 -> x0, waiting for transfers between devices: 123 us -> none  [local(): summed = lax.psum_scatter(partial, 'fsdp', scatter_dimension=0, tiled=True)]
    all_to_all x1 -> x0, waiting for transfers between devices: 52.3 us -> none  [local(): lax.all_to_all(term, 'ed', split_axis=0, concat_axis=0, tiled=True)]
    all_to_all x1 -> x0, starting transfers between devices: 19.5 us -> none  [local(): lax.all_to_all(term, 'ed', split_axis=0, concat_axis=0, tiled=True)]
    dot_general x2, matrix products: 3.71 us -> 9.38 us  [the longest x1 5.76 us: local(): jnp.einsum('fbri,ih->fbrh', selected, both, preferred_element_type=jnp.fl...]
    reduce_sum x1 -> x2, other arithmetic: 0.31 us -> 5.32 us  [the longest x1 3.39 us: local(): summed = jnp.sum(arrived, axis=0)]
  transfers between devices with their start and end apart: 4 -> 0, of which waited for: 4 -> 0; matrix products, arithmetic and copies ran while one was open for 0% -> 0% of each run, Pallas kernels for 0% -> 0%
where the time goes in v2:
time: 331 us; the launch traced here: 330 us
  Pallas kernels  307 us (93%)
  other arithmetic  11.1 us (3%)
  matrix products  10.7 us (3%)
    pallas_call x4, Pallas kernels, exchange(): pl.pallas_call(functools.partial(_exchange_kernel, axis, n, gather), out_...  307 us

profile of v2, /device:TPU:1, one launch (start us, length us, event | category | flops | bytes accessed | tf_op | source)
XLA Modules:
  0.0 330.4 jit_solution(5554821112701952699)
XLA Ops:
  0.0 0.0 copy-start
  0.0 0.8 fusion.16
  0.8 0.3 reduce-window.6
  1.1 0.2 slice_reduce_fusion
  1.3 0.2 reduce-window.9
  1.5 0.1 broadcast.182
  1.6 3.0 convert_reduce_fusion.1
  4.6 0.0 copy-done
  4.6 1.3 gather_fusion
  5.9 0.7 select_select_fusion.x_ref
  6.7 65.5 %shard_map.64 = bf16[32,81,384]{2,1,0:T(8,128)(2,1)} custom-call(bf16[81,384]{1,0:T(8,128)(2,1)} %select_select_fusion.x_ref), custom_call_target="tpu_custom_call" | custom-call | tf_op jit(solution)/shard_map/pallas_call | solution.py:113
  72.2 5.8 %fusion.x_ref = f32[16,2,81,512]{3,2,1,0:T(8,128)} fusion(bf16[16,2,81,384]{3,2,1,0:T(8,128)(2,1)} %bitcast.30, bf16[384,256]{1,0:T(8,128)(2,1)S(1)} %bitcast.32, bf16[384,256]{1,0:T(8,128)(2,1)S(1)} %bitcast.33), kind=kOutput, calls=%fused_computation.6 | convolution fusion | flops 1020002304 | bytes 7692288 | tf_op jit(solution)/shard_map/fbri,ih->fbrh/dot_general | solution.py:138
  78.0 132.0 %shard_map.65 = f32[16,2,81,512]{3,2,1,0:T(8,128)} custom-call(f32[16,2,81,512]{3,2,1,0:T(8,128)} %fusion.x_ref), custom_call_target="tpu_custom_call" | custom-call | tf_op jit(solution)/shard_map/pallas_call | solution.py:113
  210.0 0.0 copy-start.3
  210.0 3.4 %reduce_sum.51 = f32[2,81,512]{2,1,0:T(8,128)S(1)} reduce(f32[16,2,81,512]{3,2,1,0:T(8,128)} %shard_map.65, f32[]{:T(128)} %constant.15.clone.1), dimensions={0}, to_apply=%region_6.7 | reduce | flops 1244160 | bytes 5640196 | tf_op jit(solution)/shard_map/reduce_sum | solution.py:140
  213.4 0.7 fusion.4.x_ref
  214.1 47.7 %shard_map.66 = bf16[16,2,81,256]{3,2,1,0:T(8,128)(2,1)} custom-call(bf16[2,81,256]{2,1,0:T(8,128)(2,1)} %fusion.4.x_ref), custom_call_target="tpu_custom_call" | custom-call | tf_op jit(solution)/shard_map/pallas_call | solution.py:113
  261.9 0.0 copy-done.3
  261.9 3.6 %convolution_convert_fusion.x_ref = bf16[32,81,384]{2,1,0:T(8,128)(2,1)} fusion(bf16[32,81,256]{2,1,0:T(8,128)(2,1)} %bitcast.31, bf16[1,256,384]{2,1,0:T(8,128)(2,1)S(1)} %copy-done.3), kind=kOutput, calls=%fused_computation.2 | convolution fusion | flops 510603264 | bytes 3514368 | tf_op jit(solution)/shard_map/brh,hd->brd/dot_general | solution.py:146
  265.5 61.6 %shard_map.67 = bf16[32,81,384]{2,1,0:T(8,128)(2,1)} custom-call(bf16[32,81,384]{2,1,0:T(8,128)(2,1)} %convolution_convert_fusion.x_ref), custom_call_target="tpu_custom_call" | custom-call | tf_op jit(solution)/shard_map/pallas_call | solution.py:113
  327.1 0.0 copy-start.4
  327.2 0.0 copy-start.5
  327.2 1.9 convert_reduce_fusion
  329.1 1.3 convolution_convert_fusion.1
  (17 shorter events, 0.2 us)
Async XLA Ops:
  0.0 4.6 %copy-start = (bf16[288,384]{1,0:T(8,128)(2,1)S(1)}, bf16[288,384]{1,0:T(8,128)(2,1)}, u32[]{:S(2)}) copy-start(bf16[288,384]{1,0:T(8,128)(2,1)} %param.6) | copy-start | bytes 663556
  0.0 72.2 %copy-start.2 = (bf16[1,384,256]{2,1,0:T(8,128)(2,1)S(1)}, bf16[1,384,256]{2,1,0:T(8,128)(2,1)}, u32[]{:S(2)}) copy-start(bf16[1,384,256]{2,1,0:T(8,128)(2,1)} %param.9) | copy-start | bytes 589828
  0.0 72.2 %copy-start.1 = (bf16[1,384,256]{2,1,0:T(8,128)(2,1)S(1)}, bf16[1,384,256]{2,1,0:T(8,128)(2,1)}, u32[]{:S(2)}) copy-start(bf16[1,384,256]{2,1,0:T(8,128)(2,1)} %param.10) | copy-start | bytes 589828
  210.0 51.9 %copy-start.3 = (bf16[1,256,384]{2,1,0:T(8,128)(2,1)S(1)}, bf16[1,256,384]{2,1,0:T(8,128)(2,1)}, u32[]{:S(2)}) copy-start(bf16[1,256,384]{2,1,0:T(8,128)(2,1)} %param.11) | copy-start | bytes 589828
  327.1 2.0 copy-start.4
  327.2 2.0 copy-start.5

commit v3 on v2

--- a/solution.py
+++ b/solution.py
@@ -136,8 +136,8 @@
     selected = selected.reshape(n_fsdp, per_band, CAP, features_dev)
     both = jnp.concatenate([w_gate[0], w_up[0]], axis=1)
     partial = jnp.einsum("fbri,ih->fbrh", selected, both, preferred_element_type=jnp.float32)
-    arrived = exchange(partial, "fsdp", n_fsdp, False, 1)
-    summed = jnp.sum(arrived, axis=0)
+    arrived = exchange(partial.astype(jnp.bfloat16), "fsdp", n_fsdp, False, 1)
+    summed = jnp.sum(arrived.astype(jnp.float32), axis=0)
     gate_part = summed[..., :hidden_dev]
     up_part = summed[..., hidden_dev:]
     activation = (jax.nn.silu(gate_part) * up_part).astype(jnp.bfloat16)

time: 331 us -> 261 us (0.79)
  Pallas kernels: 307 us -> 239 us
    pallas_call x4, Pallas kernels: 307 us -> 239 us  [exchange(): pl.pallas_call(functools.partial(_exchange_kernel, axis, n, gather), out_...]
where the time goes in v3:
time: 261 us
  Pallas kernels  239 us (92%)
  other arithmetic  9.99 us (4%)
  matrix products  9.79 us (4%)
    pallas_call x4, Pallas kernels, exchange(): pl.pallas_call(functools.partial(_exchange_kernel, axis, n, gather), out_...  239 us

profile of v3, /device:TPU:1, one launch (start us, length us, event | category | flops | bytes accessed | tf_op | source)
XLA Modules:
  0.0 260.9 jit_solution(2629607282055558899)
XLA Ops:
  0.0 0.0 copy-start
  0.0 0.8 fusion.15
  0.8 0.3 reduce-window.6
  1.1 0.2 slice_reduce_fusion
  1.3 0.2 reduce-window.9
  1.5 0.1 broadcast.182
  1.6 3.0 %convert_reduce_fusion.2 = (s32[81]{0:T(128)S(1)}, s32[81]{0:T(128)S(1)}) fusion(pred[288]{0:T(512)(128)(4,1)S(1)} %fusion.15, s32[288]{0:T(512)S(1)} %fusion.14), kind=kLoop, calls=%fused_computation.19 | loop fusion | flops 139806 | bytes 2088 | tf_op jit(solution)/shard_map/reduce_sum | solution.py:33
  4.6 1.3 gather_fusion
  5.9 0.7 select_select_fusion.x_ref
  6.7 65.5 %shard_map.64 = bf16[32,81,384]{2,1,0:T(8,128)(2,1)} custom-call(bf16[81,384]{1,0:T(8,128)(2,1)} %select_select_fusion.x_ref), custom_call_target="tpu_custom_call" | custom-call | tf_op jit(solution)/shard_map/pallas_call | solution.py:113
  72.2 4.9 %convolution_convert_fusion.x_ref = bf16[16,2,81,512]{3,2,1,0:T(8,128)(2,1)} fusion(bf16[16,2,81,384]{3,2,1,0:T(8,128)(2,1)} %bitcast.31, bf16[384,256]{1,0:T(8,128)(2,1)S(1)} %bitcast.34, bf16[384,256]{1,0:T(8,128)(2,1)S(1)} %bitcast.35), kind=kOutput, calls=%fused_computation.3 | convolution fusion | flops 1021329408 | bytes 5038080 | tf_op jit(solution)/shard_map/fbri,ih->fbrh/dot_general | solution.py:138
  77.1 70.2 %shard_map.65 = bf16[16,2,81,512]{3,2,1,0:T(8,128)(2,1)} custom-call(bf16[16,2,81,512]{3,2,1,0:T(8,128)(2,1)} %convolution_convert_fusion.x_ref), custom_call_target="tpu_custom_call" | custom-call | tf_op jit(solution)/shard_map/pallas_call | solution.py:113
  147.3 0.0 copy-start.1
  147.3 2.3 convert_reduce_fusion
  149.7 0.7 fusion.3.x_ref
  150.3 43.9 %shard_map.66 = bf16[16,2,81,256]{3,2,1,0:T(8,128)(2,1)} custom-call(bf16[2,81,256]{2,1,0:T(8,128)(2,1)} %fusion.3.x_ref), custom_call_target="tpu_custom_call" | custom-call | tf_op jit(solution)/shard_map/pallas_call | solution.py:113
  194.3 3.6 %convolution_convert_fusion.1.x_ref = bf16[32,81,384]{2,1,0:T(8,128)(2,1)} fusion(bf16[32,81,256]{2,1,0:T(8,128)(2,1)} %bitcast.30, bf16[1,256,384]{2,1,0:T(8,128)(2,1)S(1)} %copy-done.1), kind=kOutput, calls=%fused_computation.4 | convolution fusion | flops 510603264 | bytes 3514368 | tf_op jit(solution)/shard_map/brh,hd->brd/dot_general | solution.py:146
  197.9 59.7 %shard_map.67 = bf16[32,81,384]{2,1,0:T(8,128)(2,1)} custom-call(bf16[32,81,384]{2,1,0:T(8,128)(2,1)} %convolution_convert_fusion.1.x_ref), custom_call_target="tpu_custom_call" | custom-call | tf_op jit(solution)/shard_map/pallas_call | solution.py:113
  257.6 0.0 copy-start.2
  257.6 0.0 copy-start.3
  257.7 1.9 convert_reduce_fusion.1
  259.6 0.0 copy-done.2
  259.6 0.0 copy-done.3
  259.6 1.3 convolution_convert_fusion.2
  (17 shorter events, 0.2 us)
Async XLA Ops:
  0.0 4.6 %copy-start = (bf16[288,384]{1,0:T(8,128)(2,1)S(1)}, bf16[288,384]{1,0:T(8,128)(2,1)}, u32[]{:S(2)}) copy-start(bf16[288,384]{1,0:T(8,128)(2,1)} %param.6) | copy-start | bytes 663556
  0.0 72.2 %copy-start.5 = (bf16[1,384,256]{2,1,0:T(8,128)(2,1)S(1)}, bf16[1,384,256]{2,1,0:T(8,128)(2,1)}, u32[]{:S(2)}) copy-start(bf16[1,384,256]{2,1,0:T(8,128)(2,1)} %param.9) | copy-start | bytes 589828
  0.0 72.2 %copy-start.4 = (bf16[1,384,256]{2,1,0:T(8,128)(2,1)S(1)}, bf16[1,384,256]{2,1,0:T(8,128)(2,1)}, u32[]{:S(2)}) copy-start(bf16[1,384,256]{2,1,0:T(8,128)(2,1)} %param.10) | copy-start | bytes 589828
  147.3 47.0 %copy-start.1 = (bf16[1,256,384]{2,1,0:T(8,128)(2,1)S(1)}, bf16[1,256,384]{2,1,0:T(8,128)(2,1)}, u32[]{:S(2)}) copy-start(bf16[1,256,384]{2,1,0:T(8,128)(2,1)} %param.11) | copy-start | bytes 589828
  257.6 2.0 copy-start.2
  257.6 2.0 copy-start.3

commit v4 on v3

--- a/solution.py
+++ b/solution.py
@@ -52,72 +52,77 @@
     )
 
 
-def _exchange_kernel(axis, n, gather, x_ref, o_ref, send_sem, recv_sem, own_sem):
+def _exchange_kernel(axis, m, stride, gather, x_ref, o_ref, send_sem, recv_sem, own_sem):
     me = lax.axis_index(axis)
+    k = lax.rem(me // stride, m)
+    base = me - k * stride
 
-    def peer_of(i):
-        return lax.rem(me + 1 + i, n)
+    def member(i):
+        return lax.rem(k + 1 + i, m)
 
-    def source(peer):
-        return x_ref if gather else x_ref.at[peer]
+    def device(j):
+        return {axis: base + j * stride}
 
-    def outgoing(peer):
+    def source(j):
+        return x_ref if gather else x_ref.at[j]
+
+    def outgoing(j):
         return pltpu.make_async_remote_copy(
-            src_ref=source(peer),
-            dst_ref=o_ref.at[me],
-            send_sem=send_sem.at[peer],
-            recv_sem=recv_sem.at[me],
-            device_id={axis: peer},
+            src_ref=source(j),
+            dst_ref=o_ref.at[k],
+            send_sem=send_sem.at[j],
+            recv_sem=recv_sem.at[k],
+            device_id=device(j),
             device_id_type=MESH,
         )
 
-    def incoming(peer):
+    def incoming(j):
         return pltpu.make_async_remote_copy(
-            src_ref=source(peer),
-            dst_ref=o_ref.at[peer],
-            send_sem=send_sem.at[peer],
-            recv_sem=recv_sem.at[peer],
-            device_id={axis: peer},
+            src_ref=source(j),
+            dst_ref=o_ref.at[j],
+            send_sem=send_sem.at[j],
+            recv_sem=recv_sem.at[j],
+            device_id=device(j),
             device_id_type=MESH,
         )
 
     barrier = pltpu.get_barrier_semaphore()
 
     def greet(i, carry):
-        pl.semaphore_signal(barrier, 1, device_id={axis: peer_of(i)}, device_id_type=MESH)
+        pl.semaphore_signal(barrier, 1, device_id=device(member(i)), device_id_type=MESH)
         return carry
 
-    lax.fori_loop(0, n - 1, greet, 0)
-    pl.semaphore_wait(barrier, n - 1)
+    lax.fori_loop(0, m - 1, greet, 0)
+    pl.semaphore_wait(barrier, m - 1)
 
     def send(i, carry):
-        outgoing(peer_of(i)).start()
+        outgoing(member(i)).start()
         return carry
 
-    lax.fori_loop(0, n - 1, send, 0)
-    own = pltpu.make_async_copy(source(me), o_ref.at[me], own_sem)
+    lax.fori_loop(0, m - 1, send, 0)
+    own = pltpu.make_async_copy(source(k), o_ref.at[k], own_sem)
     own.start()
 
     def finish(i, carry):
-        peer = peer_of(i)
-        outgoing(peer).wait_send()
-        incoming(peer).wait_recv()
+        j = member(i)
+        outgoing(j).wait_send()
+        incoming(j).wait_recv()
         return carry
 
-    lax.fori_loop(0, n - 1, finish, 0)
+    lax.fori_loop(0, m - 1, finish, 0)
     own.wait()
 
 
-def exchange(x, axis, n, gather, cid):
+def exchange(x, axis, m, stride, gather, cid):
     block = x.shape if gather else x.shape[1:]
     return pl.pallas_call(
-        functools.partial(_exchange_kernel, axis, n, gather),
-        out_shape=jax.ShapeDtypeStruct((n,) + tuple(block), x.dtype),
+        functools.partial(_exchange_kernel, axis, m, stride, gather),
+        out_shape=jax.ShapeDtypeStruct((m,) + tuple(block), x.dtype),
         in_specs=[pl.BlockSpec(memory_space=pl.ANY)],
         out_specs=pl.BlockSpec(memory_space=pl.ANY),
         scratch_shapes=[
-            pltpu.SemaphoreType.DMA((n,)),
-            pltpu.SemaphoreType.DMA((n,)),
+            pltpu.SemaphoreType.DMA((m,)),
+            pltpu.SemaphoreType.DMA((m,)),
             pltpu.SemaphoreType.DMA,
         ],
         compiler_params=pltpu.CompilerParams(collective_id=cid, has_side_effects=True),
@@ -130,22 +135,26 @@
     hidden_dev = w_gate.shape[2]
     n_ed = lax.axis_size("ed")
     n_fsdp = lax.axis_size("fsdp")
+    chips = n_ed // 2
     per_band = n_ed // n_fsdp
     own_slots = pick_rows(tokens[None], expert_ids[None], window, CAP)[0, 0]
-    selected = exchange(own_slots, "ed", n_ed, True, 0)
+    same_core = exchange(own_slots, "ed", chips, 2, True, 0)
+    selected = exchange(same_core, "ed", 2, 1, True, 1)
     selected = selected.reshape(n_fsdp, per_band, CAP, features_dev)
     both = jnp.concatenate([w_gate[0], w_up[0]], axis=1)
     partial = jnp.einsum("fbri,ih->fbrh", selected, both, preferred_element_type=jnp.float32)
-    arrived = exchange(partial.astype(jnp.bfloat16), "fsdp", n_fsdp, False, 1)
+    arrived = exchange(partial.astype(jnp.bfloat16), "fsdp", n_fsdp, 1, False, 2)
     summed = jnp.sum(arrived.astype(jnp.float32), axis=0)
     gate_part = summed[..., :hidden_dev]
     up_part = summed[..., hidden_dev:]
     activation = (jax.nn.silu(gate_part) * up_part).astype(jnp.bfloat16)
-    act_rows = exchange(activation, "fsdp", n_fsdp, True, 2)
-    act_rows = act_rows.reshape(n_ed, CAP, hidden_dev)
-    term = jnp.einsum("brh,hd->brd", act_rows, w_down[0], preferred_element_type=jnp.float32)
+    act_rows = exchange(activation, "fsdp", n_fsdp, 1, True, 3)
+    act_rows = act_rows.reshape(2, chips, CAP, hidden_dev)
+    term = jnp.einsum("cbrh,hd->cbrd", act_rows, w_down[0], preferred_element_type=jnp.float32)
     term = term.astype(jnp.bfloat16)
-    pieces = exchange(term, "ed", n_ed, False, 3)
+    pair = exchange(term, "ed", 2, 1, False, 4)
+    pair = (pair[0].astype(jnp.float32) + pair[1].astype(jnp.float32)).astype(jnp.bfloat16)
+    pieces = exchange(pair, "ed", chips, 2, False, 5)
     slot_out = jnp.sum(pieces.astype(jnp.float32), axis=0)
     weights_matrix = combine_matrix(expert_ids, route_weights, window, CAP)
     mixed = jnp.dot(

time: 261 us -> 281 us (1.077)
  Pallas kernels: 239 us -> 257 us
    pallas_call x4 -> x6, Pallas kernels: 239 us -> 257 us  [exchange(): pl.pallas_call(functools.partial(_exchange_kernel, axis, m, stride, gathe...]
    convert_element_type x0 -> x1, other arithmetic: none -> 2.83 us  [local(): (pair[0].astype(jnp.float32) + pair[1].astype(jnp.float32)).astype(jnp.bf...]
where the time goes in v4:
time: 281 us
  Pallas kernels  257 us (91%)
  other arithmetic  12.3 us (4%)
  matrix products  9.8 us (3%)
    pallas_call x6, Pallas kernels, exchange(): pl.pallas_call(functools.partial(_exchange_kernel, axis, m, stride, gathe...  257 us

profile of v4, /device:TPU:1, one launch (start us, length us, event | category | flops | bytes accessed | tf_op | source)
XLA Modules:
  0.0 280.6 jit_solution(14640042806122043950)
XLA Ops:
  0.0 0.0 copy-start
  0.0 0.7 fusion.17
  0.8 0.3 reduce-window.6
  1.1 0.2 slice_reduce_fusion
  1.3 0.2 reduce-window.9
  1.5 0.1 broadcast.182
  1.6 3.0 %convert_reduce_fusion.2 = (s32[81]{0:T(128)S(1)}, s32[81]{0:T(128)S(1)}) fusion(pred[288]{0:T(512)(128)(4,1)S(1)} %fusion.17, s32[288]{0:T(512)S(1)} %fusion.16), kind=kLoop, calls=%fused_computation.22 | loop fusion | flops 139806 | bytes 2088 | tf_op jit(solution)/shard_map/reduce_sum | solution.py:33
  4.6 0.0 copy-done
  4.6 1.3 gather_fusion
  5.9 0.7 select_select_fusion.x_ref
  6.6 37.3 %shard_map.64.x_ref = bf16[16,81,384]{2,1,0:T(8,128)(2,1)} custom-call(bf16[81,384]{1,0:T(8,128)(2,1)} %select_select_fusion.x_ref), custom_call_target="tpu_custom_call" | custom-call | tf_op jit(solution)/shard_map/pallas_call | solution.py:118
  44.0 37.1 %shard_map.65 = bf16[2,16,81,384]{3,2,1,0:T(8,128)(2,1)} custom-call(bf16[16,81,384]{2,1,0:T(8,128)(2,1)} %shard_map.64.x_ref), custom_call_target="tpu_custom_call" | custom-call | tf_op jit(solution)/shard_map/pallas_call | solution.py:118
  81.1 4.9 %convolution_convert_fusion.x_ref = bf16[16,2,81,512]{3,2,1,0:T(8,128)(2,1)} fusion(bf16[16,2,81,384]{3,2,1,0:T(8,128)(2,1)} %bitcast.39, bf16[384,256]{1,0:T(8,128)(2,1)S(1)} %bitcast.42, bf16[384,256]{1,0:T(8,128)(2,1)S(1)} %bitcast.43), kind=kOutput, calls=%fused_computation.2 | convolution fusion | flops 1021329408 | bytes 5038080 | tf_op jit(solution)/shard_map/fbri,ih->fbrh/dot_general | solution.py:145
  86.0 69.2 %shard_map.66 = bf16[16,2,81,512]{3,2,1,0:T(8,128)(2,1)} custom-call(bf16[16,2,81,512]{3,2,1,0:T(8,128)(2,1)} %convolution_convert_fusion.x_ref), custom_call_target="tpu_custom_call" | custom-call | tf_op jit(solution)/shard_map/pallas_call | solution.py:118
  155.1 0.0 copy-start.1
  155.2 2.3 convert_reduce_fusion
  157.5 0.7 fusion.5.x_ref
  158.2 43.9 %shard_map.67 = bf16[16,2,81,256]{3,2,1,0:T(8,128)(2,1)} custom-call(bf16[2,81,256]{2,1,0:T(8,128)(2,1)} %fusion.5.x_ref), custom_call_target="tpu_custom_call" | custom-call | tf_op jit(solution)/shard_map/pallas_call | solution.py:118
  202.1 3.6 %convolution_convert_fusion.1.x_ref = bf16[2,16,81,384]{3,2,1,0:T(8,128)(2,1)} fusion(bf16[1,256,384]{2,1,0:T(8,128)(2,1)S(1)} %copy-done.1, bf16[2,16,81,256]{3,2,1,0:T(8,128)(2,1)} %bitcast.38), kind=kOutput, calls=%fused_computation.5 | convolution fusion | flops 510603264 | bytes 3514368 | tf_op jit(solution)/shard_map/cbrh,hd->cbrd/dot_general | solution.py:153
  205.7 35.3 %shard_map.68 = bf16[2,16,81,384]{3,2,1,0:T(8,128)(2,1)} custom-call(bf16[2,16,81,384]{3,2,1,0:T(8,128)(2,1)} %convolution_convert_fusion.1.x_ref), custom_call_target="tpu_custom_call" | custom-call | tf_op jit(solution)/shard_map/pallas_call | solution.py:118
  241.0 2.8 %fusion.1.x_ref = bf16[16,81,384]{2,1,0:T(8,128)(2,1)} fusion(bf16[2,16,81,384]{3,2,1,0:T(8,128)(2,1)} %shard_map.68), kind=kLoop, calls=%fused_computation.8 | loop fusion | flops 1990656 | bytes 2985984 | tf_op jit(solution)/shard_map/convert_element_type | solution.py:156
  243.8 34.0 %shard_map.69 = bf16[16,81,384]{2,1,0:T(8,128)(2,1)} custom-call(bf16[16,81,384]{2,1,0:T(8,128)(2,1)} %fusion.1.x_ref), custom_call_target="tpu_custom_call" | custom-call | tf_op jit(solution)/shard_map/pallas_call | solution.py:118
  277.9 1.4 convert_reduce_fusion.1
  279.3 1.3 convolution_convert_fusion.2
  (20 shorter events, 0.2 us)
Async XLA Ops:
  0.0 4.6 %copy-start = (bf16[288,384]{1,0:T(8,128)(2,1)S(1)}, bf16[288,384]{1,0:T(8,128)(2,1)}, u32[]{:S(2)}) copy-start(bf16[288,384]{1,0:T(8,128)(2,1)} %param.6) | copy-start | bytes 663556
  6.6 74.4 %copy-start.4 = (bf16[1,384,256]{2,1,0:T(8,128)(2,1)S(1)}, bf16[1,384,256]{2,1,0:T(8,128)(2,1)}, u32[]{:S(2)}) copy-start(bf16[1,384,256]{2,1,0:T(8,128)(2,1)} %param.10) | copy-start | bytes 589828
  6.6 74.4 %copy-start.5 = (bf16[1,384,256]{2,1,0:T(8,128)(2,1)S(1)}, bf16[1,384,256]{2,1,0:T(8,128)(2,1)}, u32[]{:S(2)}) copy-start(bf16[1,384,256]{2,1,0:T(8,128)(2,1)} %param.9) | copy-start | bytes 589828
  155.1 46.9 %copy-start.1 = (bf16[1,256,384]{2,1,0:T(8,128)(2,1)S(1)}, bf16[1,256,384]{2,1,0:T(8,128)(2,1)}, u32[]{:S(2)}) copy-start(bf16[1,256,384]{2,1,0:T(8,128)(2,1)} %param.11) | copy-start | bytes 589828
  243.8 35.4 %copy-start.2 = (s32[288,2]{0,1:T(2,128)S(1)}, s32[288,2]{0,1:T(2,128)}, u32[]{:S(2)}) copy-start(s32[288,2]{0,1:T(2,128)} %param.7) | copy-start | bytes 6916
  243.8 35.5 %copy-start.3 = (f32[288,2]{0,1:T(2,128)S(1)}, f32[288,2]{0,1:T(2,128)}, u32[]{:S(2)}) copy-start(f32[288,2]{0,1:T(2,128)} %param.8) | copy-start | bytes 6916

commit v5 on v4

--- a/solution.py
+++ b/solution.py
@@ -118,8 +118,8 @@
     return pl.pallas_call(
         functools.partial(_exchange_kernel, axis, m, stride, gather),
         out_shape=jax.ShapeDtypeStruct((m,) + tuple(block), x.dtype),
-        in_specs=[pl.BlockSpec(memory_space=pl.ANY)],
-        out_specs=pl.BlockSpec(memory_space=pl.ANY),
+        in_specs=[pl.BlockSpec(memory_space=pltpu.VMEM)],
+        out_specs=pl.BlockSpec(memory_space=pltpu.VMEM),
         scratch_shapes=[
             pltpu.SemaphoreType.DMA((m,)),
             pltpu.SemaphoreType.DMA((m,)),

time: 281 us -> 229 us (0.81)
  Pallas kernels: 257 us -> 203 us
    pallas_call x6, Pallas kernels: 257 us -> 203 us  [exchange(): pl.pallas_call(functools.partial(_exchange_kernel, axis, m, stride, gathe...]
where the time goes in v5:
time: 229 us; the launch traced here: 227 us
  Pallas kernels  203 us (89%)
  other arithmetic  12.3 us (5%)
  matrix products  9.8 us (4%)
    pallas_call x6, Pallas kernels, exchange(): pl.pallas_call(functools.partial(_exchange_kernel, axis, m, stride, gathe...  203 us
    dot_general x1, matrix products, local(): jnp.einsum('fbri,ih->fbrh', selected, both, preferred_element_type=jnp.fl...  4.87 us

profile of v5, /device:TPU:1, one launch (start us, length us, event | category | flops | bytes accessed | tf_op | source)
XLA Modules:
  0.0 227.1 jit_solution(9683527452326252231)
XLA Ops:
  0.0 0.0 copy-start
  0.0 0.7 fusion.17
  0.8 0.3 reduce-window.6
  1.1 0.2 slice_reduce_fusion
  1.3 0.2 reduce-window.9
  1.5 0.1 broadcast.182
  1.6 3.0 %convert_reduce_fusion.2 = (s32[81]{0:T(128)S(1)}, s32[81]{0:T(128)S(1)}) fusion(pred[288]{0:T(512)(128)(4,1)S(1)} %fusion.17, s32[288]{0:T(512)S(1)} %fusion.16), kind=kLoop, calls=%fused_computation.22 | loop fusion | flops 139806 | bytes 2088 | tf_op jit(solution)/shard_map/reduce_sum | solution.py:33
  4.6 0.0 copy-done
  4.6 1.3 gather_fusion
  5.9 0.7 select_select_fusion.x_ref
  6.6 38.9 %shard_map.64.x_ref = bf16[16,81,384]{2,1,0:T(8,128)(2,1)} custom-call(bf16[81,384]{1,0:T(8,128)(2,1)} %select_select_fusion.x_ref), custom_call_target="tpu_custom_call" | custom-call | tf_op jit(solution)/shard_map/pallas_call | solution.py:118
  45.5 8.0 %shard_map.65 = bf16[2,16,81,384]{3,2,1,0:T(8,128)(2,1)} custom-call(bf16[16,81,384]{2,1,0:T(8,128)(2,1)} %shard_map.64.x_ref), custom_call_target="tpu_custom_call" | custom-call | tf_op jit(solution)/shard_map/pallas_call | solution.py:118
  53.5 4.9 %convolution_convert_fusion.x_ref = bf16[16,2,81,512]{3,2,1,0:T(8,128)(2,1)} fusion(bf16[16,2,81,384]{3,2,1,0:T(8,128)(2,1)} %bitcast.39, bf16[384,256]{1,0:T(8,128)(2,1)S(1)} %bitcast.42, bf16[384,256]{1,0:T(8,128)(2,1)S(1)} %bitcast.43), kind=kOutput, calls=%fused_computation.2 | convolution fusion | flops 1021329408 | bytes 5038080 | tf_op jit(solution)/shard_map/fbri,ih->fbrh/dot_general | solution.py:145
  58.4 72.2 %shard_map.66 = bf16[16,2,81,512]{3,2,1,0:T(8,128)(2,1)} custom-call(bf16[16,2,81,512]{3,2,1,0:T(8,128)(2,1)} %convolution_convert_fusion.x_ref), custom_call_target="tpu_custom_call" | custom-call | tf_op jit(solution)/shard_map/pallas_call | solution.py:118
  130.6 0.0 copy-start.1
  130.6 2.3 %convert_reduce_fusion = f32[2,81,512]{2,1,0:T(8,128)S(1)} fusion(bf16[16,2,81,512]{3,2,1,0:T(8,128)(2,1)} %shard_map.66), kind=kLoop, calls=%fused_computation.1 | loop fusion | flops 2571264 | bytes 2985984 | tf_op jit(solution)/shard_map/reduce_sum | solution.py:147
  132.9 0.7 fusion.5.x_ref
  133.6 42.5 %shard_map.67 = bf16[16,2,81,256]{3,2,1,0:T(8,128)(2,1)} custom-call(bf16[2,81,256]{2,1,0:T(8,128)(2,1)} %fusion.5.x_ref), custom_call_target="tpu_custom_call" | custom-call | tf_op jit(solution)/shard_map/pallas_call | solution.py:118
  176.1 3.6 %convolution_convert_fusion.1.x_ref = bf16[2,16,81,384]{3,2,1,0:T(8,128)(2,1)} fusion(bf16[1,256,384]{2,1,0:T(8,128)(2,1)S(1)} %copy-done.1, bf16[2,16,81,256]{3,2,1,0:T(8,128)(2,1)} %bitcast.38), kind=kOutput, calls=%fused_computation.5 | convolution fusion | flops 510603264 | bytes 3514368 | tf_op jit(solution)/shard_map/cbrh,hd->cbrd/dot_general | solution.py:153
  179.7 6.7 %shard_map.68 = bf16[2,16,81,384]{3,2,1,0:T(8,128)(2,1)} custom-call(bf16[2,16,81,384]{3,2,1,0:T(8,128)(2,1)} %convolution_convert_fusion.1.x_ref), custom_call_target="tpu_custom_call" | custom-call | tf_op jit(solution)/shard_map/pallas_call | solution.py:118
  186.4 2.8 %fusion.1.x_ref = bf16[16,81,384]{2,1,0:T(8,128)(2,1)} fusion(bf16[2,16,81,384]{3,2,1,0:T(8,128)(2,1)} %shard_map.68), kind=kLoop, calls=%fused_computation.8 | loop fusion | flops 1990656 | bytes 2985984 | tf_op jit(solution)/shard_map/convert_element_type | solution.py:156
  189.3 35.1 %shard_map.69 = bf16[16,81,384]{2,1,0:T(8,128)(2,1)} custom-call(bf16[16,81,384]{2,1,0:T(8,128)(2,1)} %fusion.1.x_ref), custom_call_target="tpu_custom_call" | custom-call | tf_op jit(solution)/shard_map/pallas_call | solution.py:118
  224.4 1.4 convert_reduce_fusion.1
  225.8 1.3 convolution_convert_fusion.2
  (20 shorter events, 0.2 us)
Async XLA Ops:
  0.0 4.6 %copy-start = (bf16[288,384]{1,0:T(8,128)(2,1)S(1)}, bf16[288,384]{1,0:T(8,128)(2,1)}, u32[]{:S(2)}) copy-start(bf16[288,384]{1,0:T(8,128)(2,1)} %param.6) | copy-start | bytes 663556
  6.6 46.9 %copy-start.4 = (bf16[1,384,256]{2,1,0:T(8,128)(2,1)S(1)}, bf16[1,384,256]{2,1,0:T(8,128)(2,1)}, u32[]{:S(2)}) copy-start(bf16[1,384,256]{2,1,0:T(8,128)(2,1)} %param.10) | copy-start | bytes 589828
  6.6 46.9 %copy-start.5 = (bf16[1,384,256]{2,1,0:T(8,128)(2,1)S(1)}, bf16[1,384,256]{2,1,0:T(8,128)(2,1)}, u32[]{:S(2)}) copy-start(bf16[1,384,256]{2,1,0:T(8,128)(2,1)} %param.9) | copy-start | bytes 589828
  130.6 45.5 %copy-start.1 = (bf16[1,256,384]{2,1,0:T(8,128)(2,1)S(1)}, bf16[1,256,384]{2,1,0:T(8,128)(2,1)}, u32[]{:S(2)}) copy-start(bf16[1,256,384]{2,1,0:T(8,128)(2,1)} %param.11) | copy-start | bytes 589828
  189.3 36.5 %copy-start.2 = (s32[288,2]{0,1:T(2,128)S(1)}, s32[288,2]{0,1:T(2,128)}, u32[]{:S(2)}) copy-start(s32[288,2]{0,1:T(2,128)} %param.7) | copy-start | bytes 6916
  189.3 36.5 %copy-start.3 = (f32[288,2]{0,1:T(2,128)S(1)}, f32[288,2]{0,1:T(2,128)}, u32[]{:S(2)}) copy-start(f32[288,2]{0,1:T(2,128)} %param.8) | copy-start | bytes 6916

commit v6 on v5

--- a/solution.py
+++ b/solution.py
@@ -140,21 +140,26 @@
     own_slots = pick_rows(tokens[None], expert_ids[None], window, CAP)[0, 0]
     same_core = exchange(own_slots, "ed", chips, 2, True, 0)
     selected = exchange(same_core, "ed", 2, 1, True, 1)
-    selected = selected.reshape(n_fsdp, per_band, CAP, features_dev)
+    pairs = 2
+    rings = n_fsdp // pairs
+    selected = selected.reshape(pairs, rings, per_band, CAP, features_dev)
     both = jnp.concatenate([w_gate[0], w_up[0]], axis=1)
-    partial = jnp.einsum("fbri,ih->fbrh", selected, both, preferred_element_type=jnp.float32)
-    arrived = exchange(partial.astype(jnp.bfloat16), "fsdp", n_fsdp, 1, False, 2)
+    partial = jnp.einsum("xybri,ih->xybrh", selected, both, preferred_element_type=jnp.float32)
+    half = exchange(partial.astype(jnp.bfloat16), "fsdp", pairs, 1, False, 2)
+    half = (half[0].astype(jnp.float32) + half[1].astype(jnp.float32)).astype(jnp.bfloat16)
+    arrived = exchange(half, "fsdp", rings, pairs, False, 3)
     summed = jnp.sum(arrived.astype(jnp.float32), axis=0)
     gate_part = summed[..., :hidden_dev]
     up_part = summed[..., hidden_dev:]
     activation = (jax.nn.silu(gate_part) * up_part).astype(jnp.bfloat16)
-    act_rows = exchange(activation, "fsdp", n_fsdp, 1, True, 3)
+    act_ring = exchange(activation, "fsdp", rings, pairs, True, 4)
+    act_rows = exchange(act_ring, "fsdp", pairs, 1, True, 5)
     act_rows = act_rows.reshape(2, chips, CAP, hidden_dev)
     term = jnp.einsum("cbrh,hd->cbrd", act_rows, w_down[0], preferred_element_type=jnp.float32)
     term = term.astype(jnp.bfloat16)
-    pair = exchange(term, "ed", 2, 1, False, 4)
+    pair = exchange(term, "ed", 2, 1, False, 6)
     pair = (pair[0].astype(jnp.float32) + pair[1].astype(jnp.float32)).astype(jnp.bfloat16)
-    pieces = exchange(pair, "ed", chips, 2, False, 5)
+    pieces = exchange(pair, "ed", chips, 2, False, 7)
     slot_out = jnp.sum(pieces.astype(jnp.float32), axis=0)
     weights_matrix = combine_matrix(expert_ids, route_weights, window, CAP)
     mixed = jnp.dot(

time: 229 us -> 237 us (1.035)
  Pallas kernels: 203 us -> 209 us
  other arithmetic: 12.3 us -> 14.9 us
    pallas_call x6 -> x8, Pallas kernels: 203 us -> 209 us  [exchange(): pl.pallas_call(functools.partial(_exchange_kernel, axis, m, stride, gathe...]
    convert_element_type x0 -> x1, other arithmetic: none -> 3.32 us  [local(): (half[0].astype(jnp.float32) + half[1].astype(jnp.float32)).astype(jnp.bf...]
where the time goes in v6:
time: 237 us; the launch traced here: 235 us
  Pallas kernels  209 us (88%)
  other arithmetic  14.9 us (6%)
  matrix products  9.8 us (4%)
    pallas_call x8, Pallas kernels, exchange(): pl.pallas_call(functools.partial(_exchange_kernel, axis, m, stride, gathe...  209 us
    dot_general x1, matrix products, local(): jnp.einsum('xybri,ih->xybrh', selected, both, preferred_element_type=jnp....  4.87 us

profile of v6, /device:TPU:1, one launch (start us, length us, event | category | flops | bytes accessed | tf_op | source)
XLA Modules:
  0.0 235.2 jit_solution(8619023500393950027)
XLA Ops:
  0.0 0.7 fusion.17
  0.8 0.3 reduce-window.6
  1.1 0.2 slice_reduce_fusion
  1.3 0.2 reduce-window.9
  1.5 0.1 broadcast.182
  1.6 3.0 %convert_reduce_fusion.2 = (s32[81]{0:T(128)S(1)}, s32[81]{0:T(128)S(1)}) fusion(pred[288]{0:T(512)(128)(4,1)S(1)} %fusion.17, s32[288]{0:T(512)S(1)} %fusion.16), kind=kLoop, calls=%fused_computation.23 | loop fusion | flops 139806 | bytes 2088 | tf_op jit(solution)/shard_map/reduce_sum | solution.py:33
  4.6 1.3 gather_fusion
  5.9 0.7 select_select_fusion.x_ref
  6.6 38.9 %shard_map.64.x_ref = bf16[16,81,384]{2,1,0:T(8,128)(2,1)} custom-call(bf16[81,384]{1,0:T(8,128)(2,1)} %select_select_fusion.x_ref), custom_call_target="tpu_custom_call" | custom-call | tf_op jit(solution)/shard_map/pallas_call | solution.py:118
  45.5 8.0 %shard_map.65 = bf16[2,16,81,384]{3,2,1,0:T(8,128)(2,1)} custom-call(bf16[16,81,384]{2,1,0:T(8,128)(2,1)} %shard_map.64.x_ref), custom_call_target="tpu_custom_call" | custom-call | tf_op jit(solution)/shard_map/pallas_call | solution.py:118
  53.5 4.9 %convolution_convert_fusion.x_ref = bf16[2,8,2,81,512]{4,3,2,1,0:T(8,128)(2,1)} fusion(bf16[2,8,2,81,384]{4,3,2,1,0:T(8,128)(2,1)} %bitcast.38, bf16[384,256]{1,0:T(8,128)(2,1)S(1)} %bitcast.41, bf16[384,256]{1,0:T(8,128)(2,1)S(1)} %bitcast.42), kind=kOutput, calls=%fused_computation.3 | convolution fusion | flops 1021329408 | bytes 5038080 | tf_op jit(solution)/shard_map/xybri,ih->xybrh/dot_general | solution.py:147
  58.4 37.0 %shard_map.66 = bf16[2,8,2,81,512]{4,3,2,1,0:T(8,128)(2,1)} custom-call(bf16[2,8,2,81,512]{4,3,2,1,0:T(8,128)(2,1)} %convolution_convert_fusion.x_ref), custom_call_target="tpu_custom_call" | custom-call | tf_op jit(solution)/shard_map/pallas_call | solution.py:118
  95.4 3.3 %fusion.x_ref = bf16[8,2,81,512]{3,2,1,0:T(8,128)(2,1)} fusion(bf16[2,8,2,81,512]{4,3,2,1,0:T(8,128)(2,1)} %shard_map.66), kind=kLoop, calls=%fused_computation.7 | loop fusion | flops 2654208 | bytes 3981312 | tf_op jit(solution)/shard_map/convert_element_type | solution.py:149
  98.7 40.1 %shard_map.67 = bf16[8,2,81,512]{3,2,1,0:T(8,128)(2,1)} custom-call(bf16[8,2,81,512]{3,2,1,0:T(8,128)(2,1)} %fusion.x_ref), custom_call_target="tpu_custom_call" | custom-call | tf_op jit(solution)/shard_map/pallas_call | solution.py:118
  138.8 1.6 convert_reduce_fusion
  140.4 0.7 fusion.5.x_ref
  141.1 22.5 %shard_map.68.x_ref = bf16[8,2,81,256]{3,2,1,0:T(8,128)(2,1)} custom-call(bf16[2,81,256]{2,1,0:T(8,128)(2,1)} %fusion.5.x_ref), custom_call_target="tpu_custom_call" | custom-call | tf_op jit(solution)/shard_map/pallas_call | solution.py:118
  163.6 18.8 %shard_map.69 = bf16[2,8,2,81,256]{4,3,2,1,0:T(8,128)(2,1)} custom-call(bf16[8,2,81,256]{3,2,1,0:T(8,128)(2,1)} %shard_map.68.x_ref), custom_call_target="tpu_custom_call" | custom-call | tf_op jit(solution)/shard_map/pallas_call | solution.py:118
  182.5 3.6 %convolution_convert_fusion.1.x_ref = bf16[2,16,81,384]{3,2,1,0:T(8,128)(2,1)} fusion(bf16[2,16,81,256]{3,2,1,0:T(8,128)(2,1)} %bitcast.37, bf16[1,256,384]{2,1,0:T(8,128)(2,1)S(1)} %copy-done.1), kind=kOutput, calls=%fused_computation.6 | convolution fusion | flops 510603264 | bytes 3514368 | tf_op jit(solution)/shard_map/cbrh,hd->cbrd/dot_general | solution.py:158
  186.1 8.7 %shard_map.70 = bf16[2,16,81,384]{3,2,1,0:T(8,128)(2,1)} custom-call(bf16[2,16,81,384]{3,2,1,0:T(8,128)(2,1)} %convolution_convert_fusion.1.x_ref), custom_call_target="tpu_custom_call" | custom-call | tf_op jit(solution)/shard_map/pallas_call | solution.py:118
  194.8 2.8 %fusion.1.x_ref = bf16[16,81,384]{2,1,0:T(8,128)(2,1)} fusion(bf16[2,16,81,384]{3,2,1,0:T(8,128)(2,1)} %shard_map.70), kind=kLoop, calls=%fused_computation.9 | loop fusion | flops 1990656 | bytes 2985984 | tf_op jit(solution)/shard_map/convert_element_type | solution.py:161
  197.6 34.8 %shard_map.71 = bf16[16,81,384]{2,1,0:T(8,128)(2,1)} custom-call(bf16[16,81,384]{2,1,0:T(8,128)(2,1)} %fusion.1.x_ref), custom_call_target="tpu_custom_call" | custom-call | tf_op jit(solution)/shard_map/pallas_call | solution.py:118
  232.5 1.4 convert_reduce_fusion.1
  233.9 1.3 convolution_convert_fusion.2
  (23 shorter events, 0.2 us)
Async XLA Ops:
  0.0 4.6 %copy-start = (bf16[288,384]{1,0:T(8,128)(2,1)S(1)}, bf16[288,384]{1,0:T(8,128)(2,1)}, u32[]{:S(2)}) copy-start(bf16[288,384]{1,0:T(8,128)(2,1)} %param.6) | copy-start | bytes 663556
  6.6 46.9 %copy-start.4 = (bf16[1,384,256]{2,1,0:T(8,128)(2,1)S(1)}, bf16[1,384,256]{2,1,0:T(8,128)(2,1)}, u32[]{:S(2)}) copy-start(bf16[1,384,256]{2,1,0:T(8,128)(2,1)} %param.10) | copy-start | bytes 589828
  6.6 46.9 %copy-start.5 = (bf16[1,384,256]{2,1,0:T(8,128)(2,1)S(1)}, bf16[1,384,256]{2,1,0:T(8,128)(2,1)}, u32[]{:S(2)}) copy-start(bf16[1,384,256]{2,1,0:T(8,128)(2,1)} %param.9) | copy-start | bytes 589828
  140.4 42.1 %copy-start.1 = (bf16[1,256,384]{2,1,0:T(8,128)(2,1)S(1)}, bf16[1,256,384]{2,1,0:T(8,128)(2,1)}, u32[]{:S(2)}) copy-start(bf16[1,256,384]{2,1,0:T(8,128)(2,1)} %param.11) | copy-start | bytes 589828
  197.6 36.2 %copy-start.2 = (s32[288,2]{0,1:T(2,128)S(1)}, s32[288,2]{0,1:T(2,128)}, u32[]{:S(2)}) copy-start(s32[288,2]{0,1:T(2,128)} %param.7) | copy-start | bytes 6916
  197.6 36.2 %copy-start.3 = (f32[288,2]{0,1:T(2,128)S(1)}, f32[288,2]{0,1:T(2,128)}, u32[]{:S(2)}) copy-start(f32[288,2]{0,1:T(2,128)} %param.8) | copy-start | bytes 6916

commit v7 on v5

--- a/solution.py
+++ b/solution.py
@@ -143,10 +143,10 @@
     selected = selected.reshape(n_fsdp, per_band, CAP, features_dev)
     both = jnp.concatenate([w_gate[0], w_up[0]], axis=1)
     partial = jnp.einsum("fbri,ih->fbrh", selected, both, preferred_element_type=jnp.float32)
-    arrived = exchange(partial.astype(jnp.bfloat16), "fsdp", n_fsdp, 1, False, 2)
-    summed = jnp.sum(arrived.astype(jnp.float32), axis=0)
-    gate_part = summed[..., :hidden_dev]
-    up_part = summed[..., hidden_dev:]
+    arrived = exchange(partial[..., :hidden_dev].astype(jnp.bfloat16), "fsdp", n_fsdp, 1, False, 2)
+    gate_part = jnp.sum(arrived.astype(jnp.float32), axis=0)
+    up_sum = lax.psum_scatter(partial[..., hidden_dev:].astype(jnp.bfloat16), "fsdp", scatter_dimension=0, tiled=True)
+    up_part = up_sum[0].astype(jnp.float32)
     activation = (jax.nn.silu(gate_part) * up_part).astype(jnp.bfloat16)
     act_rows = exchange(activation, "fsdp", n_fsdp, 1, True, 3)
     act_rows = act_rows.reshape(2, chips, CAP, hidden_dev)

time: 229 us -> 240 us (1.048)
  Pallas kernels: 203 us -> 174 us
  waiting for transfers between devices: 0 us -> 26.2 us
  between operations: 0.15 us -> 13.5 us
    pallas_call x6, Pallas kernels: 203 us -> 174 us  [exchange(): pl.pallas_call(functools.partial(_exchange_kernel, axis, m, stride, gathe...]
    reduce_scatter x0 -> x1, waiting for transfers between devices: none -> 26.2 us  [local(): lax.psum_scatter(partial[..., hidden_dev:].astype(jnp.bfloat16), 'fsdp',...]
  transfers between devices with their start and end apart: 0 -> 1, of which waited for: 0 -> 1; matrix products, arithmetic and copies ran while one was open for 0% -> 1% of each run, Pallas kernels for 0% -> 19%
where the time goes in v7:
time: 240 us; the launch traced here: 238 us
  Pallas kernels  174 us (72%)
  waiting for transfers between devices  26.2 us (11%)
  between operations  13.5 us (6%)
  other arithmetic  12.5 us (5%)
  matrix products  8.22 us (3%)
  local copies, waits for them, and re-layouts  3.41 us (1%)
    pallas_call x6, Pallas kernels, exchange(): pl.pallas_call(functools.partial(_exchange_kernel, axis, m, stride, gathe...  174 us
    reduce_scatter x1, waiting for transfers between devices, local(): lax.psum_scatter(partial[..., hidden_dev:].astype(jnp.bfloat16), 'fsdp',...  26.2 us
  transfers between devices with their start and end apart: 1, of which 1 were waited for; matrix products, arithmetic and copies ran while one was open for 1% of the time, Pallas kernels for 19%

profile of v7, /device:TPU:1, one launch (start us, length us, event | category | flops | bytes accessed | tf_op | source)
XLA Modules:
  0.0 238.1 jit_solution(907632370965296293)
XLA Ops:
  6.5 0.7 fusion.17
  7.3 0.3 reduce-window.6
  7.6 0.2 slice_reduce_fusion
  7.8 0.2 reduce-window.9
  8.0 0.1 broadcast.182
  8.1 3.0 %convert_reduce_fusion.2 = (s32[81]{0:T(128)S(1)}, s32[81]{0:T(128)S(1)}) fusion(pred[288]{0:T(512)(128)(4,1)S(1)} %fusion.17, s32[288]{0:T(512)S(1)} %fusion.16), kind=kLoop, calls=%fused_computation.22 | loop fusion | flops 139806 | bytes 2088 | tf_op jit(solution)/shard_map/reduce_sum | solution.py:33
  11.1 1.3 gather_fusion
  12.4 0.7 select_select_fusion.x_ref
  13.2 38.9 %shard_map.64.x_ref = bf16[16,81,384]{2,1,0:T(8,128)(2,1)} custom-call(bf16[81,384]{1,0:T(8,128)(2,1)} %select_select_fusion.x_ref), custom_call_target="tpu_custom_call" | custom-call | tf_op jit(solution)/shard_map/pallas_call | solution.py:118
  52.1 8.0 %shard_map.65 = bf16[2,16,81,384]{3,2,1,0:T(8,128)(2,1)} custom-call(bf16[16,81,384]{2,1,0:T(8,128)(2,1)} %shard_map.64.x_ref), custom_call_target="tpu_custom_call" | custom-call | tf_op jit(solution)/shard_map/pallas_call | solution.py:118
  60.1 3.3 %convolution_convert_fusion = bf16[16,2,81,512]{3,2,1,0:T(8,128)(2,1)S(1)} fusion(bf16[16,2,81,384]{3,2,1,0:T(8,128)(2,1)} %bitcast.42, bf16[384,256]{1,0:T(8,128)(2,1)S(1)} %bitcast.45, bf16[384,256]{1,0:T(8,128)(2,1)S(1)} %bitcast.46), kind=kOutput, calls=%fused_computation.2 | convolution fusion | flops 1021329408 | bytes 5038080 | tf_op jit(solution)/shard_map/fbri,ih->fbrh/dot_general | solution.py:145
  63.4 1.8 fusion.19
  65.1 0.0 reduce-scatter.2.cloned.1.call-update
  65.2 46.4 %shard_map.66 = bf16[16,2,81,256]{3,2,1,0:T(8,128)(2,1)} custom-call(bf16[16,2,81,256]{3,2,1,0:T(8,128)(2,1)} %get-tuple-element.8.x_ref), custom_call_target="tpu_custom_call" | custom-call | tf_op jit(solution)/shard_map/pallas_call | solution.py:118
  111.6 1.6 convert_reduce_fusion
  113.2 26.2 %reduce-scatter.2.cloned.1.call-done = bf16[1,2,81,256]{3,2,1,0:T(8,128)(2,1)} async-done(((bf16[16,2,81,256]{3,2,1,0:T(8,128)(2,1)}), bf16[1,2,81,256]{3,2,1,0:T(8,128)(2,1)}) %reduce-scatter.2.cloned.1.call-update) | async-done | bytes 82960 | tf_op jit(solution)/shard_map/reduce_scatter | solution.py:148
  139.5 1.6 fusion.5.x_ref
  141.1 33.4 %shard_map.67 = bf16[16,2,81,256]{3,2,1,0:T(8,128)(2,1)} custom-call(bf16[2,81,256]{2,1,0:T(8,128)(2,1)} %fusion.5.x_ref), custom_call_target="tpu_custom_call" | custom-call | tf_op jit(solution)/shard_map/pallas_call | solution.py:118
  174.5 3.6 %convolution_convert_fusion.1.x_ref = bf16[2,16,81,384]{3,2,1,0:T(8,128)(2,1)} fusion(bf16[1,256,384]{2,1,0:T(8,128)(2,1)S(1)} %copy-done.1, bf16[2,16,81,256]{3,2,1,0:T(8,128)(2,1)} %bitcast.41), kind=kOutput, calls=%fused_computation.5 | convolution fusion | flops 510603264 | bytes 3514368 | tf_op jit(solution)/shard_map/cbrh,hd->cbrd/dot_general | solution.py:153
  178.1 12.5 %shard_map.68 = bf16[2,16,81,384]{3,2,1,0:T(8,128)(2,1)} custom-call(bf16[2,16,81,384]{3,2,1,0:T(8,128)(2,1)} %convolution_convert_fusion.1.x_ref), custom_call_target="tpu_custom_call" | custom-call | tf_op jit(solution)/shard_map/pallas_call | solution.py:118
  190.6 2.8 %fusion.1.x_ref = bf16[16,81,384]{2,1,0:T(8,128)(2,1)} fusion(bf16[2,16,81,384]{3,2,1,0:T(8,128)(2,1)} %shard_map.68), kind=kLoop, calls=%fused_computation.8 | loop fusion | flops 1990656 | bytes 2985984 | tf_op jit(solution)/shard_map/convert_element_type | solution.py:156
  193.4 35.1 %shard_map.69 = bf16[16,81,384]{2,1,0:T(8,128)(2,1)} custom-call(bf16[16,81,384]{2,1,0:T(8,128)(2,1)} %fusion.1.x_ref), custom_call_target="tpu_custom_call" | custom-call | tf_op jit(solution)/shard_map/pallas_call | solution.py:118
  228.5 1.4 convert_reduce_fusion.1
  229.9 1.3 convolution_convert_fusion.2
  (24 shorter events, 0.2 us)
Async XLA Ops:
  6.5 4.6 %copy-start = (bf16[288,384]{1,0:T(8,128)(2,1)S(1)}, bf16[288,384]{1,0:T(8,128)(2,1)}, u32[]{:S(2)}) copy-start(bf16[288,384]{1,0:T(8,128)(2,1)} %param.6) | copy-start | bytes 663556
  6.5 132.9 %reduce-scatter.2.cloned.1.call-start = ((), (), s32[]{:S(2)}) async-start(), calls=%async_computation.1 | async-start | bytes 1531904 | tf_op jit(solution)/shard_map/reduce_scatter | solution.py:148
  13.2 46.9 %copy-start.4 = (bf16[1,384,256]{2,1,0:T(8,128)(2,1)S(1)}, bf16[1,384,256]{2,1,0:T(8,128)(2,1)}, u32[]{:S(2)}) copy-start(bf16[1,384,256]{2,1,0:T(8,128)(2,1)} %param.10) | copy-start | bytes 589828
  13.2 46.9 %copy-start.5 = (bf16[1,384,256]{2,1,0:T(8,128)(2,1)S(1)}, bf16[1,384,256]{2,1,0:T(8,128)(2,1)}, u32[]{:S(2)}) copy-start(bf16[1,384,256]{2,1,0:T(8,128)(2,1)} %param.9) | copy-start | bytes 589828
  65.1 46.4 %copy-start.2 = (s32[288,2]{0,1:T(2,128)S(1)}, s32[288,2]{0,1:T(2,128)}, u32[]{:S(2)}) copy-start(s32[288,2]{0,1:T(2,128)} %param.7) | copy-start | bytes 6916
  65.1 46.4 %copy-start.3 = (f32[288,2]{0,1:T(2,128)S(1)}, f32[288,2]{0,1:T(2,128)}, u32[]{:S(2)}) copy-start(f32[288,2]{0,1:T(2,128)} %param.8) | copy-start | bytes 6916
  111.6 62.9 %copy-start.1 = (bf16[1,256,384]{2,1,0:T(8,128)(2,1)S(1)}, bf16[1,256,384]{2,1,0:T(8,128)(2,1)}, u32[]{:S(2)}) copy-start(bf16[1,256,384]{2,1,0:T(8,128)(2,1)} %param.11) | copy-start | bytes 589828
Sparse Core Ops, SparseCore 0:
  65.3 74.1 reduce-scatter.1

commit v8 on v7

--- a/solution.py
+++ b/solution.py
@@ -127,6 +127,79 @@
         ],
         compiler_params=pltpu.CompilerParams(collective_id=cid, has_side_effects=True),
     )(x)
+
+
+def _gate_kernel(axis, m, hidden, sel_ref, w_ref, o_ref, out_buf, in_buf, acc, send_sem, recv_sem):
+    me = lax.axis_index(axis)
+    bands = sel_ref.shape[1]
+
+    def member(i):
+        return lax.rem(me + 1 + i, m)
+
+    def copy(j, slot):
+        return pltpu.make_async_remote_copy(
+            src_ref=out_buf.at[j],
+            dst_ref=in_buf.at[slot],
+            send_sem=send_sem.at[j],
+            recv_sem=recv_sem.at[slot],
+            device_id={axis: j},
+            device_id_type=MESH,
+        )
+
+    def partial(j, b):
+        return jnp.dot(sel_ref[j, b], w_ref[...], preferred_element_type=jnp.float32)
+
+    barrier = pltpu.get_barrier_semaphore()
+
+    def greet(i, carry):
+        pl.semaphore_signal(barrier, 1, device_id={axis: member(i)}, device_id_type=MESH)
+        return carry
+
+    lax.fori_loop(0, m - 1, greet, 0)
+    pl.semaphore_wait(barrier, m - 1)
+
+    def send(i, carry):
+        j = member(i)
+        for b in range(bands):
+            out_buf[j, b] = partial(j, b).astype(out_buf.dtype)
+        copy(j, me).start()
+        return carry
+
+    lax.fori_loop(0, m - 1, send, 0)
+    for b in range(bands):
+        acc[b] = partial(me, b)
+
+    def gather(i, carry):
+        j = member(i)
+        copy(j, me).wait_send()
+        copy(j, j).wait_recv()
+        acc[...] += in_buf[j].astype(jnp.float32)
+        return carry
+
+    lax.fori_loop(0, m - 1, gather, 0)
+    total = acc[...]
+    gate = total[..., :hidden]
+    up = total[..., hidden:]
+    o_ref[...] = (jax.nn.silu(gate) * up).astype(o_ref.dtype)
+
+
+def gate_act(sel, w, axis, m, cid):
+    _, bands, rows, _ = sel.shape
+    hidden = w.shape[1] // 2
+    return pl.pallas_call(
+        functools.partial(_gate_kernel, axis, m, hidden),
+        out_shape=jax.ShapeDtypeStruct((bands, rows, hidden), jnp.bfloat16),
+        in_specs=[pl.BlockSpec(memory_space=pltpu.VMEM)] * 2,
+        out_specs=pl.BlockSpec(memory_space=pltpu.VMEM),
+        scratch_shapes=[
+            pltpu.VMEM((m, bands, rows, 2 * hidden), jnp.bfloat16),
+            pltpu.VMEM((m, bands, rows, 2 * hidden), jnp.bfloat16),
+            pltpu.VMEM((bands, rows, 2 * hidden), jnp.float32),
+            pltpu.SemaphoreType.DMA((m,)),
+            pltpu.SemaphoreType.DMA((m,)),
+        ],
+        compiler_params=pltpu.CompilerParams(collective_id=cid, has_side_effects=True),
+    )(sel, w)
 
 
 def local(tokens, expert_ids, route_weights, w_gate, w_up, w_down):
@@ -142,12 +215,7 @@
     selected = exchange(same_core, "ed", 2, 1, True, 1)
     selected = selected.reshape(n_fsdp, per_band, CAP, features_dev)
     both = jnp.concatenate([w_gate[0], w_up[0]], axis=1)
-    partial = jnp.einsum("fbri,ih->fbrh", selected, both, preferred_element_type=jnp.float32)
-    arrived = exchange(partial[..., :hidden_dev].astype(jnp.bfloat16), "fsdp", n_fsdp, 1, False, 2)
-    gate_part = jnp.sum(arrived.astype(jnp.float32), axis=0)
-    up_sum = lax.psum_scatter(partial[..., hidden_dev:].astype(jnp.bfloat16), "fsdp", scatter_dimension=0, tiled=True)
-    up_part = up_sum[0].astype(jnp.float32)
-    activation = (jax.nn.silu(gate_part) * up_part).astype(jnp.bfloat16)
+    activation = gate_act(selected, both, "fsdp", n_fsdp, 2)
     act_rows = exchange(activation, "fsdp", n_fsdp, 1, True, 3)
     act_rows = act_rows.reshape(2, chips, CAP, hidden_dev)
     term = jnp.einsum("cbrh,hd->cbrd", act_rows, w_down[0], preferred_element_type=jnp.float32)

time: 240 us -> 222 us (0.925)
  Pallas kernels: 174 us -> 204 us
  waiting for transfers between devices: 26.2 us -> 0 us
  between operations: 13.5 us -> 0.14 us
  matrix products: 8.22 us -> 4.92 us
  other arithmetic: 12.5 us -> 10 us
    pallas_call x0 -> x1, Pallas kernels: none -> 73.7 us  [gate_act(): pl.pallas_call(functools.partial(_gate_kernel, axis, m, hidden), out_shap...]
    pallas_call x6 -> x5, Pallas kernels: 174 us -> 130 us  [exchange(): pl.pallas_call(functools.partial(_exchange_kernel, axis, m, stride, gathe...]
    reduce_scatter x1 -> x0, waiting for transfers between devices: 26.2 us -> none  [local(): lax.psum_scatter(partial[..., hidden_dev:].astype(jnp.bfloat16), 'fsdp',...]
    dot_general x1 -> x0, matrix products: 3.29 us -> none  [local(): jnp.einsum('fbri,ih->fbrh', selected, both, preferred_element_type=jnp.fl...]
  transfers between devices with their start and end apart: 1 -> 0, of which waited for: 1 -> 0; matrix products, arithmetic and copies ran while one was open for 1% -> 0% of each run, Pallas kernels for 19% -> 0%
where the time goes in v8:
time: 222 us; the launch traced here: 221 us
  Pallas kernels  204 us (92%)
  other arithmetic  10 us (5%)
  matrix products  4.92 us (2%)
    pallas_call x5, Pallas kernels, exchange(): pl.pallas_call(functools.partial(_exchange_kernel, axis, m, stride, gathe...  130 us
    pallas_call x1, Pallas kernels, gate_act(): pl.pallas_call(functools.partial(_gate_kernel, axis, m, hidden), out_shap...  73.7 us

profile of v8, /device:TPU:1, one launch (start us, length us, event | category | flops | bytes accessed | tf_op | source)
XLA Modules:
  0.0 220.5 jit_solution(14990703812522185675)
XLA Ops:
  0.0 0.0 copy-start
  0.0 0.7 fusion.14
  0.8 0.3 reduce-window.6
  1.1 0.2 slice_reduce_fusion
  1.3 0.2 reduce-window.9
  1.5 0.1 broadcast.180
  1.6 3.0 %convert_reduce_fusion.1 = (s32[81]{0:T(128)S(1)}, s32[81]{0:T(128)S(1)}) fusion(pred[288]{0:T(512)(128)(4,1)S(1)} %fusion.14, s32[288]{0:T(512)S(1)} %fusion.13), kind=kLoop, calls=%fused_computation.16 | loop fusion | flops 139806 | bytes 2088 | tf_op jit(solution)/shard_map/reduce_sum | solution.py:33
  4.6 0.0 copy-done
  4.6 1.3 gather_fusion
  5.9 0.7 select_select_fusion.x_ref
  6.6 38.9 %shard_map.64.x_ref = bf16[16,81,384]{2,1,0:T(8,128)(2,1)} custom-call(bf16[81,384]{1,0:T(8,128)(2,1)} %select_select_fusion.x_ref), custom_call_target="tpu_custom_call" | custom-call | tf_op jit(solution)/shard_map/pallas_call | solution.py:118
  45.5 8.0 %shard_map.65 = bf16[2,16,81,384]{3,2,1,0:T(8,128)(2,1)} custom-call(bf16[16,81,384]{2,1,0:T(8,128)(2,1)} %shard_map.64.x_ref), custom_call_target="tpu_custom_call" | custom-call | tf_op jit(solution)/shard_map/pallas_call | solution.py:118
  53.5 0.0 copy-done.1
  53.5 0.8 pad_maximum_fusion.w_ref
  54.3 73.7 %shard_map.66.x_ref = bf16[2,81,256]{2,1,0:T(8,128)(2,1)} custom-call(bf16[16,2,81,384]{3,2,1,0:T(8,128)(2,1)} %bitcast.32, bf16[384,512]{1,0:T(8,128)(2,1)} %pad_maximum_fusion.w_ref), custom_call_target="tpu_custom_call" | custom-call | tf_op jit(solution)/shard_map/pallas_call | solution.py:189
  128.0 39.9 %shard_map.67 = bf16[16,2,81,256]{3,2,1,0:T(8,128)(2,1)} custom-call(bf16[2,81,256]{2,1,0:T(8,128)(2,1)} %shard_map.66.x_ref), custom_call_target="tpu_custom_call" | custom-call | tf_op jit(solution)/shard_map/pallas_call | solution.py:118
  167.9 3.6 %convolution_convert_fusion.x_ref = bf16[2,16,81,384]{3,2,1,0:T(8,128)(2,1)} fusion(bf16[1,256,384]{2,1,0:T(8,128)(2,1)S(1)} %copy-done.3, bf16[2,16,81,256]{3,2,1,0:T(8,128)(2,1)} %bitcast.33), kind=kOutput, calls=%fused_computation.3 | convolution fusion | flops 510603264 | bytes 3514368 | tf_op jit(solution)/shard_map/cbrh,hd->cbrd/dot_general | solution.py:221
  171.5 8.6 %shard_map.68 = bf16[2,16,81,384]{3,2,1,0:T(8,128)(2,1)} custom-call(bf16[2,16,81,384]{3,2,1,0:T(8,128)(2,1)} %convolution_convert_fusion.x_ref), custom_call_target="tpu_custom_call" | custom-call | tf_op jit(solution)/shard_map/pallas_call | solution.py:118
  180.1 2.8 %fusion.1.x_ref = bf16[16,81,384]{2,1,0:T(8,128)(2,1)} fusion(bf16[2,16,81,384]{3,2,1,0:T(8,128)(2,1)} %shard_map.68), kind=kLoop, calls=%fused_computation.6 | loop fusion | flops 1990656 | bytes 2985984 | tf_op jit(solution)/shard_map/convert_element_type | solution.py:224
  182.9 34.8 %shard_map.69 = bf16[16,81,384]{2,1,0:T(8,128)(2,1)} custom-call(bf16[16,81,384]{2,1,0:T(8,128)(2,1)} %fusion.1.x_ref), custom_call_target="tpu_custom_call" | custom-call | tf_op jit(solution)/shard_map/pallas_call | solution.py:118
  217.8 1.4 convert_reduce_fusion
  219.2 0.0 copy-done.4
  219.2 0.0 copy-done.5
  219.2 1.3 convolution_convert_fusion.1
  (18 shorter events, 0.2 us)
Async XLA Ops:
  0.0 4.6 %copy-start = (bf16[288,384]{1,0:T(8,128)(2,1)S(1)}, bf16[288,384]{1,0:T(8,128)(2,1)}, u32[]{:S(2)}) copy-start(bf16[288,384]{1,0:T(8,128)(2,1)} %param.6) | copy-start | bytes 663556
  6.6 46.9 %copy-start.1 = (bf16[1,384,256]{2,1,0:T(8,128)(2,1)S(1)}, bf16[1,384,256]{2,1,0:T(8,128)(2,1)}, u32[]{:S(2)}) copy-start(bf16[1,384,256]{2,1,0:T(8,128)(2,1)} %param.10) | copy-start | bytes 589828
  6.6 46.9 %copy-start.2 = (bf16[1,384,256]{2,1,0:T(8,128)(2,1)S(1)}, bf16[1,384,256]{2,1,0:T(8,128)(2,1)}, u32[]{:S(2)}) copy-start(bf16[1,384,256]{2,1,0:T(8,128)(2,1)} %param.9) | copy-start | bytes 589828
  54.3 113.6 %copy-start.3 = (bf16[1,256,384]{2,1,0:T(8,128)(2,1)S(1)}, bf16[1,256,384]{2,1,0:T(8,128)(2,1)}, u32[]{:S(2)}) copy-start(bf16[1,256,384]{2,1,0:T(8,128)(2,1)} %param.11) | copy-start | bytes 589828
  182.9 36.3 %copy-start.4 = (s32[288,2]{0,1:T(2,128)S(1)}, s32[288,2]{0,1:T(2,128)}, u32[]{:S(2)}) copy-start(s32[288,2]{0,1:T(2,128)} %param.7) | copy-start | bytes 6916
  182.9 36.3 %copy-start.5 = (f32[288,2]{0,1:T(2,128)S(1)}, f32[288,2]{0,1:T(2,128)}, u32[]{:S(2)}) copy-start(f32[288,2]{0,1:T(2,128)} %param.8) | copy-start | bytes 6916

commit v9 on v8

--- a/solution.py
+++ b/solution.py
@@ -202,6 +202,135 @@
     )(sel, w)
 
 
+def _down_kernel(nf, chips, act_ref, wd_ref, o_ref, act_buf, term_buf, sib_buf, pre_buf, in_buf,
+                 a_send, a_recv, s_send, s_recv, e_send, e_recv):
+    bands = act_ref.shape[0]
+    f = lax.axis_index("fsdp")
+    e = lax.axis_index("ed")
+    core = lax.rem(e, 2)
+    chip = e // 2
+    sib = e + 1 - 2 * core
+
+    def fsdp_peer(i):
+        return lax.rem(f + 1 + i, nf)
+
+    def chip_peer(i):
+        return lax.rem(chip + 1 + i, chips)
+
+    def act_copy(g, slot):
+        return pltpu.make_async_remote_copy(
+            src_ref=act_ref,
+            dst_ref=act_buf.at[slot],
+            send_sem=a_send.at[g],
+            recv_sem=a_recv.at[slot],
+            device_id={"fsdp": g},
+            device_id_type=MESH,
+        )
+
+    def piece_copy(h, slot):
+        return pltpu.make_async_remote_copy(
+            src_ref=pre_buf.at[h],
+            dst_ref=in_buf.at[slot],
+            send_sem=e_send.at[h],
+            recv_sem=e_recv.at[slot],
+            device_id={"ed": h * 2 + core},
+            device_id_type=MESH,
+        )
+
+    barrier = pltpu.get_barrier_semaphore()
+
+    def greet_fsdp(i, carry):
+        pl.semaphore_signal(barrier, 1, device_id={"fsdp": fsdp_peer(i)}, device_id_type=MESH)
+        return carry
+
+    def greet_ed(i, carry):
+        pl.semaphore_signal(barrier, 1, device_id={"ed": chip_peer(i) * 2 + core}, device_id_type=MESH)
+        return carry
+
+    lax.fori_loop(0, nf - 1, greet_fsdp, 0)
+    lax.fori_loop(0, chips - 1, greet_ed, 0)
+    pl.semaphore_signal(barrier, 1, device_id={"ed": sib}, device_id_type=MESH)
+    pl.semaphore_wait(barrier, nf - 1 + chips)
+
+    def send_act(i, carry):
+        act_copy(fsdp_peer(i), f).start()
+        return carry
+
+    lax.fori_loop(0, nf - 1, send_act, 0)
+    for b in range(bands):
+        term_buf[f * bands + b] = jnp.dot(
+            act_ref[b], wd_ref[...], preferred_element_type=jnp.float32
+        ).astype(term_buf.dtype)
+
+    def take_act(i, carry):
+        g = fsdp_peer(i)
+        act_copy(g, f).wait_send()
+        act_copy(g, g).wait_recv()
+        for b in range(bands):
+            term_buf[g * bands + b] = jnp.dot(
+                act_buf[g, b], wd_ref[...], preferred_element_type=jnp.float32
+            ).astype(term_buf.dtype)
+        return carry
+
+    lax.fori_loop(0, nf - 1, take_act, 0)
+
+    pair = pltpu.make_async_remote_copy(
+        src_ref=term_buf.at[pl.ds((1 - core) * chips, chips)],
+        dst_ref=sib_buf,
+        send_sem=s_send,
+        recv_sem=s_recv,
+        device_id={"ed": sib},
+        device_id_type=MESH,
+    )
+    pair.start()
+    pair.wait_send()
+    pair.wait_recv()
+    mine = term_buf[pl.ds(core * chips, chips)].astype(jnp.float32)
+    pre_buf[...] = (mine + sib_buf[...].astype(jnp.float32)).astype(pre_buf.dtype)
+
+    def send_piece(i, carry):
+        piece_copy(chip_peer(i), chip).start()
+        return carry
+
+    lax.fori_loop(0, chips - 1, send_piece, 0)
+    o_ref[...] = pre_buf[chip].astype(jnp.float32)
+
+    def take_piece(i, carry):
+        h = chip_peer(i)
+        piece_copy(h, chip).wait_send()
+        piece_copy(h, h).wait_recv()
+        o_ref[...] += in_buf[h].astype(jnp.float32)
+        return carry
+
+    lax.fori_loop(0, chips - 1, take_piece, 0)
+
+
+def down_terms(act, wd, nf, chips, cid):
+    bands, rows, hidden = act.shape
+    d = wd.shape[1]
+    blocks = nf * bands
+    return pl.pallas_call(
+        functools.partial(_down_kernel, nf, chips),
+        out_shape=jax.ShapeDtypeStruct((rows, d), jnp.float32),
+        in_specs=[pl.BlockSpec(memory_space=pltpu.VMEM)] * 2,
+        out_specs=pl.BlockSpec(memory_space=pltpu.VMEM),
+        scratch_shapes=[
+            pltpu.VMEM((nf, bands, rows, hidden), jnp.bfloat16),
+            pltpu.VMEM((blocks, rows, d), jnp.bfloat16),
+            pltpu.VMEM((chips, rows, d), jnp.bfloat16),
+            pltpu.VMEM((chips, rows, d), jnp.bfloat16),
+            pltpu.VMEM((chips, rows, d), jnp.bfloat16),
+            pltpu.SemaphoreType.DMA((nf,)),
+            pltpu.SemaphoreType.DMA((nf,)),
+            pltpu.SemaphoreType.DMA,
+            pltpu.SemaphoreType.DMA,
+            pltpu.SemaphoreType.DMA((chips,)),
+            pltpu.SemaphoreType.DMA((chips,)),
+        ],
+        compiler_params=pltpu.CompilerParams(collective_id=cid, has_side_effects=True),
+    )(act, wd)
+
+
 def local(tokens, expert_ids, route_weights, w_gate, w_up, w_down):
     window = w_gate.shape[0]
     features_dev = tokens.shape[1]
@@ -216,14 +345,7 @@
     selected = selected.reshape(n_fsdp, per_band, CAP, features_dev)
     both = jnp.concatenate([w_gate[0], w_up[0]], axis=1)
     activation = gate_act(selected, both, "fsdp", n_fsdp, 2)
-    act_rows = exchange(activation, "fsdp", n_fsdp, 1, True, 3)
-    act_rows = act_rows.reshape(2, chips, CAP, hidden_dev)
-    term = jnp.einsum("cbrh,hd->cbrd", act_rows, w_down[0], preferred_element_type=jnp.float32)
-    term = term.astype(jnp.bfloat16)
-    pair = exchange(term, "ed", 2, 1, False, 4)
-    pair = (pair[0].astype(jnp.float32) + pair[1].astype(jnp.float32)).astype(jnp.bfloat16)
-    pieces = exchange(pair, "ed", chips, 2, False, 5)
-    slot_out = jnp.sum(pieces.astype(jnp.float32), axis=0)
+    slot_out = down_terms(activation, w_down[0], n_fsdp, chips, 3)
     weights_matrix = combine_matrix(expert_ids, route_weights, window, CAP)
     mixed = jnp.dot(
         weights_matrix,

time: 222 us -> 207 us (0.932)
  Pallas kernels: 204 us -> 196 us
  other arithmetic: 10 us -> 5.78 us
  matrix products: 4.92 us -> 2.2 us
    pallas_call x5 -> x2, Pallas kernels: 130 us -> 46.8 us  [exchange(): pl.pallas_call(functools.partial(_exchange_kernel, axis, m, stride, gathe...]
    pallas_call x0 -> x1, Pallas kernels: none -> 76.1 us  [down_terms(): pl.pallas_call(functools.partial(_down_kernel, nf, chips), out_shape=jax....]
    dot_general x1 -> x0, matrix products: 3.62 us -> none  [local(): jnp.einsum('cbrh,hd->cbrd', act_rows, w_down[0], preferred_element_type=j...]
    convert_element_type x1 -> x0, other arithmetic: 2.83 us -> none  [local(): (pair[0].astype(jnp.float32) + pair[1].astype(jnp.float32)).astype(jnp.bf...]
where the time goes in v9:
time: 207 us; the launch traced here: 206 us
  Pallas kernels  196 us (95%)
  other arithmetic  5.78 us (3%)
  matrix products  2.2 us (1%)
    pallas_call x1, Pallas kernels, down_terms(): pl.pallas_call(functools.partial(_down_kernel, nf, chips), out_shape=jax....  76.1 us
    pallas_call x1, Pallas kernels, gate_act(): pl.pallas_call(functools.partial(_gate_kernel, axis, m, hidden), out_shap...  73.5 us
    pallas_call x2, Pallas kernels, exchange(): pl.pallas_call(functools.partial(_exchange_kernel, axis, m, stride, gathe...  46.8 us

profile of v9, /device:TPU:1, one launch (start us, length us, event | category | flops | bytes accessed | tf_op | source)
XLA Modules:
  0.0 206.2 jit_solution(15892245945091698308)
XLA Ops:
  0.0 0.0 copy-start
  0.0 0.7 fusion.11
  0.8 0.3 reduce-window.6
  1.1 0.2 slice_reduce_fusion
  1.3 0.2 reduce-window.9
  1.5 0.1 broadcast.180
  1.6 3.0 %convert_reduce_fusion = (s32[81]{0:T(128)S(1)}, s32[81]{0:T(128)S(1)}) fusion(pred[288]{0:T(512)(128)(4,1)S(1)} %fusion.11, s32[288]{0:T(512)S(1)} %fusion.10), kind=kLoop, calls=%fused_computation.10 | loop fusion | flops 139806 | bytes 2088 | tf_op jit(solution)/shard_map/reduce_sum | solution.py:33
  4.6 0.0 copy-done
  4.6 1.3 gather_fusion
  5.9 0.7 select_select_fusion.x_ref
  6.6 0.0 copy-start.1
  6.6 0.0 copy-start.2
  6.6 38.9 %shard_map.64.x_ref = bf16[16,81,384]{2,1,0:T(8,128)(2,1)} custom-call(bf16[81,384]{1,0:T(8,128)(2,1)} %select_select_fusion.x_ref), custom_call_target="tpu_custom_call" | custom-call | tf_op jit(solution)/shard_map/pallas_call | solution.py:118
  45.5 8.0 %shard_map.65 = bf16[2,16,81,384]{3,2,1,0:T(8,128)(2,1)} custom-call(bf16[16,81,384]{2,1,0:T(8,128)(2,1)} %shard_map.64.x_ref), custom_call_target="tpu_custom_call" | custom-call | tf_op jit(solution)/shard_map/pallas_call | solution.py:118
  53.5 0.0 copy-start.3
  53.5 0.0 copy-start.4
  53.5 0.0 copy-done.1
  53.5 0.0 copy-done.2
  53.5 0.8 pad_maximum_fusion.w_ref
  54.3 73.5 %shard_map.66.act_ref = bf16[2,81,256]{2,1,0:T(8,128)(2,1)} custom-call(bf16[16,2,81,384]{3,2,1,0:T(8,128)(2,1)} %bitcast.19, bf16[384,512]{1,0:T(8,128)(2,1)} %pad_maximum_fusion.w_ref), custom_call_target="tpu_custom_call" | custom-call | tf_op jit(solution)/shard_map/pallas_call | solution.py:189
  127.9 76.1 %shard_map.67 = f32[81,384]{1,0:T(8,128)} custom-call(bf16[2,81,256]{2,1,0:T(8,128)(2,1)} %shard_map.66.act_ref, bf16[256,384]{1,0:T(8,128)(2,1)} %bitcast.20), custom_call_target="tpu_custom_call" | custom-call | tf_op jit(solution)/shard_map/pallas_call | solution.py:312
  203.9 0.0 copy-done.3
  203.9 0.0 copy-done.4
  204.0 2.2 %convolution_convert_fusion = bf16[288,384]{1,0:T(8,128)(2,1)} fusion(f32[81,384]{1,0:T(8,128)} %shard_map.67, s32[288]{0:T(512)S(1)} %fusion.10, f32[288]{0:T(512)S(1)} %select_reduce_fusion.1, pred[288]{0:T(512)(128)(4,1)S(1)} %fusion.11), kind=kOutput, calls=%fused_computation.1 | convolution fusion | flops 107722656 | bytes 348192 | tf_op jit(solution)/shard_map/dot_general | solution.py:350
  (11 shorter events, 0.1 us)
Async XLA Ops:
  0.0 4.6 %copy-start = (bf16[288,384]{1,0:T(8,128)(2,1)S(1)}, bf16[288,384]{1,0:T(8,128)(2,1)}, u32[]{:S(2)}) copy-start(bf16[288,384]{1,0:T(8,128)(2,1)} %param.6) | copy-start | bytes 663556
  6.6 46.9 %copy-start.1 = (bf16[1,384,256]{2,1,0:T(8,128)(2,1)S(1)}, bf16[1,384,256]{2,1,0:T(8,128)(2,1)}, u32[]{:S(2)}) copy-start(bf16[1,384,256]{2,1,0:T(8,128)(2,1)} %param.10) | copy-start | bytes 589828
  6.6 46.9 %copy-start.2 = (bf16[1,384,256]{2,1,0:T(8,128)(2,1)S(1)}, bf16[1,384,256]{2,1,0:T(8,128)(2,1)}, u32[]{:S(2)}) copy-start(bf16[1,384,256]{2,1,0:T(8,128)(2,1)} %param.9) | copy-start | bytes 589828
  53.5 150.4 %copy-start.3 = (s32[288,2]{0,1:T(2,128)S(1)}, s32[288,2]{0,1:T(2,128)}, u32[]{:S(2)}) copy-start(s32[288,2]{0,1:T(2,128)} %param.7) | copy-start | bytes 6916
  53.5 150.4 %copy-start.4 = (f32[288,2]{0,1:T(2,128)S(1)}, f32[288,2]{0,1:T(2,128)}, u32[]{:S(2)}) copy-start(f32[288,2]{0,1:T(2,128)} %param.8) | copy-start | bytes 6916

commit v10 on v9

--- a/solution.py
+++ b/solution.py
@@ -331,6 +331,161 @@
     )(act, wd)
 
 
+def _up_kernel(nf, chips, slot_ref, w_ref, o_ref, sel_buf, out_buf, in_buf, acc,
+               e_send, s_send, fwd_send, sel_recv, f_send, f_recv):
+    bands = o_ref.shape[0]
+    hidden = o_ref.shape[2]
+    f = lax.axis_index("fsdp")
+    e = lax.axis_index("ed")
+    core = lax.rem(e, 2)
+    chip = e // 2
+    sib = e + 1 - 2 * core
+    mine = core * chips + chip
+
+    def fsdp_peer(i):
+        return lax.rem(f + 1 + i, nf)
+
+    def chip_peer(i):
+        return lax.rem(chip + 1 + i, chips)
+
+    def direct(h):
+        return pltpu.make_async_remote_copy(
+            src_ref=slot_ref,
+            dst_ref=sel_buf.at[mine],
+            send_sem=e_send.at[h],
+            recv_sem=sel_recv.at[mine],
+            device_id={"ed": h * 2 + core},
+            device_id_type=MESH,
+        )
+
+    def forward(blk):
+        return pltpu.make_async_remote_copy(
+            src_ref=sel_buf.at[blk],
+            dst_ref=sel_buf.at[blk],
+            send_sem=fwd_send.at[lax.rem(blk, chips)],
+            recv_sem=sel_recv.at[blk],
+            device_id={"ed": sib},
+            device_id_type=MESH,
+        )
+
+    def partial_copy(g, slot):
+        return pltpu.make_async_remote_copy(
+            src_ref=out_buf.at[g],
+            dst_ref=in_buf.at[slot],
+            send_sem=f_send.at[g],
+            recv_sem=f_recv.at[slot],
+            device_id={"fsdp": g},
+            device_id_type=MESH,
+        )
+
+    barrier = pltpu.get_barrier_semaphore()
+
+    def greet_fsdp(i, carry):
+        pl.semaphore_signal(barrier, 1, device_id={"fsdp": fsdp_peer(i)}, device_id_type=MESH)
+        return carry
+
+    def greet_ed(i, carry):
+        pl.semaphore_signal(barrier, 1, device_id={"ed": chip_peer(i) * 2 + core}, device_id_type=MESH)
+        return carry
+
+    lax.fori_loop(0, nf - 1, greet_fsdp, 0)
+    lax.fori_loop(0, chips - 1, greet_ed, 0)
+    pl.semaphore_signal(barrier, 1, device_id={"ed": sib}, device_id_type=MESH)
+    pl.semaphore_wait(barrier, nf - 1 + chips)
+
+    def send_slots(i, carry):
+        direct(chip_peer(i)).start()
+        return carry
+
+    lax.fori_loop(0, chips - 1, send_slots, 0)
+    to_sib = pltpu.make_async_remote_copy(
+        src_ref=slot_ref,
+        dst_ref=sel_buf.at[mine],
+        send_sem=s_send,
+        recv_sem=sel_recv.at[mine],
+        device_id={"ed": sib},
+        device_id_type=MESH,
+    )
+    to_sib.start()
+    sel_buf[mine] = slot_ref[...]
+
+    def band(i, carry):
+        j = lax.rem(f + 1 + i, nf)
+        for t in range(bands):
+            blk = j * bands + t
+            same_core = (blk // chips) == core
+            not_mine = blk != mine
+
+            @pl.when(same_core & not_mine)
+            def _():
+                forward(blk).wait_recv()
+                forward(blk).start()
+
+            @pl.when(jnp.logical_not(same_core))
+            def _():
+                forward(blk).wait_recv()
+
+        for t in range(bands):
+            blk = j * bands + t
+            out_buf[j, t] = jnp.dot(
+                sel_buf[blk], w_ref[...], preferred_element_type=jnp.float32
+            ).astype(out_buf.dtype)
+
+        @pl.when(j != f)
+        def _():
+            partial_copy(j, f).start()
+
+        return carry
+
+    lax.fori_loop(0, nf, band, 0)
+    acc[...] = out_buf[f].astype(jnp.float32)
+
+    def gather(i, carry):
+        g = fsdp_peer(i)
+        partial_copy(g, f).wait_send()
+        partial_copy(g, g).wait_recv()
+        acc[...] += in_buf[g].astype(jnp.float32)
+        return carry
+
+    lax.fori_loop(0, nf - 1, gather, 0)
+
+    def drain(i, carry):
+        h = chip_peer(i)
+        direct(h).wait_send()
+        forward(core * chips + h).wait_send()
+        return carry
+
+    lax.fori_loop(0, chips - 1, drain, 0)
+    to_sib.wait_send()
+    total = acc[...]
+    o_ref[...] = (jax.nn.silu(total[..., :hidden]) * total[..., hidden:]).astype(o_ref.dtype)
+
+
+def slots_to_act(slots, w, nf, chips, cid):
+    rows, d = slots.shape
+    hidden = w.shape[1] // 2
+    bands = 2 * chips // nf
+    return pl.pallas_call(
+        functools.partial(_up_kernel, nf, chips),
+        out_shape=jax.ShapeDtypeStruct((bands, rows, hidden), jnp.bfloat16),
+        in_specs=[pl.BlockSpec(memory_space=pltpu.VMEM)] * 2,
+        out_specs=pl.BlockSpec(memory_space=pltpu.VMEM),
+        scratch_shapes=[
+            pltpu.VMEM((2 * chips, rows, d), jnp.bfloat16),
+            pltpu.VMEM((nf, bands, rows, 2 * hidden), jnp.bfloat16),
+            pltpu.VMEM((nf, bands, rows, 2 * hidden), jnp.bfloat16),
+            pltpu.VMEM((bands, rows, 2 * hidden), jnp.float32),
+            pltpu.SemaphoreType.DMA((chips,)),
+            pltpu.SemaphoreType.DMA,
+            pltpu.SemaphoreType.DMA((chips,)),
+            pltpu.SemaphoreType.DMA((2 * chips,)),
+            pltpu.SemaphoreType.DMA((nf,)),
+            pltpu.SemaphoreType.DMA((nf,)),
+        ],
+        compiler_params=pltpu.CompilerParams(collective_id=cid, has_side_effects=True),
+    )(slots, w)
+
+
 def local(tokens, expert_ids, route_weights, w_gate, w_up, w_down):
     window = w_gate.shape[0]
     features_dev = tokens.shape[1]
@@ -340,11 +495,8 @@
     chips = n_ed // 2
     per_band = n_ed // n_fsdp
     own_slots = pick_rows(tokens[None], expert_ids[None], window, CAP)[0, 0]
-    same_core = exchange(own_slots, "ed", chips, 2, True, 0)
-    selected = exchange(same_core, "ed", 2, 1, True, 1)
-    selected = selected.reshape(n_fsdp, per_band, CAP, features_dev)
     both = jnp.concatenate([w_gate[0], w_up[0]], axis=1)
-    activation = gate_act(selected, both, "fsdp", n_fsdp, 2)
+    activation = slots_to_act(own_slots, both, n_fsdp, chips, 2)
     slot_out = down_terms(activation, w_down[0], n_fsdp, chips, 3)
     weights_matrix = combine_matrix(expert_ids, route_weights, window, CAP)
     mixed = jnp.dot(

time: 207 us -> 196 us (0.947)
  Pallas kernels: 196 us -> 183 us
    pallas_call x3 -> x1, Pallas kernels: 120 us -> 106 us  [slots_to_act(): pl.pallas_call(functools.partial(_up_kernel, nf, chips), out_shape=jax.Sh...]
where the time goes in v10:
time: 196 us; the launch traced here: 193 us
  Pallas kernels  183 us (93%)
  other arithmetic  5.78 us (3%)
  matrix products  2.2 us (1%)
    pallas_call x1, Pallas kernels, slots_to_act(): pl.pallas_call(functools.partial(_up_kernel, nf, chips), out_shape=jax.Sh...  106 us
    pallas_call x1, Pallas kernels, down_terms(): pl.pallas_call(functools.partial(_down_kernel, nf, chips), out_shape=jax....  77 us

profile of v10, /device:TPU:1, one launch (start us, length us, event | category | flops | bytes accessed | tf_op | source)
XLA Modules:
  0.0 193.2 jit_solution(6914550267972562488)
XLA Ops:
  0.0 0.0 copy-start
  0.0 0.7 fusion.11
  0.8 0.3 reduce-window.6
  1.1 0.2 slice_reduce_fusion
  1.3 0.2 reduce-window.9
  1.5 0.1 broadcast.180
  1.6 3.0 %convert_reduce_fusion = (s32[81]{0:T(128)S(1)}, s32[81]{0:T(128)S(1)}) fusion(pred[288]{0:T(512)(128)(4,1)S(1)} %fusion.11, s32[288]{0:T(512)S(1)} %fusion.10), kind=kLoop, calls=%fused_computation.10 | loop fusion | flops 139806 | bytes 2088 | tf_op jit(solution)/shard_map/reduce_sum | solution.py:33
  4.6 0.0 copy-done
  4.6 0.0 copy-start.1
  4.6 0.0 copy-start.2
  4.6 1.3 gather_fusion
  5.9 0.7 select_select_fusion.slot_ref
  6.7 0.0 copy-done.1
  6.7 0.0 copy-done.2
  6.7 0.8 pad_maximum_fusion.w_ref
  7.4 106.5 %shard_map.64.act_ref = bf16[2,81,256]{2,1,0:T(8,128)(2,1)} custom-call(bf16[81,384]{1,0:T(8,128)(2,1)} %select_select_fusion.slot_ref, bf16[384,512]{1,0:T(8,128)(2,1)} %pad_maximum_fusion.w_ref), custom_call_target="tpu_custom_call" | custom-call | tf_op jit(solution)/shard_map/pallas_call | solution.py:468
  113.9 0.0 copy-start.3
  113.9 0.0 copy-start.4
  113.9 77.0 %shard_map.65 = f32[81,384]{1,0:T(8,128)} custom-call(bf16[2,81,256]{2,1,0:T(8,128)(2,1)} %shard_map.64.act_ref, bf16[256,384]{1,0:T(8,128)(2,1)} %bitcast.18), custom_call_target="tpu_custom_call" | custom-call | tf_op jit(solution)/shard_map/pallas_call | solution.py:312
  191.0 0.0 copy-done.3
  191.0 0.0 copy-done.4
  191.0 2.2 %convolution_convert_fusion = bf16[288,384]{1,0:T(8,128)(2,1)} fusion(f32[81,384]{1,0:T(8,128)} %shard_map.65, s32[288]{0:T(512)S(1)} %fusion.10, f32[288]{0:T(512)S(1)} %select_reduce_fusion.1, pred[288]{0:T(512)(128)(4,1)S(1)} %fusion.11), kind=kOutput, calls=%fused_computation.1 | convolution fusion | flops 107722656 | bytes 348192 | tf_op jit(solution)/shard_map/dot_general | solution.py:502
  (11 shorter events, 0.1 us)
Async XLA Ops:
  0.0 4.6 %copy-start = (bf16[288,384]{1,0:T(8,128)(2,1)S(1)}, bf16[288,384]{1,0:T(8,128)(2,1)}, u32[]{:S(2)}) copy-start(bf16[288,384]{1,0:T(8,128)(2,1)} %param.6) | copy-start | bytes 663556
  4.6 2.0 %copy-start.1 = (bf16[1,384,256]{2,1,0:T(8,128)(2,1)S(1)}, bf16[1,384,256]{2,1,0:T(8,128)(2,1)}, u32[]{:S(2)}) copy-start(bf16[1,384,256]{2,1,0:T(8,128)(2,1)} %param.10) | copy-start | bytes 589828
  4.6 2.0 %copy-start.2 = (bf16[1,384,256]{2,1,0:T(8,128)(2,1)S(1)}, bf16[1,384,256]{2,1,0:T(8,128)(2,1)}, u32[]{:S(2)}) copy-start(bf16[1,384,256]{2,1,0:T(8,128)(2,1)} %param.9) | copy-start | bytes 589828
  113.9 77.1 %copy-start.3 = (s32[288,2]{0,1:T(2,128)S(1)}, s32[288,2]{0,1:T(2,128)}, u32[]{:S(2)}) copy-start(s32[288,2]{0,1:T(2,128)} %param.7) | copy-start | bytes 6916
  113.9 77.0 %copy-start.4 = (f32[288,2]{0,1:T(2,128)S(1)}, f32[288,2]{0,1:T(2,128)}, u32[]{:S(2)}) copy-start(f32[288,2]{0,1:T(2,128)} %param.8) | copy-start | bytes 6916

commit v11 on v10

--- a/solution.py
+++ b/solution.py
@@ -331,7 +331,7 @@
     )(act, wd)
 
 
-def _up_kernel(nf, chips, slot_ref, w_ref, o_ref, sel_buf, out_buf, in_buf, acc,
+def _up_kernel(nf, chips, slot_ref, wg_ref, wu_ref, o_ref, sel_buf, out_buf, in_buf, acc,
                e_send, s_send, fwd_send, sel_recv, f_send, f_recv):
     bands = o_ref.shape[0]
     hidden = o_ref.shape[2]
@@ -427,8 +427,12 @@
 
         for t in range(bands):
             blk = j * bands + t
-            out_buf[j, t] = jnp.dot(
-                sel_buf[blk], w_ref[...], preferred_element_type=jnp.float32
+            rows_in = sel_buf[blk]
+            out_buf[j, t, :, :hidden] = jnp.dot(
+                rows_in, wg_ref[...], preferred_element_type=jnp.float32
+            ).astype(out_buf.dtype)
+            out_buf[j, t, :, hidden:] = jnp.dot(
+                rows_in, wu_ref[...], preferred_element_type=jnp.float32
             ).astype(out_buf.dtype)
 
         @pl.when(j != f)
@@ -461,14 +465,14 @@
     o_ref[...] = (jax.nn.silu(total[..., :hidden]) * total[..., hidden:]).astype(o_ref.dtype)
 
 
-def slots_to_act(slots, w, nf, chips, cid):
+def slots_to_act(slots, wg, wu, nf, chips, cid):
     rows, d = slots.shape
-    hidden = w.shape[1] // 2
+    hidden = wg.shape[1]
     bands = 2 * chips // nf
     return pl.pallas_call(
         functools.partial(_up_kernel, nf, chips),
         out_shape=jax.ShapeDtypeStruct((bands, rows, hidden), jnp.bfloat16),
-        in_specs=[pl.BlockSpec(memory_space=pltpu.VMEM)] * 2,
+        in_specs=[pl.BlockSpec(memory_space=pltpu.VMEM)] * 3,
         out_specs=pl.BlockSpec(memory_space=pltpu.VMEM),
         scratch_shapes=[
             pltpu.VMEM((2 * chips, rows, d), jnp.bfloat16),
@@ -483,7 +487,7 @@
             pltpu.SemaphoreType.DMA((nf,)),
         ],
         compiler_params=pltpu.CompilerParams(collective_id=cid, has_side_effects=True),
-    )(slots, w)
+    )(slots, wg, wu)
 
 
 def local(tokens, expert_ids, route_weights, w_gate, w_up, w_down):
@@ -494,11 +498,22 @@
     n_fsdp = lax.axis_size("fsdp")
     chips = n_ed // 2
     per_band = n_ed // n_fsdp
-    own_slots = pick_rows(tokens[None], expert_ids[None], window, CAP)[0, 0]
-    both = jnp.concatenate([w_gate[0], w_up[0]], axis=1)
-    activation = slots_to_act(own_slots, both, n_fsdp, chips, 2)
+    tok_dev = tokens.shape[0]
+    order = jnp.arange(tok_dev, dtype=jnp.int32)
+    routed = jnp.any(expert_ids == 0, axis=1)
+    lower = (order[:, None] >= order[None, :]).astype(jnp.bfloat16)
+    count = jnp.dot(lower, routed.astype(jnp.bfloat16), preferred_element_type=jnp.float32)
+    slot_ids = jnp.arange(CAP, dtype=jnp.float32)
+    match = routed[None, :] & (count[None, :] - 1.0 == slot_ids[:, None])
+    own_slots = jnp.dot(
+        match.astype(jnp.bfloat16), tokens, preferred_element_type=jnp.float32
+    ).astype(jnp.bfloat16)
+    activation = slots_to_act(own_slots, w_gate[0], w_up[0], n_fsdp, chips, 2)
     slot_out = down_terms(activation, w_down[0], n_fsdp, chips, 3)
-    weights_matrix = combine_matrix(expert_ids, route_weights, window, CAP)
+    per_expert = jnp.sum(
+        jnp.where(expert_ids == 0, route_weights, jnp.zeros_like(route_weights)), axis=1
+    )
+    weights_matrix = match.T.astype(jnp.float32) * per_expert[:, None]
     mixed = jnp.dot(
         weights_matrix,
         slot_out.reshape(window * CAP, features_dev),

time: 196 us -> 191 us (0.974)
  other arithmetic: 5.78 us -> 0.05 us
    reduce_sum x2 -> x1, other arithmetic: 2.99 us -> 0.02 us  [local(): jnp.sum(jnp.where(expert_ids == 0, route_weights, jnp.zeros_like(route_we...]
where the time goes in v11:
time: 191 us; the launch traced here: 188 us
  Pallas kernels  183 us (96%)
  matrix products  3.23 us (2%)
    pallas_call x1, Pallas kernels, slots_to_act(): pl.pallas_call(functools.partial(_up_kernel, nf, chips), out_shape=jax.Sh...  107 us
    pallas_call x1, Pallas kernels, down_terms(): pl.pallas_call(functools.partial(_down_kernel, nf, chips), out_shape=jax....  76.8 us

profile of v11, /device:TPU:1, one launch (start us, length us, event | category | flops | bytes accessed | tf_op | source)
XLA Modules:
  0.0 188.1 jit_solution(13753048386646657016)
XLA Ops:
  0.0 0.0 copy-start
  0.0 0.0 copy-start.1
  0.0 0.7 copy-done.1
  0.8 0.2 convolution_reduce_fusion
  1.0 0.0 copy-start.2
  1.0 0.7 copy-done.2
  1.7 0.0 copy-done
  1.7 0.8 convolution_convert_fusion.1.slot_ref
  2.5 106.6 %shard_map.64.act_ref = bf16[2,81,256]{2,1,0:T(8,128)(2,1)} custom-call(bf16[81,384]{1,0:T(8,128)(2,1)} %convolution_convert_fusion.1.slot_ref, bf16[384,256]{1,0:T(8,128)(2,1)} %bitcast.6, bf16[384,256]{1,0:T(8,128)(2,1)} %bitcast.7), custom_call_target="tpu_custom_call" | custom-call | tf_op jit(solution)/shard_map/pallas_call | solution.py:472
  109.1 76.8 %shard_map.65 = f32[81,384]{1,0:T(8,128)} custom-call(bf16[2,81,256]{2,1,0:T(8,128)(2,1)} %shard_map.64.act_ref, bf16[256,384]{1,0:T(8,128)(2,1)} %bitcast.8), custom_call_target="tpu_custom_call" | custom-call | tf_op jit(solution)/shard_map/pallas_call | solution.py:312
  185.9 2.2 %convolution_convert_fusion = bf16[288,384]{1,0:T(8,128)(2,1)} fusion(f32[81,384]{1,0:T(8,128)} %shard_map.65, f32[288]{0:T(512)S(1)} %select_reduce_fusion, f32[288]{0:T(512)S(1)} %broadcast_add_fusion, pred[288]{0:T(512)(128)(4,1)S(1)} %fusion.11), kind=kOutput, calls=%fused_computation | convolution fusion | flops 107676000 | bytes 348192 | tf_op jit(solution)/shard_map/dot_general | solution.py:517
  (4 shorter events, 0.1 us)
Async XLA Ops:
  0.0 1.7 copy-start
  0.0 0.7 copy-start.1
  1.0 0.7 copy-start.2

commit v12 on v11

--- a/solution.py
+++ b/solution.py
@@ -203,7 +203,7 @@
 
 
 def _down_kernel(nf, chips, act_ref, wd_ref, o_ref, act_buf, term_buf, sib_buf, pre_buf, in_buf,
-                 a_send, a_recv, s_send, s_recv, e_send, e_recv):
+                 a_send, a_recv, s_send, s_recv, e_send, e_recv, greet=True):
     bands = act_ref.shape[0]
     f = lax.axis_index("fsdp")
     e = lax.axis_index("ed")
@@ -247,10 +247,11 @@
         pl.semaphore_signal(barrier, 1, device_id={"ed": chip_peer(i) * 2 + core}, device_id_type=MESH)
         return carry
 
-    lax.fori_loop(0, nf - 1, greet_fsdp, 0)
-    lax.fori_loop(0, chips - 1, greet_ed, 0)
-    pl.semaphore_signal(barrier, 1, device_id={"ed": sib}, device_id_type=MESH)
-    pl.semaphore_wait(barrier, nf - 1 + chips)
+    if greet:
+        lax.fori_loop(0, nf - 1, greet_fsdp, 0)
+        lax.fori_loop(0, chips - 1, greet_ed, 0)
+        pl.semaphore_signal(barrier, 1, device_id={"ed": sib}, device_id_type=MESH)
+        pl.semaphore_wait(barrier, nf - 1 + chips)
 
     def send_act(i, carry):
         act_copy(fsdp_peer(i), f).start()
@@ -488,6 +489,55 @@
         ],
         compiler_params=pltpu.CompilerParams(collective_id=cid, has_side_effects=True),
     )(slots, wg, wu)
+
+def _layer_kernel(nf, chips, slot_ref, wg_ref, wu_ref, wd_ref, comb_ref, o_ref, *scratch):
+    up_scratch, act_s, down_scratch, slot_out = scratch[:10], scratch[10], scratch[11:22], scratch[22]
+    _up_kernel(nf, chips, slot_ref, wg_ref, wu_ref, act_s, *up_scratch)
+    _down_kernel(nf, chips, act_s, wd_ref, slot_out, *down_scratch, greet=False)
+    o_ref[...] = jnp.dot(
+        comb_ref[...], slot_out[...], precision=lax.Precision.HIGHEST,
+        preferred_element_type=jnp.float32,
+    ).astype(o_ref.dtype)
+
+
+def moe_layer(slots, wg, wu, wd, comb, nf, chips, cid):
+    rows, d = slots.shape
+    hidden = wg.shape[1]
+    bands = 2 * chips // nf
+    blocks = nf * bands
+    tok = comb.shape[0]
+    return pl.pallas_call(
+        functools.partial(_layer_kernel, nf, chips),
+        out_shape=jax.ShapeDtypeStruct((tok, d), jnp.bfloat16),
+        in_specs=[pl.BlockSpec(memory_space=pltpu.VMEM)] * 5,
+        out_specs=pl.BlockSpec(memory_space=pltpu.VMEM),
+        scratch_shapes=[
+            pltpu.VMEM((2 * chips, rows, d), jnp.bfloat16),
+            pltpu.VMEM((nf, bands, rows, 2 * hidden), jnp.bfloat16),
+            pltpu.VMEM((nf, bands, rows, 2 * hidden), jnp.bfloat16),
+            pltpu.VMEM((bands, rows, 2 * hidden), jnp.float32),
+            pltpu.SemaphoreType.DMA((chips,)),
+            pltpu.SemaphoreType.DMA,
+            pltpu.SemaphoreType.DMA((chips,)),
+            pltpu.SemaphoreType.DMA((2 * chips,)),
+            pltpu.SemaphoreType.DMA((nf,)),
+            pltpu.SemaphoreType.DMA((nf,)),
+            pltpu.VMEM((bands, rows, hidden), jnp.bfloat16),
+            pltpu.VMEM((nf, bands, rows, hidden), jnp.bfloat16),
+            pltpu.VMEM((blocks, rows, d), jnp.bfloat16),
+            pltpu.VMEM((chips, rows, d), jnp.bfloat16),
+            pltpu.VMEM((chips, rows, d), jnp.bfloat16),
+            pltpu.VMEM((chips, rows, d), jnp.bfloat16),
+            pltpu.SemaphoreType.DMA((nf,)),
+            pltpu.SemaphoreType.DMA((nf,)),
+            pltpu.SemaphoreType.DMA,
+            pltpu.SemaphoreType.DMA,
+            pltpu.SemaphoreType.DMA((chips,)),
+            pltpu.SemaphoreType.DMA((chips,)),
+            pltpu.VMEM((rows, d), jnp.float32),
+        ],
+        compiler_params=pltpu.CompilerParams(collective_id=cid, has_side_effects=True),
+    )(slots, wg, wu, wd, comb)
 
 
 def local(tokens, expert_ids, route_weights, w_gate, w_up, w_down):
@@ -508,19 +558,11 @@
     own_slots = jnp.dot(
         match.astype(jnp.bfloat16), tokens, preferred_element_type=jnp.float32
     ).astype(jnp.bfloat16)
-    activation = slots_to_act(own_slots, w_gate[0], w_up[0], n_fsdp, chips, 2)
-    slot_out = down_terms(activation, w_down[0], n_fsdp, chips, 3)
     per_expert = jnp.sum(
         jnp.where(expert_ids == 0, route_weights, jnp.zeros_like(route_weights)), axis=1
     )
     weights_matrix = match.T.astype(jnp.float32) * per_expert[:, None]
-    mixed = jnp.dot(
-        weights_matrix,
-        slot_out.reshape(window * CAP, features_dev),
-        precision=lax.Precision.HIGHEST,
-        preferred_element_type=jnp.float32,
-    )
-    return mixed.astype(jnp.bfloat16)
+    return moe_layer(own_slots, w_gate[0], w_up[0], w_down[0], weights_matrix, n_fsdp, chips, 2)
 
 
 def solution(mesh):

time: 191 us -> 190 us (level); the launches traced: 188 us -> 190 us
  matrix products: 3.23 us -> 1.02 us
  Pallas kernels: 183 us -> 185 us
    dot_general x1 -> x0, matrix products: 2.21 us -> none  [local(): jnp.dot(weights_matrix, slot_out.reshape(window * CAP, features_dev), pre...]
    pallas_call x2 -> x1, Pallas kernels: 183 us -> 185 us  [moe_layer(): pl.pallas_call(functools.partial(_layer_kernel, nf, chips), out_shape=jax...]
where the time goes in v12:
time: 190 us
  Pallas kernels  185 us (97%)
  local copies, waits for them, and re-layouts  3.05 us (2%)
    pallas_call x1, Pallas kernels, moe_layer(): pl.pallas_call(functools.partial(_layer_kernel, nf, chips), out_shape=jax...  185 us

profile of v12, /device:TPU:1, one launch (start us, length us, event | category | flops | bytes accessed | tf_op | source)
XLA Modules:
  0.0 190.2 jit_solution(9928621195945440042)
XLA Ops:
  0.0 0.0 copy-start
  0.0 0.0 copy-start.1
  0.0 0.7 copy-done.1
  0.8 0.2 convolution_reduce_fusion
  1.0 0.0 copy-start.2
  1.0 0.7 copy-done.2
  1.7 0.0 copy-done
  1.7 0.8 convolution_convert_fusion.slot_ref
  2.5 0.8 fusion.1.comb_ref
  3.3 185.2 %shard_map.64 = bf16[288,384]{1,0:T(8,128)(2,1)} custom-call(bf16[81,384]{1,0:T(8,128)(2,1)} %convolution_convert_fusion.slot_ref, bf16[384,256]{1,0:T(8,128)(2,1)} %bitcast.5, bf16[384,256]{1,0:T(8,128)(2,1)} %bitcast.6, bf16[256,384]{1,0:T(8,128)(2,1)} %bitcast.7, f32[288,81]{1,0:T(8,128)} %fusion.1.comb_ref), custom_call_target="tpu_custom_call" | custom-call | tf_op jit(solution)/shard_map/pallas_call | solution.py:509
  188.5 1.6 copy.8
  (4 shorter events, 0.1 us)
Async XLA Ops:
  0.0 1.7 copy-start
  0.0 0.7 copy-start.1
  1.0 0.7 copy-start.2

commit v13 on v12

--- a/solution.py
+++ b/solution.py
@@ -52,158 +52,8 @@
     )
 
 
-def _exchange_kernel(axis, m, stride, gather, x_ref, o_ref, send_sem, recv_sem, own_sem):
-    me = lax.axis_index(axis)
-    k = lax.rem(me // stride, m)
-    base = me - k * stride
-
-    def member(i):
-        return lax.rem(k + 1 + i, m)
-
-    def device(j):
-        return {axis: base + j * stride}
-
-    def source(j):
-        return x_ref if gather else x_ref.at[j]
-
-    def outgoing(j):
-        return pltpu.make_async_remote_copy(
-            src_ref=source(j),
-            dst_ref=o_ref.at[k],
-            send_sem=send_sem.at[j],
-            recv_sem=recv_sem.at[k],
-            device_id=device(j),
-            device_id_type=MESH,
-        )
-
-    def incoming(j):
-        return pltpu.make_async_remote_copy(
-            src_ref=source(j),
-            dst_ref=o_ref.at[j],
-            send_sem=send_sem.at[j],
-            recv_sem=recv_sem.at[j],
-            device_id=device(j),
-            device_id_type=MESH,
-        )
-
-    barrier = pltpu.get_barrier_semaphore()
-
-    def greet(i, carry):
-        pl.semaphore_signal(barrier, 1, device_id=device(member(i)), device_id_type=MESH)
-        return carry
-
-    lax.fori_loop(0, m - 1, greet, 0)
-    pl.semaphore_wait(barrier, m - 1)
-
-    def send(i, carry):
-        outgoing(member(i)).start()
-        return carry
-
-    lax.fori_loop(0, m - 1, send, 0)
-    own = pltpu.make_async_copy(source(k), o_ref.at[k], own_sem)
-    own.start()
-
-    def finish(i, carry):
-        j = member(i)
-        outgoing(j).wait_send()
-        incoming(j).wait_recv()
-        return carry
-
-    lax.fori_loop(0, m - 1, finish, 0)
-    own.wait()
-
-
-def exchange(x, axis, m, stride, gather, cid):
-    block = x.shape if gather else x.shape[1:]
-    return pl.pallas_call(
-        functools.partial(_exchange_kernel, axis, m, stride, gather),
-        out_shape=jax.ShapeDtypeStruct((m,) + tuple(block), x.dtype),
-        in_specs=[pl.BlockSpec(memory_space=pltpu.VMEM)],
-        out_specs=pl.BlockSpec(memory_space=pltpu.VMEM),
-        scratch_shapes=[
-            pltpu.SemaphoreType.DMA((m,)),
-            pltpu.SemaphoreType.DMA((m,)),
-            pltpu.SemaphoreType.DMA,
-        ],
-        compiler_params=pltpu.CompilerParams(collective_id=cid, has_side_effects=True),
-    )(x)
-
-
-def _gate_kernel(axis, m, hidden, sel_ref, w_ref, o_ref, out_buf, in_buf, acc, send_sem, recv_sem):
-    me = lax.axis_index(axis)
-    bands = sel_ref.shape[1]
-
-    def member(i):
-        return lax.rem(me + 1 + i, m)
-
-    def copy(j, slot):
-        return pltpu.make_async_remote_copy(
-            src_ref=out_buf.at[j],
-            dst_ref=in_buf.at[slot],
-            send_sem=send_sem.at[j],
-            recv_sem=recv_sem.at[slot],
-            device_id={axis: j},
-            device_id_type=MESH,
-        )
-
-    def partial(j, b):
-        return jnp.dot(sel_ref[j, b], w_ref[...], preferred_element_type=jnp.float32)
-
-    barrier = pltpu.get_barrier_semaphore()
-
-    def greet(i, carry):
-        pl.semaphore_signal(barrier, 1, device_id={axis: member(i)}, device_id_type=MESH)
-        return carry
-
-    lax.fori_loop(0, m - 1, greet, 0)
-    pl.semaphore_wait(barrier, m - 1)
-
-    def send(i, carry):
-        j = member(i)
-        for b in range(bands):
-            out_buf[j, b] = partial(j, b).astype(out_buf.dtype)
-        copy(j, me).start()
-        return carry
-
-    lax.fori_loop(0, m - 1, send, 0)
-    for b in range(bands):
-        acc[b] = partial(me, b)
-
-    def gather(i, carry):
-        j = member(i)
-        copy(j, me).wait_send()
-        copy(j, j).wait_recv()
-        acc[...] += in_buf[j].astype(jnp.float32)
-        return carry
-
-    lax.fori_loop(0, m - 1, gather, 0)
-    total = acc[...]
-    gate = total[..., :hidden]
-    up = total[..., hidden:]
-    o_ref[...] = (jax.nn.silu(gate) * up).astype(o_ref.dtype)
-
-
-def gate_act(sel, w, axis, m, cid):
-    _, bands, rows, _ = sel.shape
-    hidden = w.shape[1] // 2
-    return pl.pallas_call(
-        functools.partial(_gate_kernel, axis, m, hidden),
-        out_shape=jax.ShapeDtypeStruct((bands, rows, hidden), jnp.bfloat16),
-        in_specs=[pl.BlockSpec(memory_space=pltpu.VMEM)] * 2,
-        out_specs=pl.BlockSpec(memory_space=pltpu.VMEM),
-        scratch_shapes=[
-            pltpu.VMEM((m, bands, rows, 2 * hidden), jnp.bfloat16),
-            pltpu.VMEM((m, bands, rows, 2 * hidden), jnp.bfloat16),
-            pltpu.VMEM((bands, rows, 2 * hidden), jnp.float32),
-            pltpu.SemaphoreType.DMA((m,)),
-            pltpu.SemaphoreType.DMA((m,)),
-        ],
-        compiler_params=pltpu.CompilerParams(collective_id=cid, has_side_effects=True),
-    )(sel, w)
-
-
 def _down_kernel(nf, chips, act_ref, wd_ref, o_ref, act_buf, term_buf, sib_buf, pre_buf, in_buf,
-                 a_send, a_recv, s_send, s_recv, e_send, e_recv, greet=True):
+                 a_send, a_recv, s_send, s_recv, e_send, e_recv):
     bands = act_ref.shape[0]
     f = lax.axis_index("fsdp")
     e = lax.axis_index("ed")
@@ -227,6 +77,17 @@
             device_id_type=MESH,
         )
 
+    def to_sibling(blk):
+        h = lax.rem(blk, chips)
+        return pltpu.make_async_remote_copy(
+            src_ref=term_buf.at[blk],
+            dst_ref=sib_buf.at[h],
+            send_sem=s_send.at[h],
+            recv_sem=s_recv.at[h],
+            device_id={"ed": sib},
+            device_id_type=MESH,
+        )
+
     def piece_copy(h, slot):
         return pltpu.make_async_remote_copy(
             src_ref=pre_buf.at[h],
@@ -237,64 +98,51 @@
             device_id_type=MESH,
         )
 
-    barrier = pltpu.get_barrier_semaphore()
-
-    def greet_fsdp(i, carry):
-        pl.semaphore_signal(barrier, 1, device_id={"fsdp": fsdp_peer(i)}, device_id_type=MESH)
-        return carry
-
-    def greet_ed(i, carry):
-        pl.semaphore_signal(barrier, 1, device_id={"ed": chip_peer(i) * 2 + core}, device_id_type=MESH)
-        return carry
-
-    if greet:
-        lax.fori_loop(0, nf - 1, greet_fsdp, 0)
-        lax.fori_loop(0, chips - 1, greet_ed, 0)
-        pl.semaphore_signal(barrier, 1, device_id={"ed": sib}, device_id_type=MESH)
-        pl.semaphore_wait(barrier, nf - 1 + chips)
-
     def send_act(i, carry):
         act_copy(fsdp_peer(i), f).start()
         return carry
 
     lax.fori_loop(0, nf - 1, send_act, 0)
-    for b in range(bands):
-        term_buf[f * bands + b] = jnp.dot(
-            act_ref[b], wd_ref[...], preferred_element_type=jnp.float32
-        ).astype(term_buf.dtype)
-
-    def take_act(i, carry):
-        g = fsdp_peer(i)
-        act_copy(g, f).wait_send()
-        act_copy(g, g).wait_recv()
-        for b in range(bands):
-            term_buf[g * bands + b] = jnp.dot(
-                act_buf[g, b], wd_ref[...], preferred_element_type=jnp.float32
+    act_buf[f] = act_ref[...]
+    o_ref[...] = jnp.zeros_like(o_ref)
+
+    def band(i, carry):
+        j = lax.rem(f + i, nf)
+
+        @pl.when(i > 0)
+        def _():
+            act_copy(j, f).wait_send()
+            act_copy(j, j).wait_recv()
+
+        for t in range(bands):
+            blk = j * bands + t
+            h = lax.rem(blk, chips)
+            term_buf[blk] = jnp.dot(
+                act_buf[j, t], wd_ref[...], preferred_element_type=jnp.float32
             ).astype(term_buf.dtype)
-        return carry
-
-    lax.fori_loop(0, nf - 1, take_act, 0)
-
-    pair = pltpu.make_async_remote_copy(
-        src_ref=term_buf.at[pl.ds((1 - core) * chips, chips)],
-        dst_ref=sib_buf,
-        send_sem=s_send,
-        recv_sem=s_recv,
-        device_id={"ed": sib},
-        device_id_type=MESH,
-    )
-    pair.start()
-    pair.wait_send()
-    pair.wait_recv()
-    mine = term_buf[pl.ds(core * chips, chips)].astype(jnp.float32)
-    pre_buf[...] = (mine + sib_buf[...].astype(jnp.float32)).astype(pre_buf.dtype)
-
-    def send_piece(i, carry):
-        piece_copy(chip_peer(i), chip).start()
-        return carry
-
-    lax.fori_loop(0, chips - 1, send_piece, 0)
-    o_ref[...] = pre_buf[chip].astype(jnp.float32)
+            same_core = (blk // chips) == core
+
+            @pl.when(jnp.logical_not(same_core))
+            def _():
+                to_sibling(blk).start()
+
+            @pl.when(same_core)
+            def _():
+                to_sibling(blk).wait_recv()
+                pair = term_buf[blk].astype(jnp.float32) + sib_buf[h].astype(jnp.float32)
+                pre_buf[h] = pair.astype(pre_buf.dtype)
+
+                @pl.when(h == chip)
+                def _():
+                    o_ref[...] += pre_buf[h].astype(jnp.float32)
+
+                @pl.when(h != chip)
+                def _():
+                    piece_copy(h, chip).start()
+
+        return carry
+
+    lax.fori_loop(0, nf, band, 0)
 
     def take_piece(i, carry):
         h = chip_peer(i)
@@ -305,31 +153,11 @@
 
     lax.fori_loop(0, chips - 1, take_piece, 0)
 
-
-def down_terms(act, wd, nf, chips, cid):
-    bands, rows, hidden = act.shape
-    d = wd.shape[1]
-    blocks = nf * bands
-    return pl.pallas_call(
-        functools.partial(_down_kernel, nf, chips),
-        out_shape=jax.ShapeDtypeStruct((rows, d), jnp.float32),
-        in_specs=[pl.BlockSpec(memory_space=pltpu.VMEM)] * 2,
-        out_specs=pl.BlockSpec(memory_space=pltpu.VMEM),
-        scratch_shapes=[
-            pltpu.VMEM((nf, bands, rows, hidden), jnp.bfloat16),
-            pltpu.VMEM((blocks, rows, d), jnp.bfloat16),
-            pltpu.VMEM((chips, rows, d), jnp.bfloat16),
-            pltpu.VMEM((chips, rows, d), jnp.bfloat16),
-            pltpu.VMEM((chips, rows, d), jnp.bfloat16),
-            pltpu.SemaphoreType.DMA((nf,)),
-            pltpu.SemaphoreType.DMA((nf,)),
-            pltpu.SemaphoreType.DMA,
-            pltpu.SemaphoreType.DMA,
-            pltpu.SemaphoreType.DMA((chips,)),
-            pltpu.SemaphoreType.DMA((chips,)),
-        ],
-        compiler_params=pltpu.CompilerParams(collective_id=cid, has_side_effects=True),
-    )(act, wd)
+    def drain(h, carry):
+        to_sibling((1 - core) * chips + h).wait_send()
+        return carry
+
+    lax.fori_loop(0, chips, drain, 0)
 
 
 def _up_kernel(nf, chips, slot_ref, wg_ref, wu_ref, o_ref, sel_buf, out_buf, in_buf, acc,
@@ -466,34 +294,10 @@
     o_ref[...] = (jax.nn.silu(total[..., :hidden]) * total[..., hidden:]).astype(o_ref.dtype)
 
 
-def slots_to_act(slots, wg, wu, nf, chips, cid):
-    rows, d = slots.shape
-    hidden = wg.shape[1]
-    bands = 2 * chips // nf
-    return pl.pallas_call(
-        functools.partial(_up_kernel, nf, chips),
-        out_shape=jax.ShapeDtypeStruct((bands, rows, hidden), jnp.bfloat16),
-        in_specs=[pl.BlockSpec(memory_space=pltpu.VMEM)] * 3,
-        out_specs=pl.BlockSpec(memory_space=pltpu.VMEM),
-        scratch_shapes=[
-            pltpu.VMEM((2 * chips, rows, d), jnp.bfloat16),
-            pltpu.VMEM((nf, bands, rows, 2 * hidden), jnp.bfloat16),
-            pltpu.VMEM((nf, bands, rows, 2 * hidden), jnp.bfloat16),
-            pltpu.VMEM((bands, rows, 2 * hidden), jnp.float32),
-            pltpu.SemaphoreType.DMA((chips,)),
-            pltpu.SemaphoreType.DMA,
-            pltpu.SemaphoreType.DMA((chips,)),
-            pltpu.SemaphoreType.DMA((2 * chips,)),
-            pltpu.SemaphoreType.DMA((nf,)),
-            pltpu.SemaphoreType.DMA((nf,)),
-        ],
-        compiler_params=pltpu.CompilerParams(collective_id=cid, has_side_effects=True),
-    )(slots, wg, wu)
-
 def _layer_kernel(nf, chips, slot_ref, wg_ref, wu_ref, wd_ref, comb_ref, o_ref, *scratch):
     up_scratch, act_s, down_scratch, slot_out = scratch[:10], scratch[10], scratch[11:22], scratch[22]
     _up_kernel(nf, chips, slot_ref, wg_ref, wu_ref, act_s, *up_scratch)
-    _down_kernel(nf, chips, act_s, wd_ref, slot_out, *down_scratch, greet=False)
+    _down_kernel(nf, chips, act_s, wd_ref, slot_out, *down_scratch)
     o_ref[...] = jnp.dot(
         comb_ref[...], slot_out[...], precision=lax.Precision.HIGHEST,
         preferred_element_type=jnp.float32,
@@ -530,8 +334,8 @@
             pltpu.VMEM((chips, rows, d), jnp.bfloat16),
             pltpu.SemaphoreType.DMA((nf,)),
             pltpu.SemaphoreType.DMA((nf,)),
-            pltpu.SemaphoreType.DMA,
-            pltpu.SemaphoreType.DMA,
+            pltpu.SemaphoreType.DMA((chips,)),
+            pltpu.SemaphoreType.DMA((chips,)),
             pltpu.SemaphoreType.DMA((chips,)),
             pltpu.SemaphoreType.DMA((chips,)),
             pltpu.VMEM((rows, d), jnp.float32),

time: 190 us -> 178 us (0.937)
  the two profiles are of different devices: /device:TPU:1 before, /device:TPU:22 now
where the time goes in v13:
time: 178 us
  Pallas kernels  173 us (97%)
  local copies, waits for them, and re-layouts  3.05 us (2%)
    pallas_call x1, Pallas kernels, moe_layer(): pl.pallas_call(functools.partial(_layer_kernel, nf, chips), out_shape=jax...  173 us

profile of v13, /device:TPU:22, one launch (start us, length us, event | category | flops | bytes accessed | tf_op | source)
XLA Modules:
  0.0 178.0 jit_solution(7816501709140123684)
XLA Ops:
  0.0 0.0 copy-start
  0.0 0.0 copy-start.1
  0.0 0.7 copy-done.1
  0.8 0.2 convolution_reduce_fusion
  1.0 0.0 copy-start.2
  1.0 0.7 copy-done.2
  1.7 0.0 copy-done
  1.7 0.8 convolution_convert_fusion.slot_ref
  2.5 0.8 fusion.1.comb_ref
  3.3 173.0 %shard_map.64 = bf16[288,384]{1,0:T(8,128)(2,1)} custom-call(bf16[81,384]{1,0:T(8,128)(2,1)} %convolution_convert_fusion.slot_ref, bf16[384,256]{1,0:T(8,128)(2,1)} %bitcast.5, bf16[384,256]{1,0:T(8,128)(2,1)} %bitcast.6, bf16[256,384]{1,0:T(8,128)(2,1)} %bitcast.7, f32[288,81]{1,0:T(8,128)} %fusion.1.comb_ref), custom_call_target="tpu_custom_call" | custom-call | tf_op jit(solution)/shard_map/pallas_call | solution.py:313
  176.3 1.6 copy.8
  (4 shorter events, 0.1 us)
Async XLA Ops:
  0.0 1.7 copy-start
  0.0 0.7 copy-start.1
  1.0 0.7 copy-start.2

commit v14 on v13

--- a/solution.py
+++ b/solution.py
@@ -98,18 +98,25 @@
             device_id_type=MESH,
         )
 
+    shift = nf - lax.rem(chip, nf)
+
     def send_act(i, carry):
-        act_copy(fsdp_peer(i), f).start()
-        return carry
-
-    lax.fori_loop(0, nf - 1, send_act, 0)
+        g = lax.rem(f + shift + nf - i, nf)
+
+        @pl.when(g != f)
+        def _():
+            act_copy(g, f).start()
+
+        return carry
+
+    lax.fori_loop(0, nf, send_act, 0)
     act_buf[f] = act_ref[...]
     o_ref[...] = jnp.zeros_like(o_ref)
 
     def band(i, carry):
-        j = lax.rem(f + i, nf)
-
-        @pl.when(i > 0)
+        j = lax.rem(f + chip + i, nf)
+
+        @pl.when(j != f)
         def _():
             act_copy(j, f).wait_send()
             act_copy(j, j).wait_recv()

time: 178 us -> 175 us (0.983)
  the two profiles are of different devices: /device:TPU:22 before, /device:TPU:12 now
where the time goes in v14:
time: 175 us
  Pallas kernels  170 us (97%)
  local copies, waits for them, and re-layouts  3.05 us (2%)
    pallas_call x1, Pallas kernels, moe_layer(): pl.pallas_call(functools.partial(_layer_kernel, nf, chips), out_shape=jax...  170 us

profile of v14, /device:TPU:12, one launch (start us, length us, event | category | flops | bytes accessed | tf_op | source)
XLA Modules:
  0.0 174.8 jit_solution(9293042311924795258)
XLA Ops:
  0.0 0.0 copy-start
  0.0 0.0 copy-start.1
  0.0 0.7 copy-done.1
  0.8 0.2 convolution_reduce_fusion
  1.0 0.0 copy-start.2
  1.0 0.7 copy-done.2
  1.7 0.0 copy-done
  1.7 0.8 convolution_convert_fusion.slot_ref
  2.5 0.8 fusion.1.comb_ref
  3.3 169.8 %shard_map.64 = bf16[288,384]{1,0:T(8,128)(2,1)} custom-call(bf16[81,384]{1,0:T(8,128)(2,1)} %convolution_convert_fusion.slot_ref, bf16[384,256]{1,0:T(8,128)(2,1)} %bitcast.5, bf16[384,256]{1,0:T(8,128)(2,1)} %bitcast.6, bf16[256,384]{1,0:T(8,128)(2,1)} %bitcast.7, f32[288,81]{1,0:T(8,128)} %fusion.1.comb_ref), custom_call_target="tpu_custom_call" | custom-call | tf_op jit(solution)/shard_map/pallas_call | solution.py:320
  173.2 1.6 copy.8
  (4 shorter events, 0.1 us)
Async XLA Ops:
  0.0 1.7 copy-start
  0.0 0.7 copy-start.1
  1.0 0.7 copy-start.2

commit v15 on v14

--- a/solution.py
+++ b/solution.py
@@ -229,11 +229,18 @@
     pl.semaphore_signal(barrier, 1, device_id={"ed": sib}, device_id_type=MESH)
     pl.semaphore_wait(barrier, nf - 1 + chips)
 
-    def send_slots(i, carry):
-        direct(chip_peer(i)).start()
-        return carry
-
-    lax.fori_loop(0, chips - 1, send_slots, 0)
+    own_band = mine // bands
+    lift = chips * ((nf + 2 * chips) // chips)
+
+    def send_slots(k, carry):
+        h = lax.rem(own_band - f - 1 - k + lift, chips)
+
+        @pl.when(h != chip)
+        def _():
+            direct(h).start()
+
+        return carry
+
     to_sib = pltpu.make_async_remote_copy(
         src_ref=slot_ref,
         dst_ref=sel_buf.at[mine],
@@ -243,10 +250,11 @@
         device_id_type=MESH,
     )
     to_sib.start()
+    lax.fori_loop(0, chips, send_slots, 0)
     sel_buf[mine] = slot_ref[...]
 
     def band(i, carry):
-        j = lax.rem(f + 1 + i, nf)
+        j = lax.rem(f + chip + 1 + i, nf)
         for t in range(bands):
             blk = j * bands + t
             same_core = (blk // chips) == core
@@ -280,14 +288,20 @@
     lax.fori_loop(0, nf, band, 0)
     acc[...] = out_buf[f].astype(jnp.float32)
 
+    lift_f = nf * ((chips + 2 * nf) // nf)
+
     def gather(i, carry):
-        g = fsdp_peer(i)
-        partial_copy(g, f).wait_send()
-        partial_copy(g, g).wait_recv()
-        acc[...] += in_buf[g].astype(jnp.float32)
-        return carry
-
-    lax.fori_loop(0, nf - 1, gather, 0)
+        g = lax.rem(f - chip - 1 - i + lift_f, nf)
+
+        @pl.when(g != f)
+        def _():
+            partial_copy(g, f).wait_send()
+            partial_copy(g, g).wait_recv()
+            acc[...] += in_buf[g].astype(jnp.float32)
+
+        return carry
+
+    lax.fori_loop(0, nf, gather, 0)
 
     def drain(i, carry):
         h = chip_peer(i)

time: 175 us -> 166 us (0.949)
  the two profiles are of different devices: /device:TPU:12 before, /device:TPU:1 now
where the time goes in v15:
time: 166 us
  Pallas kernels  161 us (97%)
  local copies, waits for them, and re-layouts  3.05 us (2%)
    pallas_call x1, Pallas kernels, moe_layer(): pl.pallas_call(functools.partial(_layer_kernel, nf, chips), out_shape=jax...  161 us

profile of v15, /device:TPU:1, one launch (start us, length us, event | category | flops | bytes accessed | tf_op | source)
XLA Modules:
  0.0 166.1 jit_solution(14384345632115654735)
XLA Ops:
  0.0 0.0 copy-start
  0.0 0.0 copy-start.1
  0.0 0.7 copy-done.1
  0.8 0.2 convolution_reduce_fusion
  1.0 0.0 copy-start.2
  1.0 0.7 copy-done.2
  1.7 0.0 copy-done
  1.7 0.8 convolution_convert_fusion.slot_ref
  2.5 0.8 fusion.1.comb_ref
  3.3 161.1 %shard_map.64 = bf16[288,384]{1,0:T(8,128)(2,1)} custom-call(bf16[81,384]{1,0:T(8,128)(2,1)} %convolution_convert_fusion.slot_ref, bf16[384,256]{1,0:T(8,128)(2,1)} %bitcast.5, bf16[384,256]{1,0:T(8,128)(2,1)} %bitcast.6, bf16[256,384]{1,0:T(8,128)(2,1)} %bitcast.7, f32[288,81]{1,0:T(8,128)} %fusion.1.comb_ref), custom_call_target="tpu_custom_call" | custom-call | tf_op jit(solution)/shard_map/pallas_call | solution.py:334
  164.4 1.6 copy.8
  (4 shorter events, 0.1 us)
Async XLA Ops:
  0.0 1.7 %copy-start = (bf16[288,384]{1,0:T(8,128)(2,1)S(1)}, bf16[288,384]{1,0:T(8,128)(2,1)}, u32[]{:S(2)}) copy-start(bf16[288,384]{1,0:T(8,128)(2,1)} %param.6) | copy-start | bytes 663556
  0.0 0.7 copy-start.1
  1.0 0.7 copy-start.2

commit v16 on v15

--- a/solution.py
+++ b/solution.py
@@ -151,14 +151,21 @@
 
     lax.fori_loop(0, nf, band, 0)
 
+    own_band = (core * chips + chip) // bands
+    lift = chips * ((nf + 2 * chips) // chips)
+
     def take_piece(i, carry):
-        h = chip_peer(i)
-        piece_copy(h, chip).wait_send()
-        piece_copy(h, h).wait_recv()
-        o_ref[...] += in_buf[h].astype(jnp.float32)
-        return carry
-
-    lax.fori_loop(0, chips - 1, take_piece, 0)
+        h = lax.rem(own_band - f - i + lift, chips)
+
+        @pl.when(h != chip)
+        def _():
+            piece_copy(h, chip).wait_send()
+            piece_copy(h, h).wait_recv()
+            o_ref[...] += in_buf[h].astype(jnp.float32)
+
+        return carry
+
+    lax.fori_loop(0, chips, take_piece, 0)
 
     def drain(h, carry):
         to_sibling((1 - core) * chips + h).wait_send()

time: 166 us -> 167 us (level)
  no operation moved by 1% of the time
where the time goes in v16:
time: 167 us
  Pallas kernels  162 us (97%)
  local copies, waits for them, and re-layouts  3.05 us (2%)
    pallas_call x1, Pallas kernels, moe_layer(): pl.pallas_call(functools.partial(_layer_kernel, nf, chips), out_shape=jax...  162 us

profile of v16, /device:TPU:1, one launch (start us, length us, event | category | flops | bytes accessed | tf_op | source)
XLA Modules:
  0.0 166.5 jit_solution(10255277093389172037)
XLA Ops:
  0.0 0.0 copy-start
  0.0 0.0 copy-start.1
  0.0 0.7 copy-done.1
  0.8 0.2 convolution_reduce_fusion
  1.0 0.0 copy-start.2
  1.0 0.7 copy-done.2
  1.7 0.0 copy-done
  1.7 0.8 convolution_convert_fusion.slot_ref
  2.5 0.8 fusion.1.comb_ref
  3.3 161.5 %shard_map.64 = bf16[288,384]{1,0:T(8,128)(2,1)} custom-call(bf16[81,384]{1,0:T(8,128)(2,1)} %convolution_convert_fusion.slot_ref, bf16[384,256]{1,0:T(8,128)(2,1)} %bitcast.5, bf16[384,256]{1,0:T(8,128)(2,1)} %bitcast.6, bf16[256,384]{1,0:T(8,128)(2,1)} %bitcast.7, f32[288,81]{1,0:T(8,128)} %fusion.1.comb_ref), custom_call_target="tpu_custom_call" | custom-call | tf_op jit(solution)/shard_map/pallas_call | solution.py:341
  164.9 1.6 copy.8
  (4 shorter events, 0.1 us)
Async XLA Ops:
  0.0 1.7 %copy-start = (bf16[288,384]{1,0:T(8,128)(2,1)S(1)}, bf16[288,384]{1,0:T(8,128)(2,1)}, u32[]{:S(2)}) copy-start(bf16[288,384]{1,0:T(8,128)(2,1)} %param.6) | copy-start | bytes 663556
  0.0 0.7 copy-start.1
  1.0 0.7 copy-start.2

commit v17 on v15

--- a/solution.py
+++ b/solution.py
@@ -315,27 +315,39 @@
     o_ref[...] = (jax.nn.silu(total[..., :hidden]) * total[..., hidden:]).astype(o_ref.dtype)
 
 
-def _layer_kernel(nf, chips, slot_ref, wg_ref, wu_ref, wd_ref, comb_ref, o_ref, *scratch):
+def _layer_kernel(nf, chips, tok_ref, match_ref, wg_ref, wu_ref, wd_hbm, comb_hbm, o_ref, *scratch):
     up_scratch, act_s, down_scratch, slot_out = scratch[:10], scratch[10], scratch[11:22], scratch[22]
-    _up_kernel(nf, chips, slot_ref, wg_ref, wu_ref, act_s, *up_scratch)
-    _down_kernel(nf, chips, act_s, wd_ref, slot_out, *down_scratch)
+    slot_s, wd_v, comb_v, local_sem = scratch[23:]
+    wd_copy = pltpu.make_async_copy(wd_hbm, wd_v, local_sem.at[0])
+    comb_copy = pltpu.make_async_copy(comb_hbm, comb_v, local_sem.at[1])
+    wd_copy.start()
+    comb_copy.start()
+    slot_s[...] = jnp.dot(
+        match_ref[...], tok_ref[...], preferred_element_type=jnp.float32
+    ).astype(slot_s.dtype)
+    _up_kernel(nf, chips, slot_s, wg_ref, wu_ref, act_s, *up_scratch)
+    wd_copy.wait()
+    _down_kernel(nf, chips, act_s, wd_v, slot_out, *down_scratch)
+    comb_copy.wait()
     o_ref[...] = jnp.dot(
-        comb_ref[...], slot_out[...], precision=lax.Precision.HIGHEST,
+        comb_v[...], slot_out[...], precision=lax.Precision.HIGHEST,
         preferred_element_type=jnp.float32,
     ).astype(o_ref.dtype)
 
 
-def moe_layer(slots, wg, wu, wd, comb, nf, chips, cid):
-    rows, d = slots.shape
+def moe_layer(tokens, match, wg, wu, wd, comb, nf, chips, cid):
+    rows, tok = match.shape
+    d = tokens.shape[1]
     hidden = wg.shape[1]
     bands = 2 * chips // nf
     blocks = nf * bands
-    tok = comb.shape[0]
+    vmem = pl.BlockSpec(memory_space=pltpu.VMEM)
+    anywhere = pl.BlockSpec(memory_space=pl.ANY)
     return pl.pallas_call(
         functools.partial(_layer_kernel, nf, chips),
         out_shape=jax.ShapeDtypeStruct((tok, d), jnp.bfloat16),
-        in_specs=[pl.BlockSpec(memory_space=pltpu.VMEM)] * 5,
-        out_specs=pl.BlockSpec(memory_space=pltpu.VMEM),
+        in_specs=[vmem, vmem, vmem, vmem, anywhere, anywhere],
+        out_specs=vmem,
         scratch_shapes=[
             pltpu.VMEM((2 * chips, rows, d), jnp.bfloat16),
             pltpu.VMEM((nf, bands, rows, 2 * hidden), jnp.bfloat16),
@@ -360,9 +372,13 @@
             pltpu.SemaphoreType.DMA((chips,)),
             pltpu.SemaphoreType.DMA((chips,)),
             pltpu.VMEM((rows, d), jnp.float32),
+            pltpu.VMEM((rows, d), jnp.bfloat16),
+            pltpu.VMEM((hidden, d), jnp.bfloat16),
+            pltpu.VMEM((tok, rows), jnp.float32),
+            pltpu.SemaphoreType.DMA((2,)),
         ],
         compiler_params=pltpu.CompilerParams(collective_id=cid, has_side_effects=True),
-    )(slots, wg, wu, wd, comb)
+    )(tokens, match, wg, wu, wd, comb)
 
 
 def local(tokens, expert_ids, route_weights, w_gate, w_up, w_down):
@@ -380,14 +396,14 @@
     count = jnp.dot(lower, routed.astype(jnp.bfloat16), preferred_element_type=jnp.float32)
     slot_ids = jnp.arange(CAP, dtype=jnp.float32)
     match = routed[None, :] & (count[None, :] - 1.0 == slot_ids[:, None])
-    own_slots = jnp.dot(
-        match.astype(jnp.bfloat16), tokens, preferred_element_type=jnp.float32
-    ).astype(jnp.bfloat16)
     per_expert = jnp.sum(
         jnp.where(expert_ids == 0, route_weights, jnp.zeros_like(route_weights)), axis=1
     )
     weights_matrix = match.T.astype(jnp.float32) * per_expert[:, None]
-    return moe_layer(own_slots, w_gate[0], w_up[0], w_down[0], weights_matrix, n_fsdp, chips, 2)
+    return moe_layer(
+        tokens, match.astype(jnp.bfloat16), w_gate[0], w_up[0], w_down[0], weights_matrix,
+        n_fsdp, chips, 2,
+    )
 
 
 def solution(mesh):

time: 166 us -> 168 us (1.012)
  the two profiles are of different devices: /device:TPU:1 before, /device:TPU:55 now
where the time goes in v17:
time: 168 us
  Pallas kernels  163 us (97%)
  local copies, waits for them, and re-layouts  3.01 us (2%)
    pallas_call x1, Pallas kernels, moe_layer(): pl.pallas_call(functools.partial(_layer_kernel, nf, chips), out_shape=jax...  163 us

profile of v17, /device:TPU:55, one launch (start us, length us, event | category | flops | bytes accessed | tf_op | source)
XLA Modules:
  0.0 167.7 jit_solution(15869968888126819798)
XLA Ops:
  0.0 0.0 copy-start
  0.0 0.7 copy-done
  0.7 0.2 convolution_reduce_fusion
  0.9 0.0 copy-start.1
  0.9 0.7 copy-done.1
  1.6 0.7 fusion.3.match_ref
  2.3 0.8 fusion.1.comb_hbm
  3.1 162.9 %shard_map.64 = bf16[288,384]{1,0:T(8,128)(2,1)} custom-call(bf16[288,384]{1,0:T(8,128)(2,1)} %tok_ref.1, bf16[81,288]{1,0:T(8,128)(2,1)} %fusion.3.match_ref, bf16[384,256]{1,0:T(8,128)(2,1)} %bitcast.4, bf16[384,256]{1,0:T(8,128)(2,1)} %bitcast.5, bf16[256,384]{1,0:T(8,128)(2,1)} %bitcast.6, f32[288,81]{1,0:T(8,128)} %fusion.1.comb_hbm), custom_call_target="tpu_custom_call" | custom-call | tf_op jit(solution)/shard_map/pallas_call | solution.py:346
  166.0 1.6 copy.8
  (4 shorter events, 0.1 us)
Async XLA Ops:
  0.0 0.7 copy-start
  0.9 0.7 copy-start.1

commit v18 on v15

--- a/solution.py
+++ b/solution.py
@@ -118,7 +118,6 @@
 
         @pl.when(j != f)
         def _():
-            act_copy(j, f).wait_send()
             act_copy(j, j).wait_recv()
 
         for t in range(bands):
@@ -165,6 +164,12 @@
         return carry
 
     lax.fori_loop(0, chips, drain, 0)
+
+    def drain_act(i, carry):
+        act_copy(fsdp_peer(i), f).wait_send()
+        return carry
+
+    lax.fori_loop(0, nf - 1, drain_act, 0)
 
 
 def _up_kernel(nf, chips, slot_ref, wg_ref, wu_ref, o_ref, sel_buf, out_buf, in_buf, acc,
@@ -295,7 +300,6 @@
 
         @pl.when(g != f)
         def _():
-            partial_copy(g, f).wait_send()
             partial_copy(g, g).wait_recv()
             acc[...] += in_buf[g].astype(jnp.float32)
 
@@ -310,6 +314,12 @@
         return carry
 
     lax.fori_loop(0, chips - 1, drain, 0)
+
+    def drain_partial(i, carry):
+        partial_copy(fsdp_peer(i), f).wait_send()
+        return carry
+
+    lax.fori_loop(0, nf - 1, drain_partial, 0)
     to_sib.wait_send()
     total = acc[...]
     o_ref[...] = (jax.nn.silu(total[..., :hidden]) * total[..., hidden:]).astype(o_ref.dtype)

time: 166 us -> 164 us (0.988)
  the two profiles are of different devices: /device:TPU:1 before, /device:TPU:4 now
where the time goes in v18:
time: 164 us
  Pallas kernels  159 us (97%)
  local copies, waits for them, and re-layouts  3.05 us (2%)
    pallas_call x1, Pallas kernels, moe_layer(): pl.pallas_call(functools.partial(_layer_kernel, nf, chips), out_shape=jax...  159 us

profile of v18, /device:TPU:4, one launch (start us, length us, event | category | flops | bytes accessed | tf_op | source)
XLA Modules:
  0.0 163.7 jit_solution(6349462442997448689)
XLA Ops:
  0.0 0.0 copy-start
  0.0 0.0 copy-start.1
  0.0 0.7 copy-done.1
  0.8 0.2 convolution_reduce_fusion
  1.0 0.0 copy-start.2
  1.0 0.7 copy-done.2
  1.7 0.0 copy-done
  1.7 0.8 convolution_convert_fusion.slot_ref
  2.5 0.8 fusion.1.comb_ref
  3.3 158.7 %shard_map.64 = bf16[288,384]{1,0:T(8,128)(2,1)} custom-call(bf16[81,384]{1,0:T(8,128)(2,1)} %convolution_convert_fusion.slot_ref, bf16[384,256]{1,0:T(8,128)(2,1)} %bitcast.5, bf16[384,256]{1,0:T(8,128)(2,1)} %bitcast.6, bf16[256,384]{1,0:T(8,128)(2,1)} %bitcast.7, f32[288,81]{1,0:T(8,128)} %fusion.1.comb_ref), custom_call_target="tpu_custom_call" | custom-call | tf_op jit(solution)/shard_map/pallas_call | solution.py:344
  162.1 1.6 %copy.8 = bf16[288,384]{1,0:T(8,128)(2,1)} copy(bf16[288,384]{1,0:T(8,128)(2,1)} %shard_map.64) | data formatting | bytes 442368
  (4 shorter events, 0.1 us)
Async XLA Ops:
  0.0 1.7 %copy-start = (bf16[288,384]{1,0:T(8,128)(2,1)S(1)}, bf16[288,384]{1,0:T(8,128)(2,1)}, u32[]{:S(2)}) copy-start(bf16[288,384]{1,0:T(8,128)(2,1)} %param.6) | copy-start | bytes 663556
  0.0 0.7 copy-start.1
  1.0 0.7 copy-start.2

commit v19 on v18

--- a/solution.py
+++ b/solution.py
@@ -152,12 +152,17 @@
 
     def take_piece(i, carry):
         h = chip_peer(i)
-        piece_copy(h, chip).wait_send()
         piece_copy(h, h).wait_recv()
         o_ref[...] += in_buf[h].astype(jnp.float32)
         return carry
 
     lax.fori_loop(0, chips - 1, take_piece, 0)
+
+    def drain_piece(i, carry):
+        piece_copy(chip_peer(i), chip).wait_send()
+        return carry
+
+    lax.fori_loop(0, chips - 1, drain_piece, 0)
 
     def drain(h, carry):
         to_sibling((1 - core) * chips + h).wait_send()
@@ -313,22 +318,26 @@
         forward(core * chips + h).wait_send()
         return carry
 
-    lax.fori_loop(0, chips - 1, drain, 0)
-
     def drain_partial(i, carry):
         partial_copy(fsdp_peer(i), f).wait_send()
         return carry
 
-    lax.fori_loop(0, nf - 1, drain_partial, 0)
-    to_sib.wait_send()
     total = acc[...]
     o_ref[...] = (jax.nn.silu(total[..., :hidden]) * total[..., hidden:]).astype(o_ref.dtype)
 
+    def finish():
+        lax.fori_loop(0, chips - 1, drain, 0)
+        lax.fori_loop(0, nf - 1, drain_partial, 0)
+        to_sib.wait_send()
+
+    return finish
+
 
 def _layer_kernel(nf, chips, slot_ref, wg_ref, wu_ref, wd_ref, comb_ref, o_ref, *scratch):
     up_scratch, act_s, down_scratch, slot_out = scratch[:10], scratch[10], scratch[11:22], scratch[22]
-    _up_kernel(nf, chips, slot_ref, wg_ref, wu_ref, act_s, *up_scratch)
+    finish_up = _up_kernel(nf, chips, slot_ref, wg_ref, wu_ref, act_s, *up_scratch)
     _down_kernel(nf, chips, act_s, wd_ref, slot_out, *down_scratch)
+    finish_up()
     o_ref[...] = jnp.dot(
         comb_ref[...], slot_out[...], precision=lax.Precision.HIGHEST,
         preferred_element_type=jnp.float32,

time: 164 us -> 164 us (level)
  no operation moved by 1% of the time
where the time goes in v19:
time: 164 us
  Pallas kernels  159 us (97%)
  local copies, waits for them, and re-layouts  3.05 us (2%)
    pallas_call x1, Pallas kernels, moe_layer(): pl.pallas_call(functools.partial(_layer_kernel, nf, chips), out_shape=jax...  159 us

profile of v19, /device:TPU:4, one launch (start us, length us, event | category | flops | bytes accessed | tf_op | source)
XLA Modules:
  0.0 163.9 jit_solution(4177165116448902616)
XLA Ops:
  0.0 0.0 copy-start
  0.0 0.0 copy-start.1
  0.0 0.7 copy-done.1
  0.8 0.2 convolution_reduce_fusion
  1.0 0.0 copy-start.2
  1.0 0.7 copy-done.2
  1.7 0.0 copy-done
  1.7 0.8 convolution_convert_fusion.slot_ref
  2.5 0.8 fusion.1.comb_ref
  3.3 158.9 %shard_map.64 = bf16[288,384]{1,0:T(8,128)(2,1)} custom-call(bf16[81,384]{1,0:T(8,128)(2,1)} %convolution_convert_fusion.slot_ref, bf16[384,256]{1,0:T(8,128)(2,1)} %bitcast.5, bf16[384,256]{1,0:T(8,128)(2,1)} %bitcast.6, bf16[256,384]{1,0:T(8,128)(2,1)} %bitcast.7, f32[288,81]{1,0:T(8,128)} %fusion.1.comb_ref), custom_call_target="tpu_custom_call" | custom-call | tf_op jit(solution)/shard_map/pallas_call | solution.py:353
  162.2 1.6 %copy.8 = bf16[288,384]{1,0:T(8,128)(2,1)} copy(bf16[288,384]{1,0:T(8,128)(2,1)} %shard_map.64) | data formatting | bytes 442368
  (4 shorter events, 0.1 us)
Async XLA Ops:
  0.0 1.7 %copy-start = (bf16[288,384]{1,0:T(8,128)(2,1)S(1)}, bf16[288,384]{1,0:T(8,128)(2,1)}, u32[]{:S(2)}) copy-start(bf16[288,384]{1,0:T(8,128)(2,1)} %param.6) | copy-start | bytes 663556
  0.0 0.7 copy-start.1
  1.0 0.7 copy-start.2

commit v20 on v18

--- a/solution.py
+++ b/solution.py
@@ -113,26 +113,12 @@
     act_buf[f] = act_ref[...]
     o_ref[...] = jnp.zeros_like(o_ref)
 
-    def band(i, carry):
-        j = lax.rem(f + chip + i, nf)
-
-        @pl.when(j != f)
-        def _():
-            act_copy(j, j).wait_recv()
-
+    def settle(j):
         for t in range(bands):
             blk = j * bands + t
             h = lax.rem(blk, chips)
-            term_buf[blk] = jnp.dot(
-                act_buf[j, t], wd_ref[...], preferred_element_type=jnp.float32
-            ).astype(term_buf.dtype)
-            same_core = (blk // chips) == core
-
-            @pl.when(jnp.logical_not(same_core))
-            def _():
-                to_sibling(blk).start()
-
-            @pl.when(same_core)
+
+            @pl.when((blk // chips) == core)
             def _():
                 to_sibling(blk).wait_recv()
                 pair = term_buf[blk].astype(jnp.float32) + sib_buf[h].astype(jnp.float32)
@@ -146,9 +132,31 @@
                 def _():
                     piece_copy(h, chip).start()
 
+    def band(i, carry):
+        j = lax.rem(f + chip + i, nf)
+
+        @pl.when(j != f)
+        def _():
+            act_copy(j, j).wait_recv()
+
+        for t in range(bands):
+            blk = j * bands + t
+            term_buf[blk] = jnp.dot(
+                act_buf[j, t], wd_ref[...], preferred_element_type=jnp.float32
+            ).astype(term_buf.dtype)
+
+            @pl.when((blk // chips) != core)
+            def _():
+                to_sibling(blk).start()
+
+        @pl.when(i > 0)
+        def _():
+            settle(lax.rem(f + chip + i - 1, nf))
+
         return carry
 
     lax.fori_loop(0, nf, band, 0)
+    settle(lax.rem(f + chip + nf - 1, nf))
 
     def take_piece(i, carry):
         h = chip_peer(i)

time: 164 us -> 165 us (level)
  no operation moved by 1% of the time
where the time goes in v20:
time: 165 us
  Pallas kernels  160 us (97%)
  local copies, waits for them, and re-layouts  3.05 us (2%)
    pallas_call x1, Pallas kernels, moe_layer(): pl.pallas_call(functools.partial(_layer_kernel, nf, chips), out_shape=jax...  160 us

profile of v20, /device:TPU:4, one launch (start us, length us, event | category | flops | bytes accessed | tf_op | source)
XLA Modules:
  0.0 164.8 jit_solution(9973966426861084668)
XLA Ops:
  0.0 0.0 copy-start
  0.0 0.0 copy-start.1
  0.0 0.7 copy-done.1
  0.8 0.2 convolution_reduce_fusion
  1.0 0.0 copy-start.2
  1.0 0.7 copy-done.2
  1.7 0.0 copy-done
  1.7 0.8 convolution_convert_fusion.slot_ref
  2.5 0.8 fusion.1.comb_ref
  3.3 159.8 %shard_map.64 = bf16[288,384]{1,0:T(8,128)(2,1)} custom-call(bf16[81,384]{1,0:T(8,128)(2,1)} %convolution_convert_fusion.slot_ref, bf16[384,256]{1,0:T(8,128)(2,1)} %bitcast.5, bf16[384,256]{1,0:T(8,128)(2,1)} %bitcast.6, bf16[256,384]{1,0:T(8,128)(2,1)} %bitcast.7, f32[288,81]{1,0:T(8,128)} %fusion.1.comb_ref), custom_call_target="tpu_custom_call" | custom-call | tf_op jit(solution)/shard_map/pallas_call | solution.py:352
  163.2 1.6 copy.8
  (4 shorter events, 0.1 us)
Async XLA Ops:
  0.0 1.7 %copy-start = (bf16[288,384]{1,0:T(8,128)(2,1)S(1)}, bf16[288,384]{1,0:T(8,128)(2,1)}, u32[]{:S(2)}) copy-start(bf16[288,384]{1,0:T(8,128)(2,1)} %param.6) | copy-start | bytes 663556
  0.0 0.7 copy-start.1
  1.0 0.7 copy-start.2

commit v21 on v18

--- a/solution.py
+++ b/solution.py
@@ -325,26 +325,21 @@
     o_ref[...] = (jax.nn.silu(total[..., :hidden]) * total[..., hidden:]).astype(o_ref.dtype)
 
 
-def _layer_kernel(nf, chips, slot_ref, wg_ref, wu_ref, wd_ref, comb_ref, o_ref, *scratch):
-    up_scratch, act_s, down_scratch, slot_out = scratch[:10], scratch[10], scratch[11:22], scratch[22]
+def _layer_kernel(nf, chips, slot_ref, wg_ref, wu_ref, wd_ref, o_ref, *scratch):
+    up_scratch, act_s, down_scratch = scratch[:10], scratch[10], scratch[11:22]
     _up_kernel(nf, chips, slot_ref, wg_ref, wu_ref, act_s, *up_scratch)
-    _down_kernel(nf, chips, act_s, wd_ref, slot_out, *down_scratch)
-    o_ref[...] = jnp.dot(
-        comb_ref[...], slot_out[...], precision=lax.Precision.HIGHEST,
-        preferred_element_type=jnp.float32,
-    ).astype(o_ref.dtype)
-
-
-def moe_layer(slots, wg, wu, wd, comb, nf, chips, cid):
+    _down_kernel(nf, chips, act_s, wd_ref, o_ref, *down_scratch)
+
+
+def moe_layer(slots, wg, wu, wd, nf, chips, cid):
     rows, d = slots.shape
     hidden = wg.shape[1]
     bands = 2 * chips // nf
     blocks = nf * bands
-    tok = comb.shape[0]
     return pl.pallas_call(
         functools.partial(_layer_kernel, nf, chips),
-        out_shape=jax.ShapeDtypeStruct((tok, d), jnp.bfloat16),
-        in_specs=[pl.BlockSpec(memory_space=pltpu.VMEM)] * 5,
+        out_shape=jax.ShapeDtypeStruct((rows, d), jnp.float32),
+        in_specs=[pl.BlockSpec(memory_space=pltpu.VMEM)] * 4,
         out_specs=pl.BlockSpec(memory_space=pltpu.VMEM),
         scratch_shapes=[
             pltpu.VMEM((2 * chips, rows, d), jnp.bfloat16),
@@ -369,10 +364,9 @@
             pltpu.SemaphoreType.DMA((chips,)),
             pltpu.SemaphoreType.DMA((chips,)),
             pltpu.SemaphoreType.DMA((chips,)),
-            pltpu.VMEM((rows, d), jnp.float32),
         ],
         compiler_params=pltpu.CompilerParams(collective_id=cid, has_side_effects=True),
-    )(slots, wg, wu, wd, comb)
+    )(slots, wg, wu, wd)
 
 
 def local(tokens, expert_ids, route_weights, w_gate, w_up, w_down):
@@ -397,7 +391,12 @@
         jnp.where(expert_ids == 0, route_weights, jnp.zeros_like(route_weights)), axis=1
     )
     weights_matrix = match.T.astype(jnp.float32) * per_expert[:, None]
-    return moe_layer(own_slots, w_gate[0], w_up[0], w_down[0], weights_matrix, n_fsdp, chips, 2)
+    slot_out = moe_layer(own_slots, w_gate[0], w_up[0], w_down[0], n_fsdp, chips, 2)
+    mixed = jnp.dot(
+        weights_matrix, slot_out, precision=lax.Precision.HIGHEST,
+        preferred_element_type=jnp.float32,
+    )
+    return mixed.astype(jnp.bfloat16)
 
 
 def solution(mesh):

time: 164 us -> 163 us (level)
  matrix products: 1.02 us -> 3.23 us
    dot_general x0 -> x1, matrix products: none -> 2.21 us  [local(): jnp.dot(weights_matrix, slot_out, precision=lax.Precision.HIGHEST, prefer...]
    unnamed x7 -> x6, local copies, waits for them, and re-layouts: 3.04 us -> 1.4 us
where the time goes in v21:
time: 163 us
  Pallas kernels  158 us (97%)
  matrix products  3.23 us (2%)
    pallas_call x1, Pallas kernels, moe_layer(): pl.pallas_call(functools.partial(_layer_kernel, nf, chips), out_shape=jax...  158 us

profile of v21, /device:TPU:4, one launch (start us, length us, event | category | flops | bytes accessed | tf_op | source)
XLA Modules:
  0.0 162.9 jit_solution(6437284255513738137)
XLA Ops:
  0.0 0.0 copy-start
  0.0 0.0 copy-start.1
  0.0 0.7 copy-done.1
  0.8 0.2 convolution_reduce_fusion
  1.0 0.0 copy-start.2
  1.0 0.7 copy-done.2
  1.7 0.0 copy-done
  1.7 0.8 convolution_convert_fusion.1.slot_ref
  2.5 158.2 %shard_map.64 = f32[81,384]{1,0:T(8,128)} custom-call(bf16[81,384]{1,0:T(8,128)(2,1)} %convolution_convert_fusion.1.slot_ref, bf16[384,256]{1,0:T(8,128)(2,1)} %bitcast.6, bf16[384,256]{1,0:T(8,128)(2,1)} %bitcast.7, bf16[256,384]{1,0:T(8,128)(2,1)} %bitcast.8), custom_call_target="tpu_custom_call" | custom-call | tf_op jit(solution)/shard_map/pallas_call | solution.py:339
  160.7 2.2 %convolution_convert_fusion = bf16[288,384]{1,0:T(8,128)(2,1)} fusion(f32[81,384]{1,0:T(8,128)} %shard_map.64, f32[288]{0:T(512)S(1)} %select_reduce_fusion, f32[288]{0:T(512)S(1)} %broadcast_add_fusion, pred[288]{0:T(512)(128)(4,1)S(1)} %fusion.11), kind=kOutput, calls=%fused_computation | convolution fusion | flops 107676000 | bytes 348192 | tf_op jit(solution)/shard_map/dot_general | solution.py:395
  (4 shorter events, 0.1 us)
Async XLA Ops:
  0.0 1.7 %copy-start = (bf16[288,384]{1,0:T(8,128)(2,1)S(1)}, bf16[288,384]{1,0:T(8,128)(2,1)}, u32[]{:S(2)}) copy-start(bf16[288,384]{1,0:T(8,128)(2,1)} %param.6) | copy-start | bytes 663556
  0.0 0.7 copy-start.1
  1.0 0.7 copy-start.2

commit v22 on v21

--- a/solution.py
+++ b/solution.py
@@ -390,12 +390,10 @@
     per_expert = jnp.sum(
         jnp.where(expert_ids == 0, route_weights, jnp.zeros_like(route_weights)), axis=1
     )
-    weights_matrix = match.T.astype(jnp.float32) * per_expert[:, None]
     slot_out = moe_layer(own_slots, w_gate[0], w_up[0], w_down[0], n_fsdp, chips, 2)
-    mixed = jnp.dot(
-        weights_matrix, slot_out, precision=lax.Precision.HIGHEST,
-        preferred_element_type=jnp.float32,
-    )
+    slot_of = jnp.clip(count - 1.0, 0.0, CAP - 1.0).astype(jnp.int32)
+    rows = jnp.take(slot_out, slot_of, axis=0)
+    mixed = jnp.where(routed[:, None], per_expert[:, None] * rows, jnp.zeros_like(rows))
     return mixed.astype(jnp.bfloat16)
 
 

time: 163 us -> 165 us (1.012)
  local copies, waits for them, and re-layouts: 1.41 us -> 4.2 us
  matrix products: 3.23 us -> 1.02 us
    gather x0 -> x1, local copies, waits for them, and re-layouts: none -> 2.8 us  [local(): rows = jnp.take(slot_out, slot_of, axis=0)]
    dot_general x1 -> x0, matrix products: 2.21 us -> none  [local(): jnp.dot(weights_matrix, slot_out, precision=lax.Precision.HIGHEST, prefer...]
where the time goes in v22:
time: 165 us; the launch traced here: 164 us
  Pallas kernels  158 us (96%)
  local copies, waits for them, and re-layouts  4.2 us (3%)
    pallas_call x1, Pallas kernels, moe_layer(): pl.pallas_call(functools.partial(_layer_kernel, nf, chips), out_shape=jax...  158 us

profile of v22, /device:TPU:4, one launch (start us, length us, event | category | flops | bytes accessed | tf_op | source)
XLA Modules:
  0.0 164.3 jit_solution(9380827615588068429)
XLA Ops:
  0.0 0.0 copy-start
  0.0 0.0 copy-start.1
  0.0 0.7 copy-done.1
  0.8 0.2 convolution_reduce_fusion
  1.0 0.0 copy-start.2
  1.0 0.7 copy-done.2
  1.7 0.0 copy-done
  1.7 0.8 convolution_convert_fusion.slot_ref
  2.5 158.1 %shard_map.64 = f32[81,384]{1,0:T(8,128)} custom-call(bf16[81,384]{1,0:T(8,128)(2,1)} %convolution_convert_fusion.slot_ref, bf16[384,256]{1,0:T(8,128)(2,1)} %bitcast.5, bf16[384,256]{1,0:T(8,128)(2,1)} %bitcast.6, bf16[256,384]{1,0:T(8,128)(2,1)} %bitcast.7), custom_call_target="tpu_custom_call" | custom-call | tf_op jit(solution)/shard_map/pallas_call | solution.py:339
  160.6 2.8 %gather_fusion = f32[288,384]{1,0:T(8,128)S(1)} fusion(f32[81,384]{1,0:T(8,128)} %shard_map.64, s32[1024]{0:T(1024)S(1)} %pad_clamp_fusion), kind=kCustom, calls=%fused_computation | custom fusion | bytes 885888 | tf_op jit(solution)/shard_map/jit(_take)/gather | solution.py:395
  163.4 0.9 select_convert_fusion
  (7 shorter events, 0.1 us)
Async XLA Ops:
  0.0 1.7 %copy-start = (bf16[288,384]{1,0:T(8,128)(2,1)S(1)}, bf16[288,384]{1,0:T(8,128)(2,1)}, u32[]{:S(2)}) copy-start(bf16[288,384]{1,0:T(8,128)(2,1)} %param.6) | copy-start | bytes 663556
  0.0 0.7 copy-start.1
  1.0 0.7 copy-start.2

commit v23 on v21

--- a/solution.py
+++ b/solution.py
@@ -173,7 +173,7 @@
 
 
 def _up_kernel(nf, chips, slot_ref, wg_ref, wu_ref, o_ref, sel_buf, out_buf, in_buf, acc,
-               e_send, s_send, fwd_send, sel_recv, f_send, f_recv):
+               e_send, s_send, fwd_send, sel_recv, f_send, f_recv, weights=()):
     bands = o_ref.shape[0]
     hidden = o_ref.shape[2]
     f = lax.axis_index("fsdp")
@@ -257,6 +257,8 @@
     to_sib.start()
     lax.fori_loop(0, chips, send_slots, 0)
     sel_buf[mine] = slot_ref[...]
+    for c in weights:
+        c.wait()
 
     def band(i, carry):
         j = lax.rem(f + chip + 1 + i, nf)
@@ -325,10 +327,18 @@
     o_ref[...] = (jax.nn.silu(total[..., :hidden]) * total[..., hidden:]).astype(o_ref.dtype)
 
 
-def _layer_kernel(nf, chips, slot_ref, wg_ref, wu_ref, wd_ref, o_ref, *scratch):
+def _layer_kernel(nf, chips, slot_ref, wg_hbm, wu_hbm, wd_hbm, o_ref, *scratch):
     up_scratch, act_s, down_scratch = scratch[:10], scratch[10], scratch[11:22]
-    _up_kernel(nf, chips, slot_ref, wg_ref, wu_ref, act_s, *up_scratch)
-    _down_kernel(nf, chips, act_s, wd_ref, o_ref, *down_scratch)
+    wg_v, wu_v, wd_v, local_sem = scratch[22:]
+    copies = [
+        pltpu.make_async_copy(src, dst, local_sem.at[k])
+        for k, (src, dst) in enumerate(((wg_hbm, wg_v), (wu_hbm, wu_v), (wd_hbm, wd_v)))
+    ]
+    for c in copies:
+        c.start()
+    _up_kernel(nf, chips, slot_ref, wg_v, wu_v, act_s, *up_scratch, weights=copies[:2])
+    copies[2].wait()
+    _down_kernel(nf, chips, act_s, wd_v, o_ref, *down_scratch)
 
 
 def moe_layer(slots, wg, wu, wd, nf, chips, cid):
@@ -339,7 +349,7 @@
     return pl.pallas_call(
         functools.partial(_layer_kernel, nf, chips),
         out_shape=jax.ShapeDtypeStruct((rows, d), jnp.float32),
-        in_specs=[pl.BlockSpec(memory_space=pltpu.VMEM)] * 4,
+        in_specs=[pl.BlockSpec(memory_space=pltpu.VMEM)] + [pl.BlockSpec(memory_space=pl.ANY)] * 3,
         out_specs=pl.BlockSpec(memory_space=pltpu.VMEM),
         scratch_shapes=[
             pltpu.VMEM((2 * chips, rows, d), jnp.bfloat16),
@@ -364,6 +374,10 @@
             pltpu.SemaphoreType.DMA((chips,)),
             pltpu.SemaphoreType.DMA((chips,)),
             pltpu.SemaphoreType.DMA((chips,)),
+            pltpu.VMEM((d, hidden), jnp.bfloat16),
+            pltpu.VMEM((d, hidden), jnp.bfloat16),
+            pltpu.VMEM((hidden, d), jnp.bfloat16),
+            pltpu.SemaphoreType.DMA((3,)),
         ],
         compiler_params=pltpu.CompilerParams(collective_id=cid, has_side_effects=True),
     )(slots, wg, wu, wd)

time: 163 us -> 162 us (level)
  the two profiles are of different devices: /device:TPU:4 before, /device:TPU:28 now
where the time goes in v23:
time: 162 us
  Pallas kernels  157 us (97%)
  matrix products  3.23 us (2%)
    pallas_call x1, Pallas kernels, moe_layer(): pl.pallas_call(functools.partial(_layer_kernel, nf, chips), out_shape=jax...  157 us

profile of v23, /device:TPU:28, one launch (start us, length us, event | category | flops | bytes accessed | tf_op | source)
XLA Modules:
  0.0 162.0 jit_solution(4910652379265066395)
XLA Ops:
  0.0 0.0 copy-start
  0.0 0.0 copy-start.1
  0.0 0.7 copy-done.1
  0.8 0.2 convolution_reduce_fusion
  1.0 0.0 copy-start.2
  1.0 0.7 copy-done.2
  1.7 0.0 copy-done
  1.7 0.8 convolution_convert_fusion.1.slot_ref
  2.5 157.2 %shard_map.64 = f32[81,384]{1,0:T(8,128)} custom-call(bf16[81,384]{1,0:T(8,128)(2,1)} %convolution_convert_fusion.1.slot_ref, bf16[384,256]{1,0:T(8,128)(2,1)} %bitcast.6, bf16[384,256]{1,0:T(8,128)(2,1)} %bitcast.7, bf16[256,384]{1,0:T(8,128)(2,1)} %bitcast.8), custom_call_target="tpu_custom_call" | custom-call | tf_op jit(solution)/shard_map/pallas_call | solution.py:349
  159.7 2.2 %convolution_convert_fusion = bf16[288,384]{1,0:T(8,128)(2,1)} fusion(f32[81,384]{1,0:T(8,128)} %shard_map.64, f32[288]{0:T(512)S(1)} %select_reduce_fusion, f32[288]{0:T(512)S(1)} %broadcast_add_fusion, pred[288]{0:T(512)(128)(4,1)S(1)} %fusion.11), kind=kOutput, calls=%fused_computation | convolution fusion | flops 107676000 | bytes 348192 | tf_op jit(solution)/shard_map/dot_general | solution.py:409
  (4 shorter events, 0.1 us)
Async XLA Ops:
  0.0 1.7 %copy-start = (bf16[288,384]{1,0:T(8,128)(2,1)S(1)}, bf16[288,384]{1,0:T(8,128)(2,1)}, u32[]{:S(2)}) copy-start(bf16[288,384]{1,0:T(8,128)(2,1)} %param.6) | copy-start | bytes 663556
  0.0 0.7 copy-start.1
  1.0 0.7 copy-start.2

commit v24 on v23

--- a/solution.py
+++ b/solution.py
@@ -254,8 +254,8 @@
         device_id={"ed": sib},
         device_id_type=MESH,
     )
+    lax.fori_loop(0, chips, send_slots, 0)
     to_sib.start()
-    lax.fori_loop(0, chips, send_slots, 0)
     sel_buf[mine] = slot_ref[...]
     for c in weights:
         c.wait()

time: 162 us -> 163 us (level)
  the two profiles are of different devices: /device:TPU:28 before, /device:TPU:4 now
where the time goes in v24:
time: 163 us
  Pallas kernels  158 us (97%)
  matrix products  3.23 us (2%)
    pallas_call x1, Pallas kernels, moe_layer(): pl.pallas_call(functools.partial(_layer_kernel, nf, chips), out_shape=jax...  158 us

profile of v24, /device:TPU:4, one launch (start us, length us, event | category | flops | bytes accessed | tf_op | source)
XLA Modules:
  0.0 162.7 jit_solution(9082086820656733306)
XLA Ops:
  0.0 0.0 copy-start
  0.0 0.0 copy-start.1
  0.0 0.7 copy-done.1
  0.8 0.2 convolution_reduce_fusion
  1.0 0.0 copy-start.2
  1.0 0.7 copy-done.2
  1.7 0.0 copy-done
  1.7 0.8 convolution_convert_fusion.1.slot_ref
  2.5 158.0 %shard_map.64 = f32[81,384]{1,0:T(8,128)} custom-call(bf16[81,384]{1,0:T(8,128)(2,1)} %convolution_convert_fusion.1.slot_ref, bf16[384,256]{1,0:T(8,128)(2,1)} %bitcast.6, bf16[384,256]{1,0:T(8,128)(2,1)} %bitcast.7, bf16[256,384]{1,0:T(8,128)(2,1)} %bitcast.8), custom_call_target="tpu_custom_call" | custom-call | tf_op jit(solution)/shard_map/pallas_call | solution.py:349
  160.5 2.2 %convolution_convert_fusion = bf16[288,384]{1,0:T(8,128)(2,1)} fusion(f32[81,384]{1,0:T(8,128)} %shard_map.64, f32[288]{0:T(512)S(1)} %select_reduce_fusion, f32[288]{0:T(512)S(1)} %broadcast_add_fusion, pred[288]{0:T(512)(128)(4,1)S(1)} %fusion.11), kind=kOutput, calls=%fused_computation | convolution fusion | flops 107676000 | bytes 348192 | tf_op jit(solution)/shard_map/dot_general | solution.py:409
  (4 shorter events, 0.1 us)
Async XLA Ops:
  0.0 1.7 %copy-start = (bf16[288,384]{1,0:T(8,128)(2,1)S(1)}, bf16[288,384]{1,0:T(8,128)(2,1)}, u32[]{:S(2)}) copy-start(bf16[288,384]{1,0:T(8,128)(2,1)} %param.6) | copy-start | bytes 663556
  0.0 0.7 copy-start.1
  1.0 0.7 copy-start.2
